TPU v7x, 128 devices: a whole 4x4x4 slice. The times are simulated.
128 devices in a mesh: layer: 4 (over y_lo, core), latent: 16 (over x, z), row: 2 (over y_hi).
Axes of the slice: x: 4, y: 4 (y_hi: 2, y_lo: 2; y = y_hi * 2 + y_lo), z: 4, core: 2. Of those that a mesh axis runs over, the one named last changes fastest.
Arguments:
- inputs: bfloat16 [1024, 4, 3584], P('row', 'layer'), may hold values from -6 to 6
- clean_acts: bfloat16 [1024, 4, 3584], P('row', 'layer'), may hold values from -6 to 6
- enc_weight: bfloat16 [4, 3584, 12288], P('layer', None, 'latent'), may hold values from -0.0625 to 0.0625
- enc_bias: float32 [12288], P('latent'), may hold values from -3 to 3
- dec_weight: bfloat16 [4, 12288, 3584], P('layer', 'latent'), may hold values from -0.109375 to 0.109375
- dec_bias: float32 [4, 3584], P('layer'), may hold values from -3 to 3
- pairing: int32 [1024], replicated, may hold values from 0 to 1023, each once
- targets: int32 [1024], replicated, may hold values from 0 to 12287
Outputs:
- input_grad: bfloat16 [1024, 4, 3584], P('row', 'layer', 'latent')
Inputs may be any that keep to these rules, and one draw needn't show every extreme that they name: pairing is a permutation of the rows.
All inputs are finite; a program needn't handle non-finite values.
Results may differ from a plain program's by a relative error of at most 0.018.
Values may be sent and summed in bfloat16 or wider, within the bound.
A program may use at most 128 MiB of HBM per device.

v0:
```python
import jax
import jax.numpy as jnp
from jax import lax
from jax.sharding import PartitionSpec as P

MARGIN = 16.0


def local(inputs, clean_acts, enc_weight, enc_bias, dec_weight, dec_bias, pairing, targets):
    row_count = inputs.shape[0]
    lat_count = enc_weight.shape[2]
    all_rows = pairing.shape[0]
    partial_pre = jnp.einsum("rld,ldf->rf", inputs, enc_weight, preferred_element_type=jnp.float32)
    preact = lax.psum(partial_pre, "layer") + enc_bias
    features = jnp.maximum(preact, 0.0).astype(jnp.bfloat16)
    partial_recon = jnp.einsum(
        "rf,lfd->rld", features, dec_weight, preferred_element_type=jnp.float32
    )
    recon = (
        lax.psum(partial_recon.astype(jnp.bfloat16), "latent").astype(jnp.float32) + dec_bias[None]
    )
    recon_error = (recon - clean_acts.astype(jnp.float32)).astype(jnp.bfloat16)
    partial_grad = jnp.einsum(
        "rld,lfd->rf", recon_error, dec_weight, preferred_element_type=jnp.float32
    )
    feat_grad = lax.psum(partial_grad.astype(jnp.bfloat16), "layer").astype(jnp.float32)
    row_ids = lax.axis_index("row") * row_count + jnp.arange(row_count, dtype=jnp.int32)
    latent_ids = lax.axis_index("latent") * lat_count + jnp.arange(lat_count, dtype=jnp.int32)
    every_row = jnp.arange(all_rows, dtype=jnp.int32)
    pair_table = (
        (every_row[None, :] == row_ids[:, None]).astype(jnp.float32)
        - (pairing[None, :] == row_ids[:, None]).astype(jnp.float32)
    ).astype(jnp.bfloat16)
    target_hot = (targets[:, None] == latent_ids[None, :]).astype(jnp.bfloat16)
    margin_table = jnp.dot(pair_table, target_hot, preferred_element_type=jnp.float32)
    pre_grad = jnp.where(preact > 0, feat_grad - MARGIN * margin_table, 0.0).astype(jnp.bfloat16)
    partial_input = jnp.einsum(
        "rf,ldf->rld", pre_grad, enc_weight, preferred_element_type=jnp.float32
    )
    return lax.psum_scatter(
        partial_input.astype(jnp.bfloat16), "latent", scatter_dimension=2, tiled=True
    )


def solution(mesh):
    placed = (
        P("row", "layer", None),
        P("row", "layer", None),
        P("layer", None, "latent"),
        P("latent"),
        P("layer", "latent", None),
        P("layer", None),
        P(),
        P(),
    )
    return jax.shard_map(
        local, mesh=mesh, in_specs=placed, out_specs=P("row", "layer", "latent"), check_vma=False
    )
```

profile of v0, /device:TPU:1, one launch (start us, length us, event | category | flops | bytes accessed | tf_op | source)
XLA Modules:
  0.0 338.6 jit_solution(3582329185027810856)
XLA Ops:
  6.5 0.0 all-reduce.4.cloned.1.call-start
  6.5 7.9 %fusion.4 = f32[512,768]{1,0:T(8,128)} fusion(bf16[1,3584,768]{2,1,0:T(8,128)(2,1)} %param.10, bf16[512,1,3584]{2,0,1:T(8,128)(2,1)} %param.8), kind=kOutput, calls=%fused_computation.7 | convolution fusion | flops 2818572288 | bytes 10747904 | tf_op jit(solution)/shard_map/rld,ldf->rf/dot_general | solution.py:13
  14.4 0.0 all-reduce.4.cloned.1.call-update
  14.4 0.0 all-reduce.6.cloned.1.call-start
  14.5 52.5 %all-reduce.4.cloned.1.call-done = f32[512,768]{1,0:T(8,128)} async-done(((f32[512,768]{1,0:T(8,128)}), f32[512,768]{1,0:T(8,128)}) %all-reduce.4.cloned.1.call-update) | async-done | bytes 1572880 | tf_op jit(solution)/shard_map/psum | solution.py:14
  67.0 7.9 %fusion.6 = bf16[512,1,3584]{2,0,1:T(8,128)(2,1)} fusion(bf16[1,768,3584]{2,1,0:T(8,128)(2,1)} %param.12, f32[512,768]{1,0:T(8,128)} %all-reduce.4.cloned.1.call-done, f32[768]{0:T(1024)S(1)} %copy-done.2), kind=kOutput, calls=%fused_computation.9 | convolution fusion | flops 2821586944 | bytes 10750976 | tf_op jit(solution)/shard_map/rf,lfd->rld/dot_general | solution.py:16
  74.9 0.0 all-reduce.6.cloned.1.call-update
  74.9 0.0 all-reduce.8.cloned.1.call-start
  75.0 0.6 copy-done
  75.7 0.0 copy-start.3
  75.7 0.0 copy-start.4
  75.7 98.7 %all-reduce.6.cloned.1.call-done = bf16[512,1,3584]{2,0,1:T(8,128)(2,1)} async-done(((bf16[512,1,3584]{2,0,1:T(8,128)(2,1)}), bf16[512,1,3584]{2,0,1:T(8,128)(2,1)}) %all-reduce.6.cloned.1.call-update) | async-done | bytes 3670032 | tf_op jit(solution)/shard_map/psum | solution.py:20
  174.3 8.8 %fusion.20 = bf16[512,768]{1,0:T(8,128)(2,1)} fusion(bf16[1,768,3584]{2,1,0:T(8,128)(2,1)} %param.12, bf16[512,1,3584]{2,0,1:T(8,128)(2,1)} %param.9, bf16[512,1,3584]{2,0,1:T(8,128)(2,1)} %all-reduce.6.cloned.1.call-done, f32[3584]{0:T(1024)S(1)} %reduce), kind=kOutput, calls=%fused_computation.23 | convolution fusion | flops 2828140544 | bytes 13645824 | tf_op jit(solution)/shard_map/rld,lfd->rf/dot_general | solution.py:23
  183.1 0.0 all-reduce.8.cloned.1.call-update
  183.1 0.2 reduce-scatter.4.cloned.1.call-start
  183.4 39.2 %all-reduce.8.cloned.1.call-done = bf16[512,768]{1,0:T(8,128)(2,1)} async-done(((bf16[512,768]{1,0:T(8,128)(2,1)}), bf16[512,768]{1,0:T(8,128)(2,1)}) %all-reduce.8.cloned.1.call-update) | async-done | bytes 786448 | tf_op jit(solution)/shard_map/psum | solution.py:26
  222.6 0.0 copy-done.1
  222.6 9.4 %fusion.9 = bf16[512,1,3584]{2,0,1:T(8,128)(2,1)} fusion(bf16[1,3584,768]{2,1,0:T(8,128)(2,1)} %param.10, bf16[512,768]{1,0:T(8,128)(2,1)} %all-reduce.8.cloned.1.call-done, f32[512,768]{1,0:T(8,128)S(1)} %copy-done.1, s32[768]{0:T(1024)S(1)} %iota_add_fusion, s32[1024]{0:T(1024)S(1)} %copy-done.3, s32[1024]{0:T(1024)S(1)} %copy-done.4, ...), kind=kOutput, calls=%fused_computation.10 | convolution fusion | flops 3632398336 | bytes 11550720 | tf_op jit(solution)/shard_map/rf,ldf->rld/dot_general | solution.py:37
  232.0 16.5 %copy.11 = bf16[512,1,3584]{0,1,2:T(2,128)(2,1)} copy(bf16[512,1,3584]{2,0,1:T(8,128)(2,1)} %fusion.9) | data formatting | bytes 7340032
  248.6 6.1 %copy.16 = bf16[3584,1,512]{2,0,1:T(8,128)(2,1)} copy(bf16[3584,1,512]{2,1,0:T(2,128)(2,1)} %bitcast.35) | data formatting | bytes 7340032
  254.6 0.0 reduce-scatter.4.cloned.1.call-update
  254.7 75.5 %reduce-scatter.4.cloned.1.call-done = bf16[224,512]{1,0:T(8,128)(2,1)} async-done(((bf16[3584,512]{1,0:T(8,128)(2,1)}), bf16[224,512]{1,0:T(8,128)(2,1)}) %reduce-scatter.4.cloned.1.call-update) | async-done | bytes 229392
  330.1 1.2 reshape_bitcast_fusion
  331.3 0.7 copy.10
  (9 shorter events, 0.1 us)
Async XLA Ops:
  6.5 60.5 %copy-start.2 = (f32[768]{0:T(1024)S(1)}, f32[768]{0:T(1024)}, u32[]{:S(2)}) copy-start(f32[768]{0:T(1024)} %param.11) | copy-start | bytes 9220
  6.5 60.5 %all-reduce.4.cloned.1.call-start = ((), (), s32[]{:S(2)}) async-start(), calls=%async_computation.1 | async-start | bytes 3145728 | tf_op jit(solution)/shard_map/psum | solution.py:14
  14.4 159.9 %all-reduce.6.cloned.1.call-start = ((), (), s32[]{:S(2)}) async-start(), calls=%async_computation.2 | async-start | bytes 7340032 | tf_op jit(solution)/shard_map/psum | solution.py:20
  74.9 0.7 copy-start
  74.9 147.7 %all-reduce.8.cloned.1.call-start = ((), (), s32[]{:S(2)}) async-start(), calls=%async_computation.3 | async-start | bytes 1572864 | tf_op jit(solution)/shard_map/psum | solution.py:26
  75.7 147.0 %copy-start.1 = (f32[512,768]{1,0:T(8,128)S(1)}, f32[512,768]{1,0:T(8,128)}, u32[]{:S(2)}) copy-start(f32[512,768]{1,0:T(8,128)} %all-reduce.4.cloned.1.call-done) | copy-start | bytes 4718596
  75.7 147.0 %copy-start.3 = (s32[1024]{0:T(1024)S(1)}, s32[1024]{0:T(1024)}, u32[]{:S(2)}) copy-start(s32[1024]{0:T(1024)} %param.15) | copy-start | bytes 12292
  75.7 147.0 %copy-start.4 = (s32[1024]{0:T(1024)S(1)}, s32[1024]{0:T(1024)}, u32[]{:S(2)}) copy-start(s32[1024]{0:T(1024)} %param.14) | copy-start | bytes 12292
  183.1 147.0 %reduce-scatter.4.cloned.1.call-start = ((), (), s32[]{:S(2)}) async-start(), calls=%async_computation.4 | async-start | bytes 3899392
Sparse Core Ops, SparseCore 0:
  14.5 52.4 all-reduce.3
  75.1 99.2 all-reduce.5
  183.3 39.3 all-reduce.7
  254.8 75.3 reduce-scatter.3
where the time goes:
time: 340 us; the launch traced here: 339 us
  waiting for transfers between devices  266 us (78%)
  matrix products  33.9 us (10%)
  local copies, waits for them, and re-layouts  25.1 us (7%)
  between operations  13.2 us (4%)
    psum x1, waiting for transfers between devices, local(): lax.psum(partial_recon.astype(jnp.bfloat16), 'latent').astype(jnp.float32)  98.7 us
    unnamed x5, waiting for transfers between devices  75.5 us
    psum x1, waiting for transfers between devices, local(): preact = lax.psum(partial_pre, 'layer') + enc_bias  52.5 us
    psum x1, waiting for transfers between devices, local(): lax.psum(partial_grad.astype(jnp.bfloat16), 'layer').astype(jnp.float32)  39.2 us
    unnamed x13, local copies, waits for them, and re-layouts  24.4 us
    dot_general x1, matrix products, local(): jnp.einsum('rf,ldf->rld', pre_grad, enc_weight, preferred_element_type=jn...  9.4 us
    dot_general x1, matrix products, local(): jnp.einsum('rld,lfd->rf', recon_error, dec_weight, preferred_element_type...  8.76 us
    dot_general x1, matrix products, local(): jnp.einsum('rf,lfd->rld', features, dec_weight, preferred_element_type=jn...  7.9 us
  transfers between devices with their start and end apart: 4, of which 4 were waited for; matrix products, arithmetic and copies ran while one was open for 0% of the time, Pallas kernels for 0%

commit v1 on v0

--- a/solution.py
+++ b/solution.py
@@ -10,6 +10,9 @@
     row_count = inputs.shape[0]
     lat_count = enc_weight.shape[2]
     all_rows = pairing.shape[0]
+    n_lat = lax.psum(1, "latent")
+    d_model = inputs.shape[2]
+    chunk = d_model // n_lat
     partial_pre = jnp.einsum("rld,ldf->rf", inputs, enc_weight, preferred_element_type=jnp.float32)
     preact = lax.psum(partial_pre, "layer") + enc_bias
     features = jnp.maximum(preact, 0.0).astype(jnp.bfloat16)
@@ -34,12 +37,13 @@
     target_hot = (targets[:, None] == latent_ids[None, :]).astype(jnp.bfloat16)
     margin_table = jnp.dot(pair_table, target_hot, preferred_element_type=jnp.float32)
     pre_grad = jnp.where(preact > 0, feat_grad - MARGIN * margin_table, 0.0).astype(jnp.bfloat16)
+    enc_split = enc_weight[0].reshape(n_lat, chunk, lat_count)
     partial_input = jnp.einsum(
-        "rf,ldf->rld", pre_grad, enc_weight, preferred_element_type=jnp.float32
-    )
-    return lax.psum_scatter(
-        partial_input.astype(jnp.bfloat16), "latent", scatter_dimension=2, tiled=True
-    )
+        "rf,gdf->grd", pre_grad, enc_split, preferred_element_type=jnp.float32
+    ).astype(jnp.bfloat16)
+    gathered = lax.all_to_all(partial_input, "latent", 0, 0, tiled=True)
+    total = jnp.sum(gathered.astype(jnp.float32), axis=0).astype(jnp.bfloat16)
+    return total[:, None, :]
 
 
 def solution(mesh):

time: 340 us -> 293 us (0.86)
  waiting for transfers between devices: 266 us -> 191 us
  blocking collectives: 0 us -> 50.7 us
  local copies, waits for them, and re-layouts: 25.1 us -> 0.66 us
    unnamed x5 -> x3, waiting for transfers between devices: 75.5 us -> 0.05 us
    all_to_all x0 -> x1, blocking collectives: none -> 50.7 us  [local(): gathered = lax.all_to_all(partial_input, 'latent', 0, 0, tiled=True)]
    unnamed x13 -> x10, local copies, waits for them, and re-layouts: 24.4 us -> 0.66 us
  transfers between devices with their start and end apart: 4 -> 3, of which waited for: 4 -> 3; matrix products, arithmetic and copies ran while one was open for 0% -> 0% of each run, Pallas kernels for 0% -> 0%
where the time goes in v1:
time: 293 us; the launch traced here: 292 us
  waiting for transfers between devices  191 us (65%)
  blocking collectives  50.7 us (17%)
  matrix products  33.4 us (11%)
  between operations  13.2 us (5%)
  other arithmetic  3.35 us (1%)
    psum x1, waiting for transfers between devices, local(): lax.psum(partial_recon.astype(jnp.bfloat16), 'latent').astype(jnp.float32)  98.7 us
    psum x1, waiting for transfers between devices, local(): preact = lax.psum(partial_pre, 'layer') + enc_bias  52.5 us
    all_to_all x1, blocking collectives, local(): gathered = lax.all_to_all(partial_input, 'latent', 0, 0, tiled=True)  50.7 us
    psum x1, waiting for transfers between devices, local(): lax.psum(partial_grad.astype(jnp.bfloat16), 'layer').astype(jnp.float32)  39.5 us
    dot_general x1, matrix products, local(): jnp.einsum('rf,gdf->grd', pre_grad, enc_split, preferred_element_type=jnp...  8.91 us
    dot_general x1, matrix products, local(): jnp.einsum('rld,lfd->rf', recon_error, dec_weight, preferred_element_type...  8.77 us
    dot_general x1, matrix products, local(): jnp.einsum('rf,lfd->rld', features, dec_weight, preferred_element_type=jn...  7.9 us
    dot_general x1, matrix products, local(): jnp.einsum('rld,ldf->rf', inputs, enc_weight, preferred_element_type=jnp....  7.84 us
  transfers between devices with their start and end apart: 3, of which 3 were waited for; matrix products, arithmetic and copies ran while one was open for 0% of the time, Pallas kernels for 0%

profile of v1, /device:TPU:1, one launch (start us, length us, event | category | flops | bytes accessed | tf_op | source)
XLA Modules:
  0.0 292.1 jit_solution(8561482036106748665)
XLA Ops:
  6.5 0.0 all-reduce.4.cloned.1.call-start
  6.5 7.8 %fusion.3 = f32[512,768]{1,0:T(8,128)} fusion(bf16[1,3584,768]{2,1,0:T(8,128)(2,1)} %param.10, bf16[512,1,3584]{2,0,1:T(8,128)(2,1)} %param.8), kind=kOutput, calls=%fused_computation.5 | convolution fusion | flops 2818572288 | bytes 10747904 | tf_op jit(solution)/shard_map/rld,ldf->rf/dot_general | solution.py:16
  14.4 0.0 all-reduce.4.cloned.1.call-update
  14.4 0.0 all-reduce.6.cloned.1.call-start
  14.5 52.5 %all-reduce.4.cloned.1.call-done = f32[512,768]{1,0:T(8,128)} async-done(((f32[512,768]{1,0:T(8,128)}), f32[512,768]{1,0:T(8,128)}) %all-reduce.4.cloned.1.call-update) | async-done | bytes 1572880 | tf_op jit(solution)/shard_map/psum | solution.py:17
  67.0 0.0 copy-done.3
  67.0 7.9 %fusion.5 = bf16[512,1,3584]{2,0,1:T(8,128)(2,1)} fusion(bf16[1,768,3584]{2,1,0:T(8,128)(2,1)} %param.12, f32[512,768]{1,0:T(8,128)} %all-reduce.4.cloned.1.call-done, f32[768]{0:T(1024)S(1)} %copy-done.3), kind=kOutput, calls=%fused_computation.7 | convolution fusion | flops 2821586944 | bytes 10750976 | tf_op jit(solution)/shard_map/rf,lfd->rld/dot_general | solution.py:19
  74.9 0.0 copy-start
  74.9 0.0 all-reduce.6.cloned.1.call-update
  74.9 0.0 all-reduce.8.cloned.1.call-start
  75.0 0.6 copy-done
  75.6 0.0 copy-start.1
  75.7 0.0 copy-start.2
  75.7 0.0 copy-start.4
  75.7 98.7 %all-reduce.6.cloned.1.call-done = bf16[512,1,3584]{2,0,1:T(8,128)(2,1)} async-done(((bf16[512,1,3584]{2,0,1:T(8,128)(2,1)}), bf16[512,1,3584]{2,0,1:T(8,128)(2,1)}) %all-reduce.6.cloned.1.call-update) | async-done | bytes 3670032 | tf_op jit(solution)/shard_map/psum | solution.py:23
  174.4 8.8 %fusion.16 = bf16[512,768]{1,0:T(8,128)(2,1)} fusion(bf16[1,768,3584]{2,1,0:T(8,128)(2,1)} %param.12, bf16[512,1,3584]{2,0,1:T(8,128)(2,1)} %param.9, bf16[512,1,3584]{2,0,1:T(8,128)(2,1)} %all-reduce.6.cloned.1.call-done, f32[3584]{0:T(1024)S(1)} %reduce.1), kind=kOutput, calls=%fused_computation.20 | convolution fusion | flops 2828140544 | bytes 13645824 | tf_op jit(solution)/shard_map/rld,lfd->rf/dot_general | solution.py:26
  183.1 0.0 all-reduce.8.cloned.1.call-update
  183.2 39.5 %all-reduce.8.cloned.1.call-done = bf16[512,768]{1,0:T(8,128)(2,1)} async-done(((bf16[512,768]{1,0:T(8,128)(2,1)}), bf16[512,768]{1,0:T(8,128)(2,1)}) %all-reduce.8.cloned.1.call-update) | async-done | bytes 786448 | tf_op jit(solution)/shard_map/psum | solution.py:29
  222.7 0.0 copy-done.1
  222.7 0.0 copy-done.2
  222.7 0.0 copy-done.4
  222.7 8.9 %convert_bitcast_fusion = bf16[16,512,224]{1,2,0:T(8,128)(2,1)} fusion(bf16[16,224,768]{2,1,0:T(8,128)(2,1)} %bitcast.31, s32[768]{0:T(1024)S(1)} %iota_add_fusion, s32[1024]{0:T(1024)S(1)} %copy-done.2, bf16[512,768]{1,0:T(8,128)(2,1)} %all-reduce.8.cloned.1.call-done, f32[512,768]{1,0:T(8,128)S(1)} %copy-done.1, s32[1024]{0:T(1024)S(1)} %copy-done.4, ...), kind=kOutput, calls=%fused_computation.10 | convolution fusion | flops 3632398336 | bytes 11550720 | tf_op jit(solution)/shard_map/rf,gdf->grd/dot_general | solution.py:41
  231.6 50.7 %all_to_all.5 = bf16[16,512,224]{1,2,0:T(8,128)(2,1)} all-to-all(bf16[16,512,224]{1,2,0:T(8,128)(2,1)} %convert_bitcast_fusion), channel_id=1, replica_groups=mesh['layer'=4,'latent'=16,'row'=2] {'latent'}, dimensions={0} | all-to-all | bytes 7340032 | tf_op jit(solution)/shard_map/all_to_all | solution.py:44
  282.3 3.3 %reduce_sum.12 = bf16[512,224]{0,1:T(8,128)(2,1)} reduce(bf16[16,512,224]{1,2,0:T(8,128)(2,1)} %all_to_all.5, bf16[]{:T(256)} %constant.18.clone.1), dimensions={0}, to_apply=%region_3.4 | reduce | flops 1720320 | bytes 3899394 | tf_op jit(solution)/shard_map/reduce_sum | solution.py:45
  (4 shorter events, 0.0 us)
Async XLA Ops:
  6.5 60.5 %copy-start.3 = (f32[768]{0:T(1024)S(1)}, f32[768]{0:T(1024)}, u32[]{:S(2)}) copy-start(f32[768]{0:T(1024)} %param.11) | copy-start | bytes 9220
  6.5 60.4 %all-reduce.4.cloned.1.call-start = ((), (), s32[]{:S(2)}) async-start(), calls=%async_computation.1 | async-start | bytes 3145728 | tf_op jit(solution)/shard_map/psum | solution.py:17
  14.4 160.0 %all-reduce.6.cloned.1.call-start = ((), (), s32[]{:S(2)}) async-start(), calls=%async_computation.2 | async-start | bytes 7340032 | tf_op jit(solution)/shard_map/psum | solution.py:23
  74.9 0.7 copy-start
  74.9 147.8 %all-reduce.8.cloned.1.call-start = ((), (), s32[]{:S(2)}) async-start(), calls=%async_computation.3 | async-start | bytes 1572864 | tf_op jit(solution)/shard_map/psum | solution.py:29
  75.6 147.1 %copy-start.1 = (f32[512,768]{1,0:T(8,128)S(1)}, f32[512,768]{1,0:T(8,128)}, u32[]{:S(2)}) copy-start(f32[512,768]{1,0:T(8,128)} %all-reduce.4.cloned.1.call-done) | copy-start | bytes 4718596
  75.7 147.1 %copy-start.2 = (s32[1024]{0:T(1024)S(1)}, s32[1024]{0:T(1024)}, u32[]{:S(2)}) copy-start(s32[1024]{0:T(1024)} %param.15) | copy-start | bytes 12292
  75.7 147.0 %copy-start.4 = (s32[1024]{0:T(1024)S(1)}, s32[1024]{0:T(1024)}, u32[]{:S(2)}) copy-start(s32[1024]{0:T(1024)} %param.14) | copy-start | bytes 12292
Sparse Core Ops, SparseCore 0:
  14.5 52.4 all-reduce.3
  75.0 99.2 all-reduce.5
  183.3 39.3 all-reduce.7

commit v2 on v1

--- a/solution.py
+++ b/solution.py
@@ -1,9 +1,66 @@
 import jax
 import jax.numpy as jnp
 from jax import lax
+from jax.experimental import pallas as pl
+from jax.experimental.pallas import tpu as pltpu
 from jax.sharding import PartitionSpec as P
 
 MARGIN = 16.0
+MESH = pl.DeviceIdType.MESH
+
+
+def _layer_sum_kernel(x_ref, o_ref, recv_a, recv_b, recv_c, send_sems, recv_sems):
+    me = lax.axis_index("layer")
+    core = me % 2
+    chip = me // 2
+    mate = me + 1 - 2 * core
+    far = me + 2 - 4 * chip
+    half = x_ref.shape[0] // 2
+    mine = pl.ds(pl.multiple_of(core * half, half), half)
+    other = pl.ds(pl.multiple_of((1 - core) * half, half), half)
+
+    barrier = pltpu.get_barrier_semaphore()
+    for peer in (mate, far):
+        pl.semaphore_signal(barrier, inc=1, device_id={"layer": peer}, device_id_type=MESH)
+    pl.semaphore_wait(barrier, 2)
+
+    def send(src, dst, slot, peer):
+        return pltpu.make_async_remote_copy(
+            src_ref=src, dst_ref=dst, send_sem=send_sems.at[slot], recv_sem=recv_sems.at[slot],
+            device_id={"layer": peer}, device_id_type=MESH,
+        )
+
+    step_a = send(x_ref.at[other], recv_a, 0, mate)
+    step_a.start()
+    step_a.wait()
+    o_ref[mine] = x_ref[mine].astype(jnp.float32) + recv_a[...].astype(jnp.float32)
+    step_b = send(o_ref.at[mine], recv_b, 1, far)
+    step_b.start()
+    step_b.wait()
+    o_ref[mine] = o_ref[mine] + recv_b[...]
+    step_c = send(o_ref.at[mine], recv_c, 2, mate)
+    step_c.start()
+    step_c.wait()
+    o_ref[other] = recv_c[...]
+
+
+def layer_sum(x, collective_id):
+    rows, cols = x.shape
+    half = rows // 2
+    return pl.pallas_call(
+        _layer_sum_kernel,
+        out_shape=jax.ShapeDtypeStruct((rows, cols), jnp.float32),
+        in_specs=[pl.BlockSpec(memory_space=pltpu.VMEM)],
+        out_specs=pl.BlockSpec(memory_space=pltpu.VMEM),
+        scratch_shapes=[
+            pltpu.VMEM((half, cols), x.dtype),
+            pltpu.VMEM((half, cols), jnp.float32),
+            pltpu.VMEM((half, cols), jnp.float32),
+            pltpu.SemaphoreType.DMA((3,)),
+            pltpu.SemaphoreType.DMA((3,)),
+        ],
+        compiler_params=pltpu.CompilerParams(collective_id=collective_id, has_side_effects=True),
+    )(x)
 
 
 def local(inputs, clean_acts, enc_weight, enc_bias, dec_weight, dec_bias, pairing, targets):
@@ -14,7 +71,7 @@
     d_model = inputs.shape[2]
     chunk = d_model // n_lat
     partial_pre = jnp.einsum("rld,ldf->rf", inputs, enc_weight, preferred_element_type=jnp.float32)
-    preact = lax.psum(partial_pre, "layer") + enc_bias
+    preact = layer_sum(partial_pre, 1) + enc_bias
     features = jnp.maximum(preact, 0.0).astype(jnp.bfloat16)
     partial_recon = jnp.einsum(
         "rf,lfd->rld", features, dec_weight, preferred_element_type=jnp.float32
@@ -26,7 +83,7 @@
     partial_grad = jnp.einsum(
         "rld,lfd->rf", recon_error, dec_weight, preferred_element_type=jnp.float32
     )
-    feat_grad = lax.psum(partial_grad.astype(jnp.bfloat16), "layer").astype(jnp.float32)
+    feat_grad = layer_sum(partial_grad.astype(jnp.bfloat16), 2)
     row_ids = lax.axis_index("row") * row_count + jnp.arange(row_count, dtype=jnp.int32)
     latent_ids = lax.axis_index("latent") * lat_count + jnp.arange(lat_count, dtype=jnp.int32)
     every_row = jnp.arange(all_rows, dtype=jnp.int32)

time: 293 us -> 256 us (0.87)
  waiting for transfers between devices: 191 us -> 100 us
  Pallas kernels: 0 us -> 55 us
    psum x2 -> x0, waiting for transfers between devices: 92.1 us -> none  [the longest x1 52.5 us: local(): preact = lax.psum(partial_pre, 'layer') + enc_bias]
    pallas_call x0 -> x2, Pallas kernels: none -> 55 us  [layer_sum(): pl.pallas_call(_layer_sum_kernel, out_shape=jax.ShapeDtypeStruct((rows, c...]
  transfers between devices with their start and end apart: 3 -> 1, of which waited for: 3 -> 1; matrix products, arithmetic and copies ran while one was open for 0% -> 0% of each run, Pallas kernels for 0% -> 0%
where the time goes in v2:
time: 256 us; the launch traced here: 255 us
  waiting for transfers between devices  100 us (39%)
  Pallas kernels  55 us (21%)
  blocking collectives  48.6 us (19%)
  matrix products  33.7 us (13%)
  between operations  13.5 us (5%)
  other arithmetic  3.35 us (1%)
    psum x1, waiting for transfers between devices, local(): lax.psum(partial_recon.astype(jnp.bfloat16), 'latent').astype(jnp.float32)  100 us
    pallas_call x2, Pallas kernels, layer_sum(): pl.pallas_call(_layer_sum_kernel, out_shape=jax.ShapeDtypeStruct((rows, c...  55 us
    all_to_all x1, blocking collectives, local(): gathered = lax.all_to_all(partial_input, 'latent', 0, 0, tiled=True)  48.6 us
    dot_general x1, matrix products, local(): jnp.einsum('rf,gdf->grd', pre_grad, enc_split, preferred_element_type=jnp...  9.13 us
    dot_general x1, matrix products, local(): jnp.einsum('rld,lfd->rf', recon_error, dec_weight, preferred_element_type...  8.78 us
    dot_general x1, matrix products, local(): jnp.einsum('rf,lfd->rld', features, dec_weight, preferred_element_type=jn...  7.9 us
    dot_general x1, matrix products, local(): jnp.einsum('rld,ldf->rf', inputs, enc_weight, preferred_element_type=jnp....  7.84 us
  transfers between devices with their start and end apart: 1, of which 1 were waited for; matrix products, arithmetic and copies ran while one was open for 0% of the time, Pallas kernels for 0%

profile of v2, /device:TPU:1, one launch (start us, length us, event | category | flops | bytes accessed | tf_op | source)
XLA Modules:
  0.0 254.8 jit_solution(14348653753811794921)
XLA Ops:
  6.5 0.0 copy-start.2
  6.5 0.0 all-reduce.2.cloned.1.call-start
  6.5 7.8 %fusion.3.x_ref = f32[512,768]{1,0:T(8,128)} fusion(bf16[1,3584,768]{2,1,0:T(8,128)(2,1)} %param.10, bf16[512,1,3584]{2,0,1:T(8,128)(2,1)} %param.8), kind=kOutput, calls=%fused_computation.5 | convolution fusion | flops 2818572288 | bytes 10747904 | tf_op jit(solution)/shard_map/rld,ldf->rf/dot_general | solution.py:73
  14.4 28.1 %shard_map.82 = f32[512,768]{1,0:T(8,128)} custom-call(f32[512,768]{1,0:T(8,128)} %fusion.3.x_ref), custom_call_target="tpu_custom_call" | custom-call | tf_op jit(solution)/shard_map/pallas_call | solution.py:50
  42.5 0.0 copy-done.2
  42.5 7.9 %fusion.5 = bf16[512,1,3584]{2,0,1:T(8,128)(2,1)} fusion(bf16[1,768,3584]{2,1,0:T(8,128)(2,1)} %param.12, f32[512,768]{1,0:T(8,128)} %shard_map.82, f32[768]{0:T(1024)S(1)} %copy-done.2), kind=kOutput, calls=%fused_computation.7 | convolution fusion | flops 2821586944 | bytes 10750976 | tf_op jit(solution)/shard_map/rf,lfd->rld/dot_general | solution.py:76
  50.4 0.0 copy-start.1
  50.4 0.0 all-reduce.2.cloned.1.call-update
  50.4 0.7 copy-done.1
  51.2 0.0 copy-start
  51.2 0.0 copy-start.3
  51.2 0.0 copy-start.4
  51.2 100.0 %all-reduce.2.cloned.1.call-done = bf16[512,1,3584]{2,0,1:T(8,128)(2,1)} async-done(((bf16[512,1,3584]{2,0,1:T(8,128)(2,1)}), bf16[512,1,3584]{2,0,1:T(8,128)(2,1)}) %all-reduce.2.cloned.1.call-update) | async-done | bytes 3670032 | tf_op jit(solution)/shard_map/psum | solution.py:80
  151.3 8.8 %fusion.16.x_ref = bf16[512,768]{1,0:T(8,128)(2,1)} fusion(bf16[1,768,3584]{2,1,0:T(8,128)(2,1)} %param.12, bf16[512,1,3584]{2,0,1:T(8,128)(2,1)} %param.9, bf16[512,1,3584]{2,0,1:T(8,128)(2,1)} %all-reduce.2.cloned.1.call-done, f32[3584]{0:T(1024)S(1)} %reduce.1), kind=kOutput, calls=%fused_computation.20 | convolution fusion | flops 2828140544 | bytes 13645824 | tf_op jit(solution)/shard_map/rld,lfd->rf/dot_general | solution.py:83
  160.0 26.9 %shard_map.83 = f32[512,768]{1,0:T(8,128)} custom-call(bf16[512,768]{1,0:T(8,128)(2,1)} %fusion.16.x_ref), custom_call_target="tpu_custom_call" | custom-call | tf_op jit(solution)/shard_map/pallas_call | solution.py:50
  186.9 0.0 copy-done
  186.9 0.0 copy-done.3
  186.9 0.0 copy-done.4
  186.9 9.1 %convert_bitcast_fusion = bf16[16,512,224]{1,2,0:T(8,128)(2,1)} fusion(bf16[16,224,768]{2,1,0:T(8,128)(2,1)} %bitcast.31, f32[512,768]{1,0:T(8,128)} %shard_map.83, s32[768]{0:T(1024)S(1)} %iota_add_fusion, s32[1024]{0:T(1024)S(1)} %copy-done.3, f32[512,768]{1,0:T(8,128)S(1)} %copy-done, s32[1024]{0:T(1024)S(1)} %copy-done.4, s32[512]{0:T(512)S(1)} %iota_add_fusion.1, ...), kind=kOutput, calls=%fused_computation.10 | convolution fusion | flops 3632005120 | bytes 12337152 | tf_op jit(solution)/shard_map/rf,gdf->grd/dot_general | solution.py:98
  196.1 48.6 %all_to_all.5 = bf16[16,512,224]{1,2,0:T(8,128)(2,1)} all-to-all(bf16[16,512,224]{1,2,0:T(8,128)(2,1)} %convert_bitcast_fusion), channel_id=1, replica_groups=mesh['layer'=4,'latent'=16,'row'=2] {'latent'}, dimensions={0} | all-to-all | bytes 7340032 | tf_op jit(solution)/shard_map/all_to_all | solution.py:101
  244.7 3.3 %reduce_sum.12 = bf16[512,224]{0,1:T(8,128)(2,1)} reduce(bf16[16,512,224]{1,2,0:T(8,128)(2,1)} %all_to_all.5, bf16[]{:T(256)} %constant.18.clone.1), dimensions={0}, to_apply=%region_1.2 | reduce | flops 1720320 | bytes 3899394 | tf_op jit(solution)/shard_map/reduce_sum | solution.py:102
  (3 shorter events, 0.0 us)
Async XLA Ops:
  6.5 36.0 %copy-start.2 = (f32[768]{0:T(1024)S(1)}, f32[768]{0:T(1024)}, u32[]{:S(2)}) copy-start(f32[768]{0:T(1024)} %param.11) | copy-start | bytes 9220
  6.5 144.7 %all-reduce.2.cloned.1.call-start = ((), (), s32[]{:S(2)}) async-start(), calls=%async_computation.1 | async-start | bytes 7340032 | tf_op jit(solution)/shard_map/psum | solution.py:80
  50.4 0.7 copy-start.1
  51.2 135.7 %copy-start = (f32[512,768]{1,0:T(8,128)S(1)}, f32[512,768]{1,0:T(8,128)}, u32[]{:S(2)}) copy-start(f32[512,768]{1,0:T(8,128)} %shard_map.82) | copy-start | bytes 4718596
  51.2 135.7 %copy-start.3 = (s32[1024]{0:T(1024)S(1)}, s32[1024]{0:T(1024)}, u32[]{:S(2)}) copy-start(s32[1024]{0:T(1024)} %param.15) | copy-start | bytes 12292
  51.2 135.7 %copy-start.4 = (s32[1024]{0:T(1024)S(1)}, s32[1024]{0:T(1024)}, u32[]{:S(2)}) copy-start(s32[1024]{0:T(1024)} %param.14) | copy-start | bytes 12292
Sparse Core Ops, SparseCore 0:
  50.6 100.6 all-reduce.1

commit v3 on v2

--- a/solution.py
+++ b/solution.py
@@ -7,6 +7,167 @@
 
 MARGIN = 16.0
 MESH = pl.DeviceIdType.MESH
+RING = 4
+
+
+def _latent_coords():
+    me = lax.axis_index("latent")
+    return me // RING, me % RING
+
+
+def _greet(a, b):
+    barrier = pltpu.get_barrier_semaphore()
+    for k in range(1, RING):
+        pl.semaphore_signal(barrier, inc=1, device_id={"latent": a * RING + (b + k) % RING}, device_id_type=MESH)
+        pl.semaphore_signal(barrier, inc=1, device_id={"latent": ((a + k) % RING) * RING + b}, device_id_type=MESH)
+    pl.semaphore_wait(barrier, 2 * (RING - 1))
+
+
+def _copy(src, dst, send_sem, recv_sem, peer):
+    return pltpu.make_async_remote_copy(
+        src_ref=src, dst_ref=dst, send_sem=send_sem, recv_sem=recv_sem,
+        device_id={"latent": peer}, device_id_type=MESH,
+    )
+
+
+def _reduce_kernel(xa, xb, out, r1a, r1b, s1a, s1b, r2a, r2b, send_sems, recv_sems):
+    a, b = _latent_coords()
+    _greet(a, b)
+    peers_z = [(b + k) % RING for k in range(1, RING)]
+    peers_x = [(a + k) % RING for k in range(1, RING)]
+    first = []
+    for t in peers_z:
+        c = _copy(xa.at[t], r1a.at[b], send_sems.at[0, t], recv_sems.at[0, b], a * RING + t)
+        c.start()
+        first.append(c)
+    for t in peers_x:
+        c = _copy(xb.at[t], r1b.at[a], send_sems.at[1, t], recv_sems.at[1, a], t * RING + b)
+        c.start()
+        first.append(c)
+    for t in peers_z:
+        _copy(xa.at[t], r1a.at[t], send_sems.at[0, t], recv_sems.at[0, t], 0).wait_recv()
+    for t in peers_x:
+        _copy(xb.at[t], r1b.at[t], send_sems.at[1, t], recv_sems.at[1, t], 0).wait_recv()
+    sum_a = xa[b].astype(jnp.float32)
+    for t in peers_z:
+        sum_a = sum_a + r1a[t].astype(jnp.float32)
+    sum_b = xb[a].astype(jnp.float32)
+    for t in peers_x:
+        sum_b = sum_b + r1b[t].astype(jnp.float32)
+    s1a[...] = sum_a.astype(s1a.dtype)
+    s1b[...] = sum_b.astype(s1b.dtype)
+    second = []
+    for t in peers_x:
+        c = _copy(s1a.at[t], r2a.at[a], send_sems.at[2, t], recv_sems.at[2, a], t * RING + b)
+        c.start()
+        second.append(c)
+    for t in peers_z:
+        c = _copy(s1b.at[t], r2b.at[b], send_sems.at[3, t], recv_sems.at[3, b], a * RING + t)
+        c.start()
+        second.append(c)
+    for t in peers_x:
+        _copy(s1a.at[t], r2a.at[t], send_sems.at[2, t], recv_sems.at[2, t], 0).wait_recv()
+    for t in peers_z:
+        _copy(s1b.at[t], r2b.at[t], send_sems.at[3, t], recv_sems.at[3, t], 0).wait_recv()
+    own_a = xa[b, a].astype(jnp.float32)
+    for t in peers_z:
+        own_a = own_a + r1a[t, a].astype(jnp.float32)
+    own_b = xb[a, b].astype(jnp.float32)
+    for t in peers_x:
+        own_b = own_b + r1b[t, b].astype(jnp.float32)
+    for t in peers_x:
+        own_a = own_a + r2a[t].astype(jnp.float32)
+    for t in peers_z:
+        own_b = own_b + r2b[t].astype(jnp.float32)
+    out[0] = own_a
+    out[1] = own_b
+    for c in first + second:
+        c.wait_send()
+
+
+def latent_reduce(xa, xb, collective_id):
+    n, _, h, c = xa.shape
+    dt = xa.dtype
+    return pl.pallas_call(
+        _reduce_kernel,
+        out_shape=jax.ShapeDtypeStruct((2, h, c), jnp.float32),
+        in_specs=[pl.BlockSpec(memory_space=pltpu.VMEM)] * 2,
+        out_specs=pl.BlockSpec(memory_space=pltpu.VMEM),
+        scratch_shapes=[
+            pltpu.VMEM((n, n, h, c), dt),
+            pltpu.VMEM((n, n, h, c), dt),
+            pltpu.VMEM((n, h, c), dt),
+            pltpu.VMEM((n, h, c), dt),
+            pltpu.VMEM((n, h, c), dt),
+            pltpu.VMEM((n, h, c), dt),
+            pltpu.SemaphoreType.DMA((4, n)),
+            pltpu.SemaphoreType.DMA((4, n)),
+        ],
+        compiler_params=pltpu.CompilerParams(collective_id=collective_id, has_side_effects=True),
+    )(xa, xb)
+
+
+def _gather_kernel(e, oa, ob, g1a, g1b, ga, gb, send_sems, recv_sems):
+    a, b = _latent_coords()
+    _greet(a, b)
+    peers_z = [(b + k) % RING for k in range(1, RING)]
+    peers_x = [(a + k) % RING for k in range(1, RING)]
+    first = []
+    for t in peers_z:
+        c = _copy(e.at[0], g1a.at[b], send_sems.at[0, t], recv_sems.at[0, b], a * RING + t)
+        c.start()
+        first.append(c)
+    for t in peers_x:
+        c = _copy(e.at[1], g1b.at[a], send_sems.at[1, t], recv_sems.at[1, a], t * RING + b)
+        c.start()
+        first.append(c)
+    g1a[b] = e[0]
+    g1b[a] = e[1]
+    for t in peers_z:
+        _copy(e.at[0], g1a.at[t], send_sems.at[0, t], recv_sems.at[0, t], 0).wait_recv()
+    for t in peers_x:
+        _copy(e.at[1], g1b.at[t], send_sems.at[1, t], recv_sems.at[1, t], 0).wait_recv()
+    second = []
+    for t in peers_x:
+        c = _copy(g1a, ga.at[a], send_sems.at[2, t], recv_sems.at[2, a], t * RING + b)
+        c.start()
+        second.append(c)
+    for t in peers_z:
+        c = _copy(g1b, gb.at[b], send_sems.at[3, t], recv_sems.at[3, b], a * RING + t)
+        c.start()
+        second.append(c)
+    oa[a] = g1a[...]
+    ob[b] = g1b[...]
+    for t in peers_x:
+        _copy(g1a, ga.at[t], send_sems.at[2, t], recv_sems.at[2, t], 0).wait_recv()
+        oa[t] = ga[t]
+    for t in peers_z:
+        _copy(g1b, gb.at[t], send_sems.at[3, t], recv_sems.at[3, t], 0).wait_recv()
+        ob[t] = gb[t]
+    for c in first + second:
+        c.wait_send()
+
+
+def latent_gather(e, collective_id):
+    _, h, c = e.shape
+    n = RING
+    dt = e.dtype
+    full = jax.ShapeDtypeStruct((n, n, h, c), dt)
+    return pl.pallas_call(
+        _gather_kernel,
+        out_shape=(full, full),
+        in_specs=[pl.BlockSpec(memory_space=pltpu.VMEM)],
+        out_specs=(pl.BlockSpec(memory_space=pltpu.VMEM), pl.BlockSpec(memory_space=pltpu.VMEM)),
+        scratch_shapes=[
+            pltpu.VMEM((n, h, c), dt),
+            pltpu.VMEM((n, h, c), dt),
+            pltpu.VMEM((n, n, h, c), dt),
+            pltpu.VMEM((n, n, h, c), dt),
+            pltpu.SemaphoreType.DMA((4, n)),
+            pltpu.SemaphoreType.DMA((4, n)),
+        ],
+        compiler_params=pltpu.CompilerParams(collective_id=collective_id, has_side_effects=True),
+    )(e)
 
 
 def _layer_sum_kernel(x_ref, o_ref, recv_a, recv_b, recv_c, send_sems, recv_sems):
@@ -67,25 +228,29 @@
     row_count = inputs.shape[0]
     lat_count = enc_weight.shape[2]
     all_rows = pairing.shape[0]
-    n_lat = lax.psum(1, "latent")
     d_model = inputs.shape[2]
-    chunk = d_model // n_lat
+    chunk = d_model // (RING * RING)
+    half = row_count // 2
+    me = lax.axis_index("latent")
     partial_pre = jnp.einsum("rld,ldf->rf", inputs, enc_weight, preferred_element_type=jnp.float32)
     preact = layer_sum(partial_pre, 1) + enc_bias
     features = jnp.maximum(preact, 0.0).astype(jnp.bfloat16)
-    partial_recon = jnp.einsum(
-        "rf,lfd->rld", features, dec_weight, preferred_element_type=jnp.float32
-    )
-    recon = (
-        lax.psum(partial_recon.astype(jnp.bfloat16), "latent").astype(jnp.float32) + dec_bias[None]
-    )
-    recon_error = (recon - clean_acts.astype(jnp.float32)).astype(jnp.bfloat16)
-    partial_grad = jnp.einsum(
-        "rld,lfd->rf", recon_error, dec_weight, preferred_element_type=jnp.float32
-    )
+    dec4 = dec_weight[0].reshape(lat_count, RING, RING, chunk)
+    recon_a = jnp.einsum("rf,fabd->bard", features[:half], dec4, preferred_element_type=jnp.float32)
+    recon_b = jnp.einsum("rf,fabd->abrd", features[half:], dec4, preferred_element_type=jnp.float32)
+    recon_sum = latent_reduce(recon_a.astype(jnp.bfloat16), recon_b.astype(jnp.bfloat16), 3)
+    bias_part = lax.dynamic_slice_in_dim(dec_bias[0], me * chunk, chunk)
+    clean_part = lax.dynamic_slice_in_dim(clean_acts[:, 0, :], me * chunk, chunk, axis=1)
+    recon_error = (
+        recon_sum + bias_part - clean_part.reshape(2, half, chunk).astype(jnp.float32)
+    ).astype(jnp.bfloat16)
+    error_a, error_b = latent_gather(recon_error, 4)
+    grad_a = jnp.einsum("abrd,fabd->rf", error_a, dec4, preferred_element_type=jnp.float32)
+    grad_b = jnp.einsum("bard,fabd->rf", error_b, dec4, preferred_element_type=jnp.float32)
+    partial_grad = jnp.concatenate([grad_a, grad_b], axis=0)
     feat_grad = layer_sum(partial_grad.astype(jnp.bfloat16), 2)
     row_ids = lax.axis_index("row") * row_count + jnp.arange(row_count, dtype=jnp.int32)
-    latent_ids = lax.axis_index("latent") * lat_count + jnp.arange(lat_count, dtype=jnp.int32)
+    latent_ids = me * lat_count + jnp.arange(lat_count, dtype=jnp.int32)
     every_row = jnp.arange(all_rows, dtype=jnp.int32)
     pair_table = (
         (every_row[None, :] == row_ids[:, None]).astype(jnp.float32)
@@ -94,13 +259,11 @@
     target_hot = (targets[:, None] == latent_ids[None, :]).astype(jnp.bfloat16)
     margin_table = jnp.dot(pair_table, target_hot, preferred_element_type=jnp.float32)
     pre_grad = jnp.where(preact > 0, feat_grad - MARGIN * margin_table, 0.0).astype(jnp.bfloat16)
-    enc_split = enc_weight[0].reshape(n_lat, chunk, lat_count)
-    partial_input = jnp.einsum(
-        "rf,gdf->grd", pre_grad, enc_split, preferred_element_type=jnp.float32
-    ).astype(jnp.bfloat16)
-    gathered = lax.all_to_all(partial_input, "latent", 0, 0, tiled=True)
-    total = jnp.sum(gathered.astype(jnp.float32), axis=0).astype(jnp.bfloat16)
-    return total[:, None, :]
+    enc4 = enc_weight[0].reshape(RING, RING, chunk, lat_count)
+    input_a = jnp.einsum("rf,abdf->bard", pre_grad[:half], enc4, preferred_element_type=jnp.float32)
+    input_b = jnp.einsum("rf,abdf->abrd", pre_grad[half:], enc4, preferred_element_type=jnp.float32)
+    total = latent_reduce(input_a.astype(jnp.bfloat16), input_b.astype(jnp.bfloat16), 5)
+    return total.reshape(row_count, 1, chunk).astype(jnp.bfloat16)
 
 
 def solution(mesh):

time: 256 us -> 233 us (0.910)
  Pallas kernels: 55 us -> 171 us
  waiting for transfers between devices: 100 us -> 0 us
  blocking collectives: 48.6 us -> 0 us
  local copies, waits for them, and re-layouts: 0.7 us -> 20.6 us
  between operations: 13.5 us -> 0.23 us
    pallas_call x0 -> x3, Pallas kernels: none -> 116 us  [the longest x2 78.1 us: latent_reduce(): pl.pallas_call(_reduce_kernel, out_shape=jax.ShapeDtypeStruct((2, h, c),...]
    psum x1 -> x0, waiting for transfers between devices: 100 us -> none  [local(): lax.psum(partial_recon.astype(jnp.bfloat16), 'latent').astype(jnp.float32)]
    all_to_all x1 -> x0, blocking collectives: 48.6 us -> none  [local(): gathered = lax.all_to_all(partial_input, 'latent', 0, 0, tiled=True)]
    convert_element_type x0 -> x5, local copies, waits for them, and re-layouts: none -> 10.4 us  [the longest x1 2.54 us: local(): recon_a.astype(jnp.bfloat16)]
    unnamed x0 -> x2, matrix products: none -> 9.88 us
    dot_general x3 -> x5, matrix products: 25.8 us -> 17.3 us  [the longest x1 4.37 us: local(): jnp.einsum('abrd,fabd->rf', error_a, dec4, preferred_element_type=jnp.flo...]
    unnamed x10 -> x17, local copies, waits for them, and re-layouts: 0.7 us -> 8.95 us
    convert_element_type x0 -> x5, other arithmetic: none -> 4.89 us  [the longest x1 1.83 us: local(): recon_error = (recon_sum + bias_part - clean_part.reshape(2, half, chunk)...]
  transfers between devices with their start and end apart: 1 -> 0, of which waited for: 1 -> 0; matrix products, arithmetic and copies ran while one was open for 0% -> 0% of each run, Pallas kernels for 0% -> 0%
where the time goes in v3:
time: 233 us
  Pallas kernels  171 us (73%)
  matrix products  35 us (15%)
  local copies, waits for them, and re-layouts  20.6 us (9%)
  other arithmetic  5.83 us (3%)
    pallas_call x2, Pallas kernels, latent_reduce(): pl.pallas_call(_reduce_kernel, out_shape=jax.ShapeDtypeStruct((2, h, c),...  78.1 us
    pallas_call x2, Pallas kernels, layer_sum(): pl.pallas_call(_layer_sum_kernel, out_shape=jax.ShapeDtypeStruct((rows, c...  55 us
    pallas_call x1, Pallas kernels, latent_gather(): pl.pallas_call(_gather_kernel, out_shape=(full, full), in_specs=[pl.Block...  37.9 us
    unnamed x2, matrix products  9.88 us
    unnamed x17, local copies, waits for them, and re-layouts  8.95 us
    dot_general x1, matrix products, local(): jnp.einsum('rld,ldf->rf', inputs, enc_weight, preferred_element_type=jnp....  7.83 us

profile of v3, /device:TPU:1, one launch (start us, length us, event | category | flops | bytes accessed | tf_op | source)
XLA Modules:
  0.0 232.7 jit_solution(6717579130989759648)
XLA Ops:
  0.0 1.1 constant_dynamic-slice_fusion
  1.2 7.8 %fusion.4.x_ref = f32[512,768]{1,0:T(8,128)} fusion(bf16[1,3584,768]{2,1,0:T(8,128)(2,1)} %param.10, bf16[512,1,3584]{2,0,1:T(8,128)(2,1)} %param.8), kind=kOutput, calls=%fused_computation.4 | convolution fusion | flops 2818572288 | bytes 10747904 | tf_op jit(solution)/shard_map/rld,ldf->rf/dot_general | solution.py:235
  9.1 28.0 %shard_map.82 = f32[512,768]{1,0:T(8,128)} custom-call(f32[512,768]{1,0:T(8,128)} %fusion.4.x_ref), custom_call_target="tpu_custom_call" | custom-call | tf_op jit(solution)/shard_map/pallas_call | solution.py:211
  37.1 1.5 maximum_convert_fusion
  38.7 4.9 %fusion.2 = f32[256,3584]{0,1:S(1)} fusion(bf16[1,768,3584]{2,1,0:T(8,128)(2,1)} %param.12, bf16[512,768]{1,0:T(8,128)(2,1)S(1)} %maximum_convert_fusion), kind=kOutput, calls=%fused_computation.2 | convolution fusion | flops 1409286144 | bytes 9568256
  43.9 2.5 %copy.29 = bf16[256,4,4,224]{3,0,1,2:T(8,128)(2,1)} copy(bf16[256,4,4,224]{0,3,2,1:T(8,128)(2,1)S(1)} %convert_element_type.61) | data formatting | bytes 3670016 | tf_op jit(solution)/shard_map/convert_element_type | solution.py:241
  46.4 4.9 %fusion = f32[256,3584]{0,1:S(1)} fusion(bf16[1,768,3584]{2,1,0:T(8,128)(2,1)} %param.12, bf16[512,768]{1,0:T(8,128)(2,1)S(1)} %maximum_convert_fusion), kind=kOutput, calls=%fused_computation | convolution fusion | flops 1409286144 | bytes 9568256
  51.6 2.3 %copy.30 = bf16[256,4,4,224]{3,0,2,1:T(8,128)(2,1)} copy(bf16[256,4,4,224]{0,3,2,1:T(8,128)(2,1)S(1)} %convert_element_type.63) | data formatting | bytes 3670016 | tf_op jit(solution)/shard_map/convert_element_type | solution.py:241
  53.9 40.8 %shard_map.83 = f32[2,256,224]{2,1,0:T(8,128)} custom-call(bf16[4,4,256,224]{3,2,1,0:T(8,128)(2,1)} %bitcast.56, bf16[4,4,256,224]{3,2,1,0:T(8,128)(2,1)} %bitcast.58), custom_call_target="tpu_custom_call" | custom-call | tf_op jit(solution)/shard_map/pallas_call | solution.py:91
  94.7 1.8 fusion.24.e
  96.5 37.9 %shard_map.84 = (bf16[4,4,256,224]{3,2,1,0:T(8,128)(2,1)}, bf16[4,4,256,224]{3,2,1,0:T(8,128)(2,1)}) custom-call(bf16[2,256,224]{2,1,0:T(8,128)(2,1)} %fusion.24.e), custom_call_target="tpu_custom_call" | custom-call | tf_op jit(solution)/shard_map/pallas_call | solution.py:156
  134.5 8.5 %copy.28 = bf16[1,768,3584]{1,2,0:T(8,128)(2,1)} copy(bf16[1,768,3584]{2,1,0:T(8,128)(2,1)} %param.12) | data formatting | bytes 11010048 | tf_op args[4]
  142.9 4.4 %fusion.18 = bf16[256,768]{1,0:T(8,128)(2,1)S(1)} fusion(bf16[4,4,256,224]{3,2,1,0:T(8,128)(2,1)S(1)} %copy-done.5, bf16[768,4,4,224]{0,3,2,1:T(8,128)(2,1)} %bitcast.60), kind=kOutput, calls=%fused_computation.21 | convolution fusion | flops 1409482752 | bytes 7733248 | tf_op jit(solution)/shard_map/abrd,fabd->rf/dot_general | solution.py:248
  147.8 1.7 fusion.19
  149.5 0.9 pad_maximum_fusion.x_ref
  150.4 27.0 %shard_map.85 = f32[512,768]{1,0:T(8,128)} custom-call(bf16[512,768]{1,0:T(8,128)(2,1)} %pad_maximum_fusion.x_ref), custom_call_target="tpu_custom_call" | custom-call | tf_op jit(solution)/shard_map/pallas_call | solution.py:211
  177.5 2.9 %select_convert_fusion = bf16[512,768]{1,0:T(8,128)(2,1)S(1)} fusion(f32[512,768]{1,0:T(8,128)} %shard_map.85, f32[512,768]{1,0:T(8,128)S(1)} %copy-done.1, s32[768]{0:T(1024)S(1)} %iota_add_fusion, s32[1024]{0:T(1024)S(1)} %copy-done.6, s32[1024]{0:T(1024)S(1)} %copy-done.7, s32[512]{0:T(512)S(1)} %iota_add_fusion.1, f32[768]{0:T(1024)S(1)} %copy-done.3), kind=kOutput, calls=%fused_computation.15 | convolution fusion | flops 811597824 | bytes 3948544 | tf_op jit(solution)/shard_map/dot_general | solution.py:260
  180.4 4.2 %convolution_convert_fusion.1 = bf16[256,4,4,224]{0,3,2,1:T(8,128)(2,1)S(1)} fusion(bf16[4,4,224,768]{3,2,1,0:T(8,128)(2,1)} %bitcast.65, bf16[512,768]{1,0:T(8,128)(2,1)S(1)} %select_convert_fusion), kind=kOutput, calls=%fused_computation.14 | convolution fusion | flops 1410203648 | bytes 7733248 | tf_op jit(solution)/shard_map/rf,abdf->bard/dot_general | solution.py:263
  184.6 2.4 %copy.33 = bf16[256,4,4,224]{3,0,1,2:T(8,128)(2,1)} copy(bf16[256,4,4,224]{0,3,2,1:T(8,128)(2,1)S(1)} %convolution_convert_fusion.1) | data formatting | bytes 3670016 | tf_op jit(solution)/shard_map/convert_element_type | solution.py:265
  186.9 4.2 %convolution_convert_fusion = bf16[256,4,4,224]{0,3,2,1:T(8,128)(2,1)S(1)} fusion(bf16[4,4,224,768]{3,2,1,0:T(8,128)(2,1)} %bitcast.66, bf16[512,768]{1,0:T(8,128)(2,1)S(1)} %select_convert_fusion), kind=kOutput, calls=%fused_computation.13 | convolution fusion | flops 1410203648 | bytes 7733248 | tf_op jit(solution)/shard_map/rf,abdf->abrd/dot_general | solution.py:264
  191.1 2.3 %copy.34 = bf16[256,4,4,224]{3,0,2,1:T(8,128)(2,1)} copy(bf16[256,4,4,224]{0,3,2,1:T(8,128)(2,1)S(1)} %convolution_convert_fusion) | data formatting | bytes 3670016 | tf_op jit(solution)/shard_map/convert_element_type | solution.py:265
  193.5 37.3 %shard_map.86 = f32[2,256,224]{2,1,0:T(8,128)} custom-call(bf16[4,4,256,224]{3,2,1,0:T(8,128)(2,1)} %bitcast.57, bf16[4,4,256,224]{3,2,1,0:T(8,128)(2,1)} %bitcast.59), custom_call_target="tpu_custom_call" | custom-call | tf_op jit(solution)/shard_map/pallas_call | solution.py:91
  230.8 1.1 convert_element_type.76
  231.9 0.8 copy.35
  (21 shorter events, 1.0 us)
Async XLA Ops:
  0.0 1.2 copy-start
  9.1 28.1 %copy-start.3 = (f32[768]{0:T(1024)S(1)}, f32[768]{0:T(1024)}, u32[]{:S(2)}) copy-start(f32[768]{0:T(1024)} %param.11) | copy-start | bytes 9220
  134.4 8.5 %copy-start.5 = (bf16[4,4,256,224]{3,2,1,0:T(8,128)(2,1)S(1)}, bf16[4,4,256,224]{3,2,1,0:T(8,128)(2,1)}, u32[]{:S(2)}) copy-start(bf16[4,4,256,224]{3,2,1,0:T(8,128)(2,1)} %get-tuple-element.7) | copy-start | bytes 5505028
  142.9 4.4 %copy-start.2 = (bf16[1,768,3584]{1,2,0:T(8,128)(2,1)S(1)}, bf16[1,768,3584]{1,2,0:T(8,128)(2,1)}, u32[]{:S(2)}) copy-start(bf16[1,768,3584]{1,2,0:T(8,128)(2,1)} %copy.28) | copy-start | bytes 16515076
  142.9 4.8 %copy-start.4 = (bf16[4,4,256,224]{3,2,1,0:T(8,128)(2,1)S(1)}, bf16[4,4,256,224]{3,2,1,0:T(8,128)(2,1)}, u32[]{:S(2)}) copy-start(bf16[4,4,256,224]{3,2,1,0:T(8,128)(2,1)} %get-tuple-element.8) | copy-start | bytes 5505028
  149.5 28.0 %copy-start.1 = (f32[512,768]{1,0:T(8,128)S(1)}, f32[512,768]{1,0:T(8,128)}, u32[]{:S(2)}) copy-start(f32[512,768]{1,0:T(8,128)} %shard_map.82) | copy-start | bytes 4718596
  149.5 28.0 %copy-start.6 = (s32[1024]{0:T(1024)S(1)}, s32[1024]{0:T(1024)}, u32[]{:S(2)}) copy-start(s32[1024]{0:T(1024)} %param.15) | copy-start | bytes 12292
  149.5 28.0 %copy-start.7 = (s32[1024]{0:T(1024)S(1)}, s32[1024]{0:T(1024)}, u32[]{:S(2)}) copy-start(s32[1024]{0:T(1024)} %param.14) | copy-start | bytes 12292

commit v4 on v3

--- a/solution.py
+++ b/solution.py
@@ -17,72 +17,116 @@
 
 def _greet(a, b):
     barrier = pltpu.get_barrier_semaphore()
-    for k in range(1, RING):
-        pl.semaphore_signal(barrier, inc=1, device_id={"latent": a * RING + (b + k) % RING}, device_id_type=MESH)
-        pl.semaphore_signal(barrier, inc=1, device_id={"latent": ((a + k) % RING) * RING + b}, device_id_type=MESH)
-    pl.semaphore_wait(barrier, 2 * (RING - 1))
-
-
-def _copy(src, dst, send_sem, recv_sem, peer):
-    return pltpu.make_async_remote_copy(
-        src_ref=src, dst_ref=dst, send_sem=send_sem, recv_sem=recv_sem,
-        device_id={"latent": peer}, device_id_type=MESH,
-    )
-
-
-def _reduce_kernel(xa, xb, out, r1a, r1b, s1a, s1b, r2a, r2b, send_sems, recv_sems):
+    for peer in (a * RING + (b + 1) % RING, a * RING + (b + RING - 1) % RING,
+                 ((a + 1) % RING) * RING + b, ((a + RING - 1) % RING) * RING + b):
+        pl.semaphore_signal(barrier, inc=1, device_id={"latent": peer}, device_id_type=MESH)
+    pl.semaphore_wait(barrier, 4)
+
+
+def _rows(ref, lo, n):
+    return ref.at[(slice(None),) * (len(ref.shape) - 2) + (pl.ds(lo, n), slice(None))]
+
+
+class _RingStage:
+    def __init__(self, src, dst, relay_l, relay_r, send_sems, recv_sems, a, b, on_z):
+        self.src, self.dst = src, dst
+        self.relay_l, self.relay_r = relay_l, relay_r
+        self.ss, self.rs = send_sems, recv_sems
+        self.a, self.b, self.on_z = a, b, on_z
+        self.m = b if on_z else a
+        self.p1 = (self.m + 1) % RING
+        self.m1 = (self.m + RING - 1) % RING
+        self.p2 = (self.m + 2) % RING
+        self.sent = []
+
+    def _peer(self, c):
+        return self.a * RING + c if self.on_z else c * RING + self.b
+
+    def _copy(self, src, dst, k, c):
+        return pltpu.make_async_remote_copy(
+            src_ref=src, dst_ref=dst, send_sem=self.ss.at[k], recv_sem=self.rs.at[k],
+            device_id={"latent": self._peer(c)}, device_id_type=MESH,
+        )
+
+    def _half(self):
+        return self.relay_l.shape[-2]
+
+    def start(self):
+        h = self._half()
+        far = self.src(self.p2)
+        for c in (
+            self._copy(self.src(self.p1), self.dst(self.m), 0, self.p1),
+            self._copy(self.src(self.m1), self.dst(self.m), 1, self.m1),
+            self._copy(_rows(far, 0, h), self.relay_l, 2, self.p1),
+            self._copy(_rows(far, h, h), self.relay_r, 3, self.m1),
+        ):
+            c.start()
+            self.sent.append(c)
+
+    def forward(self):
+        h = self._half()
+        self._copy(self.relay_l, self.relay_l, 2, 0).wait_recv()
+        fl = self._copy(self.relay_l, _rows(self.dst(self.m1), 0, h), 4, self.p1)
+        fl.start()
+        self._copy(self.relay_r, self.relay_r, 3, 0).wait_recv()
+        fr = self._copy(self.relay_r, _rows(self.dst(self.p1), h, h), 5, self.m1)
+        fr.start()
+        self.sent += [fl, fr]
+
+    def finish(self):
+        h = self._half()
+        self._copy(self.src(0), self.dst(self.m1), 0, 0).wait_recv()
+        self._copy(self.src(0), self.dst(self.p1), 1, 0).wait_recv()
+        self._copy(self.relay_l, _rows(self.dst(self.p2), 0, h), 4, 0).wait_recv()
+        self._copy(self.relay_r, _rows(self.dst(self.p2), h, h), 5, 0).wait_recv()
+
+    def drain(self):
+        for c in self.sent:
+            c.wait_send()
+
+
+def _reduce_kernel(xa, xb, out, r1a, r1b, s1a, s1b, r2a, r2b, l1, r1, l2, r2, send_sems, recv_sems):
     a, b = _latent_coords()
     _greet(a, b)
-    peers_z = [(b + k) % RING for k in range(1, RING)]
-    peers_x = [(a + k) % RING for k in range(1, RING)]
-    first = []
-    for t in peers_z:
-        c = _copy(xa.at[t], r1a.at[b], send_sems.at[0, t], recv_sems.at[0, b], a * RING + t)
-        c.start()
-        first.append(c)
-    for t in peers_x:
-        c = _copy(xb.at[t], r1b.at[a], send_sems.at[1, t], recv_sems.at[1, a], t * RING + b)
-        c.start()
-        first.append(c)
-    for t in peers_z:
-        _copy(xa.at[t], r1a.at[t], send_sems.at[0, t], recv_sems.at[0, t], 0).wait_recv()
-    for t in peers_x:
-        _copy(xb.at[t], r1b.at[t], send_sems.at[1, t], recv_sems.at[1, t], 0).wait_recv()
+    st_a = _RingStage(lambda c: xa.at[c], lambda s: r1a.at[s], l1.at[0], r1.at[0],
+                      send_sems.at[0], recv_sems.at[0], a, b, True)
+    st_b = _RingStage(lambda c: xb.at[c], lambda s: r1b.at[s], l1.at[1], r1.at[1],
+                      send_sems.at[1], recv_sems.at[1], a, b, False)
+    for st in (st_a, st_b):
+        st.start()
+    for st in (st_a, st_b):
+        st.forward()
+    for st in (st_a, st_b):
+        st.finish()
     sum_a = xa[b].astype(jnp.float32)
-    for t in peers_z:
-        sum_a = sum_a + r1a[t].astype(jnp.float32)
     sum_b = xb[a].astype(jnp.float32)
-    for t in peers_x:
-        sum_b = sum_b + r1b[t].astype(jnp.float32)
+    for k in range(1, RING):
+        sum_a = sum_a + r1a[(b + k) % RING].astype(jnp.float32)
+        sum_b = sum_b + r1b[(a + k) % RING].astype(jnp.float32)
     s1a[...] = sum_a.astype(s1a.dtype)
     s1b[...] = sum_b.astype(s1b.dtype)
-    second = []
-    for t in peers_x:
-        c = _copy(s1a.at[t], r2a.at[a], send_sems.at[2, t], recv_sems.at[2, a], t * RING + b)
-        c.start()
-        second.append(c)
-    for t in peers_z:
-        c = _copy(s1b.at[t], r2b.at[b], send_sems.at[3, t], recv_sems.at[3, b], a * RING + t)
-        c.start()
-        second.append(c)
-    for t in peers_x:
-        _copy(s1a.at[t], r2a.at[t], send_sems.at[2, t], recv_sems.at[2, t], 0).wait_recv()
-    for t in peers_z:
-        _copy(s1b.at[t], r2b.at[t], send_sems.at[3, t], recv_sems.at[3, t], 0).wait_recv()
+    nd_a = _RingStage(lambda c: s1a.at[c], lambda s: r2a.at[s], l2.at[0], r2.at[0],
+                      send_sems.at[2], recv_sems.at[2], a, b, False)
+    nd_b = _RingStage(lambda c: s1b.at[c], lambda s: r2b.at[s], l2.at[1], r2.at[1],
+                      send_sems.at[3], recv_sems.at[3], a, b, True)
+    for st in (nd_a, nd_b):
+        st.start()
+    for st in (nd_a, nd_b):
+        st.forward()
+    for st in (nd_a, nd_b):
+        st.finish()
     own_a = xa[b, a].astype(jnp.float32)
-    for t in peers_z:
-        own_a = own_a + r1a[t, a].astype(jnp.float32)
     own_b = xb[a, b].astype(jnp.float32)
-    for t in peers_x:
-        own_b = own_b + r1b[t, b].astype(jnp.float32)
-    for t in peers_x:
-        own_a = own_a + r2a[t].astype(jnp.float32)
-    for t in peers_z:
-        own_b = own_b + r2b[t].astype(jnp.float32)
+    for k in range(1, RING):
+        own_a = own_a + r1a[(b + k) % RING, a].astype(jnp.float32)
+        own_b = own_b + r1b[(a + k) % RING, b].astype(jnp.float32)
+    for k in range(1, RING):
+        own_a = own_a + r2a[(a + k) % RING].astype(jnp.float32)
+        own_b = own_b + r2b[(b + k) % RING].astype(jnp.float32)
     out[0] = own_a
     out[1] = own_b
-    for c in first + second:
-        c.wait_send()
+    for st in (st_a, st_b, nd_a, nd_b):
+        st.drain()
 
 
 def latent_reduce(xa, xb, collective_id):
@@ -100,52 +144,49 @@
             pltpu.VMEM((n, h, c), dt),
             pltpu.VMEM((n, h, c), dt),
             pltpu.VMEM((n, h, c), dt),
-            pltpu.SemaphoreType.DMA((4, n)),
-            pltpu.SemaphoreType.DMA((4, n)),
+            pltpu.VMEM((2, n, h // 2, c), dt),
+            pltpu.VMEM((2, n, h // 2, c), dt),
+            pltpu.VMEM((2, h // 2, c), dt),
+            pltpu.VMEM((2, h // 2, c), dt),
+            pltpu.SemaphoreType.DMA((4, 6)),
+            pltpu.SemaphoreType.DMA((4, 6)),
         ],
         compiler_params=pltpu.CompilerParams(collective_id=collective_id, has_side_effects=True),
     )(xa, xb)
 
 
-def _gather_kernel(e, oa, ob, g1a, g1b, ga, gb, send_sems, recv_sems):
+def _gather_kernel(e, oa, ob, g1a, g1b, ga, gb, l1, r1, l2, r2, send_sems, recv_sems):
     a, b = _latent_coords()
     _greet(a, b)
-    peers_z = [(b + k) % RING for k in range(1, RING)]
-    peers_x = [(a + k) % RING for k in range(1, RING)]
-    first = []
-    for t in peers_z:
-        c = _copy(e.at[0], g1a.at[b], send_sems.at[0, t], recv_sems.at[0, b], a * RING + t)
-        c.start()
-        first.append(c)
-    for t in peers_x:
-        c = _copy(e.at[1], g1b.at[a], send_sems.at[1, t], recv_sems.at[1, a], t * RING + b)
-        c.start()
-        first.append(c)
+    st_a = _RingStage(lambda c: e.at[0], lambda s: g1a.at[s], l1.at[0], r1.at[0],
+                      send_sems.at[0], recv_sems.at[0], a, b, True)
+    st_b = _RingStage(lambda c: e.at[1], lambda s: g1b.at[s], l1.at[1], r1.at[1],
+                      send_sems.at[1], recv_sems.at[1], a, b, False)
+    for st in (st_a, st_b):
+        st.start()
     g1a[b] = e[0]
     g1b[a] = e[1]
-    for t in peers_z:
-        _copy(e.at[0], g1a.at[t], send_sems.at[0, t], recv_sems.at[0, t], 0).wait_recv()
-    for t in peers_x:
-        _copy(e.at[1], g1b.at[t], send_sems.at[1, t], recv_sems.at[1, t], 0).wait_recv()
-    second = []
-    for t in peers_x:
-        c = _copy(g1a, ga.at[a], send_sems.at[2, t], recv_sems.at[2, a], t * RING + b)
-        c.start()
-        second.append(c)
-    for t in peers_z:
-        c = _copy(g1b, gb.at[b], send_sems.at[3, t], recv_sems.at[3, b], a * RING + t)
-        c.start()
-        second.append(c)
+    for st in (st_a, st_b):
+        st.forward()
+    for st in (st_a, st_b):
+        st.finish()
+    nd_a = _RingStage(lambda c: g1a, lambda s: ga.at[s], l2.at[0], r2.at[0],
+                      send_sems.at[2], recv_sems.at[2], a, b, False)
+    nd_b = _RingStage(lambda c: g1b, lambda s: gb.at[s], l2.at[1], r2.at[1],
+                      send_sems.at[3], recv_sems.at[3], a, b, True)
+    for st in (nd_a, nd_b):
+        st.start()
     oa[a] = g1a[...]
     ob[b] = g1b[...]
-    for t in peers_x:
-        _copy(g1a, ga.at[t], send_sems.at[2, t], recv_sems.at[2, t], 0).wait_recv()
-        oa[t] = ga[t]
-    for t in peers_z:
-        _copy(g1b, gb.at[t], send_sems.at[3, t], recv_sems.at[3, t], 0).wait_recv()
-        ob[t] = gb[t]
-    for c in first + second:
-        c.wait_send()
+    for st in (nd_a, nd_b):
+        st.forward()
+    for st in (nd_a, nd_b):
+        st.finish()
+    for k in range(1, RING):
+        oa[(a + k) % RING] = ga[(a + k) % RING]
+        ob[(b + k) % RING] = gb[(b + k) % RING]
+    for st in (st_a, st_b, nd_a, nd_b):
+        st.drain()
 
 
 def latent_gather(e, collective_id):
@@ -163,8 +204,12 @@
             pltpu.VMEM((n, h, c), dt),
             pltpu.VMEM((n, n, h, c), dt),
             pltpu.VMEM((n, n, h, c), dt),
-            pltpu.SemaphoreType.DMA((4, n)),
-            pltpu.SemaphoreType.DMA((4, n)),
+            pltpu.VMEM((2, h // 2, c), dt),
+            pltpu.VMEM((2, h // 2, c), dt),
+            pltpu.VMEM((2, n, h // 2, c), dt),
+            pltpu.VMEM((2, n, h // 2, c), dt),
+            pltpu.SemaphoreType.DMA((4, 6)),
+            pltpu.SemaphoreType.DMA((4, 6)),
         ],
         compiler_params=pltpu.CompilerParams(collective_id=collective_id, has_side_effects=True),
     )(e)

time: 233 us -> 242 us (1.039)
  Pallas kernels: 171 us -> 178 us
    pallas_call x2, Pallas kernels: 55 us -> 60.7 us  [layer_sum(): pl.pallas_call(_layer_sum_kernel, out_shape=jax.ShapeDtypeStruct((rows, c...]
    pallas_call x2, Pallas kernels: 78.1 us -> 81.8 us  [latent_reduce(): pl.pallas_call(_reduce_kernel, out_shape=jax.ShapeDtypeStruct((2, h, c),...]
where the time goes in v4:
time: 242 us; the launch traced here: 240 us
  Pallas kernels  178 us (74%)
  matrix products  35 us (14%)
  local copies, waits for them, and re-layouts  20.6 us (9%)
  other arithmetic  5.83 us (2%)
    pallas_call x2, Pallas kernels, latent_reduce(): pl.pallas_call(_reduce_kernel, out_shape=jax.ShapeDtypeStruct((2, h, c),...  81.8 us
    pallas_call x2, Pallas kernels, layer_sum(): pl.pallas_call(_layer_sum_kernel, out_shape=jax.ShapeDtypeStruct((rows, c...  60.7 us
    pallas_call x1, Pallas kernels, latent_gather(): pl.pallas_call(_gather_kernel, out_shape=(full, full), in_specs=[pl.Block...  35.8 us
    unnamed x2, matrix products  9.88 us
    unnamed x17, local copies, waits for them, and re-layouts  8.96 us
    dot_general x1, matrix products, local(): jnp.einsum('rld,ldf->rf', inputs, enc_weight, preferred_element_type=jnp....  7.83 us

profile of v4, /device:TPU:1, one launch (start us, length us, event | category | flops | bytes accessed | tf_op | source)
XLA Modules:
  0.0 240.0 jit_solution(3537970602716877105)
XLA Ops:
  0.0 1.1 constant_dynamic-slice_fusion
  1.2 7.8 %fusion.4.x_ref = f32[512,768]{1,0:T(8,128)} fusion(bf16[1,3584,768]{2,1,0:T(8,128)(2,1)} %param.10, bf16[512,1,3584]{2,0,1:T(8,128)(2,1)} %param.8), kind=kOutput, calls=%fused_computation.4 | convolution fusion | flops 2818572288 | bytes 10747904 | tf_op jit(solution)/shard_map/rld,ldf->rf/dot_general | solution.py:280
  9.1 28.0 %shard_map.82 = f32[512,768]{1,0:T(8,128)} custom-call(f32[512,768]{1,0:T(8,128)} %fusion.4.x_ref), custom_call_target="tpu_custom_call" | custom-call | tf_op jit(solution)/shard_map/pallas_call | solution.py:256
  37.1 1.5 maximum_convert_fusion
  38.7 4.9 %fusion.2 = f32[256,3584]{0,1:S(1)} fusion(bf16[1,768,3584]{2,1,0:T(8,128)(2,1)} %param.12, bf16[512,768]{1,0:T(8,128)(2,1)S(1)} %maximum_convert_fusion), kind=kOutput, calls=%fused_computation.2 | convolution fusion | flops 1409286144 | bytes 9568256
  43.9 2.5 %copy.29 = bf16[256,4,4,224]{3,0,1,2:T(8,128)(2,1)} copy(bf16[256,4,4,224]{0,3,2,1:T(8,128)(2,1)S(1)} %convert_element_type.61) | data formatting | bytes 3670016 | tf_op jit(solution)/shard_map/convert_element_type | solution.py:286
  46.4 4.9 %fusion = f32[256,3584]{0,1:S(1)} fusion(bf16[1,768,3584]{2,1,0:T(8,128)(2,1)} %param.12, bf16[512,768]{1,0:T(8,128)(2,1)S(1)} %maximum_convert_fusion), kind=kOutput, calls=%fused_computation | convolution fusion | flops 1409286144 | bytes 9568256
  51.6 2.3 copy.30
  53.9 42.6 %shard_map.83 = f32[2,256,224]{2,1,0:T(8,128)} custom-call(bf16[4,4,256,224]{3,2,1,0:T(8,128)(2,1)} %bitcast.56, bf16[4,4,256,224]{3,2,1,0:T(8,128)(2,1)} %bitcast.58), custom_call_target="tpu_custom_call" | custom-call | tf_op jit(solution)/shard_map/pallas_call | solution.py:135
  96.5 1.8 fusion.24.e
  98.4 35.8 %shard_map.84 = (bf16[4,4,256,224]{3,2,1,0:T(8,128)(2,1)}, bf16[4,4,256,224]{3,2,1,0:T(8,128)(2,1)}) custom-call(bf16[2,256,224]{2,1,0:T(8,128)(2,1)} %fusion.24.e), custom_call_target="tpu_custom_call" | custom-call | tf_op jit(solution)/shard_map/pallas_call | solution.py:197
  134.2 8.5 %copy.28 = bf16[1,768,3584]{1,2,0:T(8,128)(2,1)} copy(bf16[1,768,3584]{2,1,0:T(8,128)(2,1)} %param.12) | data formatting | bytes 11010048 | tf_op args[4]
  142.7 4.4 %fusion.18 = bf16[256,768]{1,0:T(8,128)(2,1)S(1)} fusion(bf16[4,4,256,224]{3,2,1,0:T(8,128)(2,1)S(1)} %copy-done.5, bf16[768,4,4,224]{0,3,2,1:T(8,128)(2,1)} %bitcast.60), kind=kOutput, calls=%fused_computation.21 | convolution fusion | flops 1409482752 | bytes 7733248 | tf_op jit(solution)/shard_map/abrd,fabd->rf/dot_general | solution.py:293
  147.5 1.7 fusion.19
  149.2 0.9 pad_maximum_fusion.x_ref
  150.2 32.6 %shard_map.85 = f32[512,768]{1,0:T(8,128)} custom-call(bf16[512,768]{1,0:T(8,128)(2,1)} %pad_maximum_fusion.x_ref), custom_call_target="tpu_custom_call" | custom-call | tf_op jit(solution)/shard_map/pallas_call | solution.py:256
  182.9 2.9 %select_convert_fusion = bf16[512,768]{1,0:T(8,128)(2,1)S(1)} fusion(f32[512,768]{1,0:T(8,128)} %shard_map.85, f32[512,768]{1,0:T(8,128)S(1)} %copy-done.1, s32[768]{0:T(1024)S(1)} %iota_add_fusion, s32[1024]{0:T(1024)S(1)} %copy-done.6, s32[1024]{0:T(1024)S(1)} %copy-done.7, s32[512]{0:T(512)S(1)} %iota_add_fusion.1, f32[768]{0:T(1024)S(1)} %copy-done.3), kind=kOutput, calls=%fused_computation.15 | convolution fusion | flops 811597824 | bytes 3948544 | tf_op jit(solution)/shard_map/dot_general | solution.py:305
  185.7 4.2 %convolution_convert_fusion.1 = bf16[256,4,4,224]{0,3,2,1:T(8,128)(2,1)S(1)} fusion(bf16[4,4,224,768]{3,2,1,0:T(8,128)(2,1)} %bitcast.65, bf16[512,768]{1,0:T(8,128)(2,1)S(1)} %select_convert_fusion), kind=kOutput, calls=%fused_computation.14 | convolution fusion | flops 1410203648 | bytes 7733248 | tf_op jit(solution)/shard_map/rf,abdf->bard/dot_general | solution.py:308
  189.9 2.4 copy.33
  192.3 4.2 %convolution_convert_fusion = bf16[256,4,4,224]{0,3,2,1:T(8,128)(2,1)S(1)} fusion(bf16[4,4,224,768]{3,2,1,0:T(8,128)(2,1)} %bitcast.66, bf16[512,768]{1,0:T(8,128)(2,1)S(1)} %select_convert_fusion), kind=kOutput, calls=%fused_computation.13 | convolution fusion | flops 1410203648 | bytes 7733248 | tf_op jit(solution)/shard_map/rf,abdf->abrd/dot_general | solution.py:309
  196.5 2.3 copy.34
  198.8 39.3 %shard_map.86 = f32[2,256,224]{2,1,0:T(8,128)} custom-call(bf16[4,4,256,224]{3,2,1,0:T(8,128)(2,1)} %bitcast.57, bf16[4,4,256,224]{3,2,1,0:T(8,128)(2,1)} %bitcast.59), custom_call_target="tpu_custom_call" | custom-call | tf_op jit(solution)/shard_map/pallas_call | solution.py:135
  238.1 1.1 convert_element_type.76
  239.2 0.8 copy.35
  (21 shorter events, 1.0 us)
Async XLA Ops:
  0.0 1.2 copy-start
  9.1 28.1 %copy-start.3 = (f32[768]{0:T(1024)S(1)}, f32[768]{0:T(1024)}, u32[]{:S(2)}) copy-start(f32[768]{0:T(1024)} %param.11) | copy-start | bytes 9220
  134.2 8.5 %copy-start.5 = (bf16[4,4,256,224]{3,2,1,0:T(8,128)(2,1)S(1)}, bf16[4,4,256,224]{3,2,1,0:T(8,128)(2,1)}, u32[]{:S(2)}) copy-start(bf16[4,4,256,224]{3,2,1,0:T(8,128)(2,1)} %get-tuple-element.7) | copy-start | bytes 5505028
  142.7 4.4 %copy-start.2 = (bf16[1,768,3584]{1,2,0:T(8,128)(2,1)S(1)}, bf16[1,768,3584]{1,2,0:T(8,128)(2,1)}, u32[]{:S(2)}) copy-start(bf16[1,768,3584]{1,2,0:T(8,128)(2,1)} %copy.28) | copy-start | bytes 16515076
  142.7 4.8 %copy-start.4 = (bf16[4,4,256,224]{3,2,1,0:T(8,128)(2,1)S(1)}, bf16[4,4,256,224]{3,2,1,0:T(8,128)(2,1)}, u32[]{:S(2)}) copy-start(bf16[4,4,256,224]{3,2,1,0:T(8,128)(2,1)} %get-tuple-element.8) | copy-start | bytes 5505028
  149.2 33.6 %copy-start.1 = (f32[512,768]{1,0:T(8,128)S(1)}, f32[512,768]{1,0:T(8,128)}, u32[]{:S(2)}) copy-start(f32[512,768]{1,0:T(8,128)} %shard_map.82) | copy-start | bytes 4718596
  149.2 33.6 %copy-start.6 = (s32[1024]{0:T(1024)S(1)}, s32[1024]{0:T(1024)}, u32[]{:S(2)}) copy-start(s32[1024]{0:T(1024)} %param.15) | copy-start | bytes 12292
  149.2 33.6 %copy-start.7 = (s32[1024]{0:T(1024)S(1)}, s32[1024]{0:T(1024)}, u32[]{:S(2)}) copy-start(s32[1024]{0:T(1024)} %param.14) | copy-start | bytes 12292

commit v5 on v3

--- a/solution.py
+++ b/solution.py
@@ -236,17 +236,16 @@
     preact = layer_sum(partial_pre, 1) + enc_bias
     features = jnp.maximum(preact, 0.0).astype(jnp.bfloat16)
     dec4 = dec_weight[0].reshape(lat_count, RING, RING, chunk)
-    recon_a = jnp.einsum("rf,fabd->bard", features[:half], dec4, preferred_element_type=jnp.float32)
-    recon_b = jnp.einsum("rf,fabd->abrd", features[half:], dec4, preferred_element_type=jnp.float32)
+    recon_a = jnp.einsum("rf,fabd->badr", features[:half], dec4, preferred_element_type=jnp.float32)
+    recon_b = jnp.einsum("rf,fabd->abdr", features[half:], dec4, preferred_element_type=jnp.float32)
     recon_sum = latent_reduce(recon_a.astype(jnp.bfloat16), recon_b.astype(jnp.bfloat16), 3)
     bias_part = lax.dynamic_slice_in_dim(dec_bias[0], me * chunk, chunk)
     clean_part = lax.dynamic_slice_in_dim(clean_acts[:, 0, :], me * chunk, chunk, axis=1)
-    recon_error = (
-        recon_sum + bias_part - clean_part.reshape(2, half, chunk).astype(jnp.float32)
-    ).astype(jnp.bfloat16)
+    clean_t = jnp.swapaxes(clean_part.reshape(2, half, chunk), 1, 2).astype(jnp.float32)
+    recon_error = (recon_sum + bias_part[:, None] - clean_t).astype(jnp.bfloat16)
     error_a, error_b = latent_gather(recon_error, 4)
-    grad_a = jnp.einsum("abrd,fabd->rf", error_a, dec4, preferred_element_type=jnp.float32)
-    grad_b = jnp.einsum("bard,fabd->rf", error_b, dec4, preferred_element_type=jnp.float32)
+    grad_a = jnp.einsum("abdr,fabd->rf", error_a, dec4, preferred_element_type=jnp.float32)
+    grad_b = jnp.einsum("badr,fabd->rf", error_b, dec4, preferred_element_type=jnp.float32)
     partial_grad = jnp.concatenate([grad_a, grad_b], axis=0)
     feat_grad = layer_sum(partial_grad.astype(jnp.bfloat16), 2)
     row_ids = lax.axis_index("row") * row_count + jnp.arange(row_count, dtype=jnp.int32)
@@ -260,10 +259,10 @@
     margin_table = jnp.dot(pair_table, target_hot, preferred_element_type=jnp.float32)
     pre_grad = jnp.where(preact > 0, feat_grad - MARGIN * margin_table, 0.0).astype(jnp.bfloat16)
     enc4 = enc_weight[0].reshape(RING, RING, chunk, lat_count)
-    input_a = jnp.einsum("rf,abdf->bard", pre_grad[:half], enc4, preferred_element_type=jnp.float32)
-    input_b = jnp.einsum("rf,abdf->abrd", pre_grad[half:], enc4, preferred_element_type=jnp.float32)
+    input_a = jnp.einsum("rf,abdf->badr", pre_grad[:half], enc4, preferred_element_type=jnp.float32)
+    input_b = jnp.einsum("rf,abdf->abdr", pre_grad[half:], enc4, preferred_element_type=jnp.float32)
     total = latent_reduce(input_a.astype(jnp.bfloat16), input_b.astype(jnp.bfloat16), 5)
-    return total.reshape(row_count, 1, chunk).astype(jnp.bfloat16)
+    return jnp.swapaxes(total.astype(jnp.bfloat16), 1, 2).reshape(row_count, 1, chunk)
 
 
 def solution(mesh):

time: 233 us -> 213 us (0.914)
  Pallas kernels: 171 us -> 160 us
  local copies, waits for them, and re-layouts: 20.6 us -> 13.3 us
    convert_element_type x5 -> x1, local copies, waits for them, and re-layouts: 10.4 us -> 0.28 us  [local(): jnp.swapaxes(clean_part.reshape(2, half, chunk), 1, 2).astype(jnp.float32)]
    pallas_call x2, Pallas kernels: 78.1 us -> 70.4 us  [latent_reduce(): pl.pallas_call(_reduce_kernel, out_shape=jax.ShapeDtypeStruct((2, h, c),...]
    pallas_call x1, Pallas kernels: 37.9 us -> 31.9 us  [latent_gather(): pl.pallas_call(_gather_kernel, out_shape=(full, full), in_specs=[pl.Block...]
    unnamed x2, matrix products: 9.88 us -> 7.46 us
    unnamed x17 -> x26, local copies, waits for them, and re-layouts: 8.95 us -> 9.17 us
where the time goes in v5:
time: 213 us
  Pallas kernels  160 us (75%)
  matrix products  32.8 us (15%)
  local copies, waits for them, and re-layouts  13.3 us (6%)
  other arithmetic  6.98 us (3%)
    pallas_call x2, Pallas kernels, latent_reduce(): pl.pallas_call(_reduce_kernel, out_shape=jax.ShapeDtypeStruct((2, h, c),...  70.4 us
    pallas_call x2, Pallas kernels, layer_sum(): pl.pallas_call(_layer_sum_kernel, out_shape=jax.ShapeDtypeStruct((rows, c...  57.3 us
    pallas_call x1, Pallas kernels, latent_gather(): pl.pallas_call(_gather_kernel, out_shape=(full, full), in_specs=[pl.Block...  31.9 us
    unnamed x26, local copies, waits for them, and re-layouts  9.17 us
    dot_general x1, matrix products, local(): jnp.einsum('rld,ldf->rf', inputs, enc_weight, preferred_element_type=jnp....  7.86 us
    unnamed x2, matrix products  7.46 us
    dot_general x1, matrix products, local(): jnp.einsum('rf,abdf->abdr', pre_grad[half:], enc4, preferred_element_type...  5.53 us
    dot_general x1, matrix products, local(): jnp.einsum('abdr,fabd->rf', error_a, dec4, preferred_element_type=jnp.flo...  4.33 us

profile of v5, /device:TPU:1, one launch (start us, length us, event | category | flops | bytes accessed | tf_op | source)
XLA Modules:
  0.0 212.9 jit_solution(8334922843699878613)
XLA Ops:
  0.0 1.1 constant_dynamic-slice_fusion
  1.3 0.3 reshape.31
  1.7 7.9 %fusion.4.x_ref = f32[512,768]{1,0:T(8,128)} fusion(bf16[1,3584,768]{2,1,0:T(8,128)(2,1)} %param.10, bf16[512,1,3584]{2,0,1:T(8,128)(2,1)} %param.8), kind=kOutput, calls=%fused_computation.4 | convolution fusion | flops 2818572288 | bytes 10747904 | tf_op jit(solution)/shard_map/rld,ldf->rf/dot_general | solution.py:235
  9.5 28.1 %shard_map.82 = f32[512,768]{1,0:T(8,128)} custom-call(f32[512,768]{1,0:T(8,128)} %fusion.4.x_ref), custom_call_target="tpu_custom_call" | custom-call | tf_op jit(solution)/shard_map/pallas_call | solution.py:211
  37.6 1.7 maximum_convert_fusion
  39.3 5.0 %fusion.2 = f32[256,3584]{0,1:S(1)} fusion(bf16[1,768,3584]{2,1,0:T(8,128)(2,1)} %param.12, bf16[512,768]{1,0:T(8,128)(2,1)S(1)} %maximum_convert_fusion), kind=kOutput, calls=%fused_computation.2 | convolution fusion | flops 1409286144 | bytes 9568256
  44.4 1.5 copy.50
  45.9 2.4 %fusion = f32[256,3584]{0,1:S(1)} fusion(bf16[1,768,3584]{2,1,0:T(8,128)(2,1)S(1)} %bitcast.64, bf16[512,768]{1,0:T(8,128)(2,1)S(1)} %maximum_convert_fusion), kind=kOutput, calls=%fused_computation | convolution fusion | flops 1409286144 | bytes 9568256
  48.3 1.5 convert_bitcast_fusion.2.xb
  49.8 37.0 %shard_map.83 = f32[2,224,256]{2,1,0:T(8,128)} custom-call(bf16[4,4,224,256]{3,2,1,0:T(8,128)(2,1)} %bitcast.69, bf16[4,4,224,256]{3,2,1,0:T(8,128)(2,1)} %convert_bitcast_fusion.2.xb), custom_call_target="tpu_custom_call" | custom-call | tf_op jit(solution)/shard_map/pallas_call | solution.py:91
  86.8 1.8 fusion.29.e
  88.6 31.9 %shard_map.84 = (bf16[4,4,224,256]{3,2,1,0:T(8,128)(2,1)}, bf16[4,4,224,256]{3,2,1,0:T(8,128)(2,1)}) custom-call(bf16[2,224,256]{2,1,0:T(8,128)(2,1)} %fusion.29.e), custom_call_target="tpu_custom_call" | custom-call | tf_op jit(solution)/shard_map/pallas_call | solution.py:156
  120.5 8.6 %copy.23 = bf16[1,768,3584]{1,2,0:T(8,128)(2,1)} copy(bf16[1,768,3584]{2,1,0:T(8,128)(2,1)} %param.12) | data formatting | bytes 11010048 | tf_op args[4]
  129.0 4.3 %fusion.23 = bf16[256,768]{1,0:T(8,128)(2,1)S(1)} fusion(bf16[4,4,224,256]{3,2,1,0:T(8,128)(2,1)S(1)} %copy-done.4, bf16[768,4,4,224]{0,3,2,1:T(8,128)(2,1)} %bitcast.65), kind=kOutput, calls=%fused_computation.26 | convolution fusion | flops 1409482752 | bytes 7733248 | tf_op jit(solution)/shard_map/abdr,fabd->rf/dot_general | solution.py:247
  133.4 0.4 copy-done.3
  133.8 1.6 fusion.24
  135.5 0.9 pad_maximum_fusion.x_ref
  136.4 29.3 %shard_map.85 = f32[512,768]{1,0:T(8,128)} custom-call(bf16[512,768]{1,0:T(8,128)(2,1)} %pad_maximum_fusion.x_ref), custom_call_target="tpu_custom_call" | custom-call | tf_op jit(solution)/shard_map/pallas_call | solution.py:211
  165.8 3.0 %select_convert_fusion = bf16[512,768]{1,0:T(8,128)(2,1)S(1)} fusion(f32[512,768]{1,0:T(8,128)} %shard_map.85, f32[512,768]{1,0:T(8,128)S(1)} %copy-done.2, s32[768]{0:T(1024)S(1)} %iota_add_fusion, s32[1024]{0:T(1024)S(1)} %copy-done.6, s32[1024]{0:T(1024)S(1)} %copy-done.7, s32[512]{0:T(512)S(1)} %iota_add_fusion.1, f32[768]{0:T(1024)S(1)} %copy-done.5), kind=kOutput, calls=%fused_computation.20 | convolution fusion | flops 811597824 | bytes 3948544 | tf_op jit(solution)/shard_map/dot_general | solution.py:259
  168.8 5.5 %convert_bitcast_fusion.xb = bf16[4,4,224,256]{3,2,1,0:T(8,128)(2,1)} fusion(bf16[4,4,224,768]{3,2,1,0:T(8,128)(2,1)} %bitcast.71, bf16[512,768]{1,0:T(8,128)(2,1)S(1)} %select_convert_fusion), kind=kOutput, calls=%fused_computation.17 | convolution fusion | flops 1410203648 | bytes 7733248 | tf_op jit(solution)/shard_map/rf,abdf->abdr/dot_general | solution.py:263
  174.3 3.0 %convert_bitcast_fusion.1.xa = bf16[4,4,224,256]{3,2,1,0:T(8,128)(2,1)} fusion(bf16[4,4,224,768]{3,2,1,0:T(8,128)(2,1)S(1)} %bitcast.74, bf16[512,768]{1,0:T(8,128)(2,1)S(1)} %select_convert_fusion), kind=kOutput, calls=%fused_computation.18 | convolution fusion | flops 1410203648 | bytes 7733248 | tf_op jit(solution)/shard_map/rf,abdf->badr/dot_general | solution.py:262
  177.3 33.5 %shard_map.86 = f32[2,224,256]{2,1,0:T(8,128)} custom-call(bf16[4,4,224,256]{3,2,1,0:T(8,128)(2,1)} %convert_bitcast_fusion.1.xa, bf16[4,4,224,256]{3,2,1,0:T(8,128)(2,1)} %convert_bitcast_fusion.xb), custom_call_target="tpu_custom_call" | custom-call | tf_op jit(solution)/shard_map/pallas_call | solution.py:91
  210.8 1.0 convert_bitcast_fusion.3
  212.1 0.8 reshape.30
  (30 shorter events, 0.5 us)
Async XLA Ops:
  0.0 1.6 copy-start
  9.5 28.1 %copy-start.5 = (f32[768]{0:T(1024)S(1)}, f32[768]{0:T(1024)}, u32[]{:S(2)}) copy-start(f32[768]{0:T(1024)} %param.11) | copy-start | bytes 9220
  37.6 8.3 %slice-start = ((s8[5505024]{0:T(1024)(128)(4,1)}), s8[4194304]{0:T(1024)(128)(4,1)S(1)}, s32[]{:S(2)}) async-start(s8[5505024]{0:T(1024)(128)(4,1)} %bitcast.63), calls=%async_computation | async-start | bytes 8388608
  39.3 6.6 %slice-start.1 = ((s8[5505024]{0:T(1024)(128)(4,1)}), s8[1310720]{0:T(1024)(128)(4,1)S(1)}, s32[]{:S(2)}) async-start(s8[5505024]{0:T(1024)(128)(4,1)} %bitcast.63), calls=%async_computation.1 | async-start | bytes 2621440
  120.5 8.6 %copy-start.4 = (bf16[4,4,224,256]{3,2,1,0:T(8,128)(2,1)S(1)}, bf16[4,4,224,256]{3,2,1,0:T(8,128)(2,1)}, u32[]{:S(2)}) copy-start(bf16[4,4,224,256]{3,2,1,0:T(8,128)(2,1)} %get-tuple-element.7) | copy-start | bytes 5505028
  129.0 4.3 %copy-start.1 = (bf16[1,768,3584]{1,2,0:T(8,128)(2,1)S(1)}, bf16[1,768,3584]{1,2,0:T(8,128)(2,1)}, u32[]{:S(2)}) copy-start(bf16[1,768,3584]{1,2,0:T(8,128)(2,1)} %copy.23) | copy-start | bytes 16515076
  129.0 4.8 %copy-start.3 = (bf16[4,4,224,256]{3,2,1,0:T(8,128)(2,1)S(1)}, bf16[4,4,224,256]{3,2,1,0:T(8,128)(2,1)}, u32[]{:S(2)}) copy-start(bf16[4,4,224,256]{3,2,1,0:T(8,128)(2,1)} %get-tuple-element.8) | copy-start | bytes 5505028
  135.4 30.3 %copy-start.2 = (f32[512,768]{1,0:T(8,128)S(1)}, f32[512,768]{1,0:T(8,128)}, u32[]{:S(2)}) copy-start(f32[512,768]{1,0:T(8,128)} %shard_map.82) | copy-start | bytes 4718596
  135.4 30.3 %copy-start.6 = (s32[1024]{0:T(1024)S(1)}, s32[1024]{0:T(1024)}, u32[]{:S(2)}) copy-start(s32[1024]{0:T(1024)} %param.15) | copy-start | bytes 12292
  135.5 30.3 %copy-start.7 = (s32[1024]{0:T(1024)S(1)}, s32[1024]{0:T(1024)}, u32[]{:S(2)}) copy-start(s32[1024]{0:T(1024)} %param.14) | copy-start | bytes 12292
  165.7 8.6 %slice-start.2 = ((s8[5505024]{0:T(1024)(128)(4,1)}), s8[4194304]{0:T(1024)(128)(4,1)S(1)}, s32[]{:S(2)}) async-start(s8[5505024]{0:T(1024)(128)(4,1)} %bitcast.72), calls=%async_computation.2 | async-start | bytes 8388608
  168.8 5.6 %slice-start.3 = ((s8[5505024]{0:T(1024)(128)(4,1)}), s8[1310720]{0:T(1024)(128)(4,1)S(1)}, s32[]{:S(2)}) async-start(s8[5505024]{0:T(1024)(128)(4,1)} %bitcast.72), calls=%async_computation.3 | async-start | bytes 2621440

commit v6 on v5

--- a/solution.py
+++ b/solution.py
@@ -137,13 +137,15 @@
         c.start()
         second.append(c)
     oa[a] = g1a[...]
-    ob[b] = g1b[...]
+    for j in range(RING):
+        ob[j, b] = g1b[j]
     for t in peers_x:
         _copy(g1a, ga.at[t], send_sems.at[2, t], recv_sems.at[2, t], 0).wait_recv()
         oa[t] = ga[t]
     for t in peers_z:
         _copy(g1b, gb.at[t], send_sems.at[3, t], recv_sems.at[3, t], 0).wait_recv()
-        ob[t] = gb[t]
+        for j in range(RING):
+            ob[j, t] = gb[t, j]
     for c in first + second:
         c.wait_send()
 
@@ -244,23 +246,24 @@
     clean_t = jnp.swapaxes(clean_part.reshape(2, half, chunk), 1, 2).astype(jnp.float32)
     recon_error = (recon_sum + bias_part[:, None] - clean_t).astype(jnp.bfloat16)
     error_a, error_b = latent_gather(recon_error, 4)
-    grad_a = jnp.einsum("abdr,fabd->rf", error_a, dec4, preferred_element_type=jnp.float32)
-    grad_b = jnp.einsum("badr,fabd->rf", error_b, dec4, preferred_element_type=jnp.float32)
-    partial_grad = jnp.concatenate([grad_a, grad_b], axis=0)
-    feat_grad = layer_sum(partial_grad.astype(jnp.bfloat16), 2)
+    error_all = jnp.concatenate(
+        [error_a.reshape(d_model, half), error_b.reshape(d_model, half)], axis=1
+    )
+    partial_grad_t = jnp.dot(dec_weight[0], error_all, preferred_element_type=jnp.float32)
+    feat_grad_t = layer_sum(partial_grad_t.astype(jnp.bfloat16), 2)
     row_ids = lax.axis_index("row") * row_count + jnp.arange(row_count, dtype=jnp.int32)
     latent_ids = me * lat_count + jnp.arange(lat_count, dtype=jnp.int32)
     every_row = jnp.arange(all_rows, dtype=jnp.int32)
-    pair_table = (
-        (every_row[None, :] == row_ids[:, None]).astype(jnp.float32)
-        - (pairing[None, :] == row_ids[:, None]).astype(jnp.float32)
+    pair_table_t = (
+        (every_row[:, None] == row_ids[None, :]).astype(jnp.float32)
+        - (pairing[:, None] == row_ids[None, :]).astype(jnp.float32)
     ).astype(jnp.bfloat16)
-    target_hot = (targets[:, None] == latent_ids[None, :]).astype(jnp.bfloat16)
-    margin_table = jnp.dot(pair_table, target_hot, preferred_element_type=jnp.float32)
-    pre_grad = jnp.where(preact > 0, feat_grad - MARGIN * margin_table, 0.0).astype(jnp.bfloat16)
+    target_hot_t = (latent_ids[:, None] == targets[None, :]).astype(jnp.bfloat16)
+    margin_t = jnp.dot(target_hot_t, pair_table_t, preferred_element_type=jnp.float32)
+    pre_grad_t = jnp.where(preact.T > 0, feat_grad_t - MARGIN * margin_t, 0.0).astype(jnp.bfloat16)
     enc4 = enc_weight[0].reshape(RING, RING, chunk, lat_count)
-    input_a = jnp.einsum("rf,abdf->badr", pre_grad[:half], enc4, preferred_element_type=jnp.float32)
-    input_b = jnp.einsum("rf,abdf->abdr", pre_grad[half:], enc4, preferred_element_type=jnp.float32)
+    input_a = jnp.einsum("abdf,fr->badr", enc4, pre_grad_t[:, :half], preferred_element_type=jnp.float32)
+    input_b = jnp.einsum("abdf,fr->abdr", enc4, pre_grad_t[:, half:], preferred_element_type=jnp.float32)
     total = latent_reduce(input_a.astype(jnp.bfloat16), input_b.astype(jnp.bfloat16), 5)
     return jnp.swapaxes(total.astype(jnp.bfloat16), 1, 2).reshape(row_count, 1, chunk)
 

time: 213 us -> 204 us (0.958)
  local copies, waits for them, and re-layouts: 13.3 us -> 6.12 us
  other arithmetic: 6.98 us -> 4.53 us
    unnamed x26 -> x17, local copies, waits for them, and re-layouts: 9.17 us -> 0.18 us
    dot_general x5 -> x4, matrix products: 17.5 us -> 18.8 us  [the longest x1 7.52 us: local(): jnp.dot(dec_weight[0], error_all, preferred_element_type=jnp.float32)]
where the time goes in v6:
time: 204 us; the launch traced here: 203 us
  Pallas kernels  160 us (78%)
  matrix products  32.8 us (16%)
  local copies, waits for them, and re-layouts  6.12 us (3%)
  other arithmetic  4.53 us (2%)
    pallas_call x2, Pallas kernels, latent_reduce(): pl.pallas_call(_reduce_kernel, out_shape=jax.ShapeDtypeStruct((2, h, c),...  70.4 us
    pallas_call x2, Pallas kernels, layer_sum(): pl.pallas_call(_layer_sum_kernel, out_shape=jax.ShapeDtypeStruct((rows, c...  57.3 us
    pallas_call x1, Pallas kernels, latent_gather(): pl.pallas_call(_gather_kernel, out_shape=(full, full), in_specs=[pl.Block...  31.9 us
    dot_general x1, matrix products, local(): jnp.einsum('rld,ldf->rf', inputs, enc_weight, preferred_element_type=jnp....  7.85 us
    dot_general x1, matrix products, local(): jnp.dot(dec_weight[0], error_all, preferred_element_type=jnp.float32)  7.52 us
    unnamed x2, matrix products  6.05 us
    dot_general x1, matrix products, local(): jnp.einsum('abdf,fr->badr', enc4, pre_grad_t[:, :half], preferred_element...  5.51 us

profile of v6, /device:TPU:1, one launch (start us, length us, event | category | flops | bytes accessed | tf_op | source)
XLA Modules:
  0.0 203.2 jit_solution(580600396942206778)
XLA Ops:
  0.0 1.1 constant_dynamic-slice_fusion
  1.2 0.1 copy.43
  1.3 0.3 reshape.39
  1.6 7.8 %fusion.6.x_ref = f32[512,768]{1,0:T(8,128)} fusion(bf16[1,3584,768]{2,1,0:T(8,128)(2,1)} %param.10, bf16[512,1,3584]{2,0,1:T(8,128)(2,1)} %param.8), kind=kOutput, calls=%fused_computation.6 | convolution fusion | flops 2818572288 | bytes 10747904 | tf_op jit(solution)/shard_map/rld,ldf->rf/dot_general | solution.py:237
  9.4 28.0 %shard_map.82 = f32[512,768]{1,0:T(8,128)} custom-call(f32[512,768]{1,0:T(8,128)} %fusion.6.x_ref), custom_call_target="tpu_custom_call" | custom-call | tf_op jit(solution)/shard_map/pallas_call | solution.py:213
  37.5 1.9 copy.27
  39.4 0.2 maximum_convert_fusion
  39.6 4.4 %fusion.2 = f32[256,3584]{0,1:S(1)} fusion(bf16[1,768,3584]{2,1,0:T(8,128)(2,1)} %param.12, bf16[512,768]{0,1:T(8,128)(2,1)S(1)} %maximum_convert_fusion), kind=kOutput, calls=%fused_computation.2 | convolution fusion | flops 1409286144 | bytes 9568256
  44.0 1.5 copy.52
  45.5 1.6 fusion
  47.2 1.5 convert_bitcast_fusion.2.xb
  48.6 37.0 %shard_map.83 = f32[2,224,256]{2,1,0:T(8,128)} custom-call(bf16[4,4,224,256]{3,2,1,0:T(8,128)(2,1)} %bitcast.61, bf16[4,4,224,256]{3,2,1,0:T(8,128)(2,1)} %convert_bitcast_fusion.2.xb), custom_call_target="tpu_custom_call" | custom-call | tf_op jit(solution)/shard_map/pallas_call | solution.py:91
  85.6 0.1 constant_dynamic-slice_fusion.1
  85.7 1.8 fusion.35.e
  87.5 31.9 %shard_map.84 = (bf16[4,4,224,256]{3,2,1,0:T(8,128)(2,1)}, bf16[4,4,224,256]{3,2,1,0:T(8,128)(2,1)}) custom-call(bf16[2,224,256]{2,1,0:T(8,128)(2,1)} %fusion.35.e), custom_call_target="tpu_custom_call" | custom-call | tf_op jit(solution)/shard_map/pallas_call | solution.py:158
  119.4 7.5 %fusion.28.x_ref = bf16[768,512]{1,0:T(8,128)(2,1)} fusion(bf16[3584,256]{1,0:T(8,128)(2,1)} %bitcast.72, bf16[3584,256]{1,0:T(8,128)(2,1)} %bitcast.71, bf16[1,768,3584]{2,1,0:T(8,128)(2,1)} %param.12), kind=kOutput, calls=%fused_computation.28 | convolution fusion | flops 2826305536 | bytes 9961472 | tf_op jit(solution)/shard_map/dot_general | solution.py:252
  126.9 29.2 %shard_map.85 = f32[768,512]{1,0:T(8,128)} custom-call(bf16[768,512]{1,0:T(8,128)(2,1)} %fusion.28.x_ref), custom_call_target="tpu_custom_call" | custom-call | tf_op jit(solution)/shard_map/pallas_call | solution.py:213
  156.2 2.9 %select_convert_fusion = bf16[768,512]{1,0:T(8,128)(2,1)S(1)} fusion(f32[768,512]{1,0:T(8,128)} %shard_map.85, f32[512,768]{0,1:T(8,128)S(1)} %copy.27, s32[1024]{0:T(1024)S(1)} %copy-done.2, s32[768]{0:T(1024)S(1)} %iota_add_fusion, s32[512]{0:T(512)S(1)} %iota_add_fusion.1, s32[1024]{0:T(1024)S(1)} %copy-done.3, f32[768]{0:T(1024)S(1)} %copy-done.1), kind=kOutput, calls=%fused_computation.23 | convolution fusion | flops 811597824 | bytes 3948544 | tf_op jit(solution)/shard_map/dot_general | solution.py:262
  159.2 5.5 %convert_bitcast_fusion.1.xa = bf16[4,4,224,256]{3,2,1,0:T(8,128)(2,1)} fusion(bf16[4,4,224,768]{3,2,1,0:T(8,128)(2,1)} %bitcast.67, bf16[768,512]{1,0:T(8,128)(2,1)S(1)} %select_convert_fusion), kind=kOutput, calls=%fused_computation.21 | convolution fusion | flops 1410203648 | bytes 7733248 | tf_op jit(solution)/shard_map/abdf,fr->badr/dot_general | solution.py:265
  164.7 2.9 %convert_bitcast_fusion.xb = bf16[4,4,224,256]{3,2,1,0:T(8,128)(2,1)} fusion(bf16[4,4,224,768]{3,2,1,0:T(8,128)(2,1)S(1)} %bitcast.70, bf16[768,512]{1,0:T(8,128)(2,1)S(1)} %select_convert_fusion), kind=kOutput, calls=%fused_computation.20 | convolution fusion | flops 1410203648 | bytes 7733248 | tf_op jit(solution)/shard_map/abdf,fr->abdr/dot_general | solution.py:266
  167.6 33.5 %shard_map.86 = f32[2,224,256]{2,1,0:T(8,128)} custom-call(bf16[4,4,224,256]{3,2,1,0:T(8,128)(2,1)} %convert_bitcast_fusion.1.xa, bf16[4,4,224,256]{3,2,1,0:T(8,128)(2,1)} %convert_bitcast_fusion.xb), custom_call_target="tpu_custom_call" | custom-call | tf_op jit(solution)/shard_map/pallas_call | solution.py:91
  201.0 1.0 convert_bitcast_fusion.3
  202.1 0.2 copy.36
  202.3 0.8 reshape.38
  (20 shorter events, 0.1 us)
Async XLA Ops:
  0.0 85.6 %copy-start = (f32[1,3584]{1,0:T(1,128)S(1)}, f32[1,3584]{1,0:T(1,128)}, u32[]{:S(2)}) copy-start(f32[1,3584]{1,0:T(1,128)} %param.13) | copy-start | bytes 43012
  9.4 29.9 %copy-start.1 = (f32[768]{0:T(1024)S(1)}, f32[768]{0:T(1024)}, u32[]{:S(2)}) copy-start(f32[768]{0:T(1024)} %param.11) | copy-start | bytes 9220
  39.4 6.1 %slice-start = ((s8[5505024]{0:T(1024)(128)(4,1)}), s8[4194304]{0:T(1024)(128)(4,1)S(1)}, s32[]{:S(2)}) async-start(s8[5505024]{0:T(1024)(128)(4,1)} %bitcast.65), calls=%async_computation | async-start | bytes 8388608
  39.6 5.9 %slice-start.1 = ((s8[5505024]{0:T(1024)(128)(4,1)}), s8[1310720]{0:T(1024)(128)(4,1)S(1)}, s32[]{:S(2)}) async-start(s8[5505024]{0:T(1024)(128)(4,1)} %bitcast.65), calls=%async_computation.1 | async-start | bytes 2621440
  119.4 36.8 %copy-start.2 = (s32[1024]{0:T(1024)S(1)}, s32[1024]{0:T(1024)}, u32[]{:S(2)}) copy-start(s32[1024]{0:T(1024)} %param.15) | copy-start | bytes 12292
  119.4 36.8 %copy-start.3 = (s32[1024]{0:T(1024)S(1)}, s32[1024]{0:T(1024)}, u32[]{:S(2)}) copy-start(s32[1024]{0:T(1024)} %param.14) | copy-start | bytes 12292
  156.2 8.5 %slice-start.2 = ((s8[5505024]{0:T(1024)(128)(4,1)}), s8[4194304]{0:T(1024)(128)(4,1)S(1)}, s32[]{:S(2)}) async-start(s8[5505024]{0:T(1024)(128)(4,1)} %bitcast.68), calls=%async_computation.2 | async-start | bytes 8388608
  159.2 5.5 %slice-start.3 = ((s8[5505024]{0:T(1024)(128)(4,1)}), s8[1310720]{0:T(1024)(128)(4,1)S(1)}, s32[]{:S(2)}) async-start(s8[5505024]{0:T(1024)(128)(4,1)} %bitcast.68), calls=%async_computation.3 | async-start | bytes 2621440

commit v7 on v6

--- a/solution.py
+++ b/solution.py
@@ -8,6 +8,7 @@
 MARGIN = 16.0
 MESH = pl.DeviceIdType.MESH
 RING = 4
+LAYERS = 4
 
 
 def _latent_coords():
@@ -172,58 +173,115 @@
     )(e)
 
 
-def _layer_sum_kernel(x_ref, o_ref, recv_a, recv_b, recv_c, send_sems, recv_sems):
+def _layer_peers():
     me = lax.axis_index("layer")
-    core = me % 2
-    chip = me // 2
-    mate = me + 1 - 2 * core
-    far = me + 2 - 4 * chip
-    half = x_ref.shape[0] // 2
-    mine = pl.ds(pl.multiple_of(core * half, half), half)
-    other = pl.ds(pl.multiple_of((1 - core) * half, half), half)
-
+    return me, [(me + k) % LAYERS for k in range(1, LAYERS)]
+
+
+def _layer_greet(peers):
     barrier = pltpu.get_barrier_semaphore()
-    for peer in (mate, far):
-        pl.semaphore_signal(barrier, inc=1, device_id={"layer": peer}, device_id_type=MESH)
-    pl.semaphore_wait(barrier, 2)
-
-    def send(src, dst, slot, peer):
-        return pltpu.make_async_remote_copy(
-            src_ref=src, dst_ref=dst, send_sem=send_sems.at[slot], recv_sem=recv_sems.at[slot],
-            device_id={"layer": peer}, device_id_type=MESH,
-        )
-
-    step_a = send(x_ref.at[other], recv_a, 0, mate)
-    step_a.start()
-    step_a.wait()
-    o_ref[mine] = x_ref[mine].astype(jnp.float32) + recv_a[...].astype(jnp.float32)
-    step_b = send(o_ref.at[mine], recv_b, 1, far)
-    step_b.start()
-    step_b.wait()
-    o_ref[mine] = o_ref[mine] + recv_b[...]
-    step_c = send(o_ref.at[mine], recv_c, 2, mate)
-    step_c.start()
-    step_c.wait()
-    o_ref[other] = recv_c[...]
-
-
-def layer_sum(x, collective_id):
+    for p in peers:
+        pl.semaphore_signal(barrier, inc=1, device_id={"layer": p}, device_id_type=MESH)
+    pl.semaphore_wait(barrier, LAYERS - 1)
+
+
+def _layer_copy(src, dst, send_sems, recv_sems, k, p, slot):
+    return pltpu.make_async_remote_copy(
+        src_ref=src, dst_ref=dst, send_sem=send_sems.at[k, p], recv_sem=recv_sems.at[k, slot],
+        device_id={"layer": p}, device_id_type=MESH,
+    )
+
+
+def _layer_pre_kernel(x, bias, feats, pre_q, r1, r2, send_sems, recv_sems):
+    me, peers = _layer_peers()
+    q = x.shape[0] // LAYERS
+    rows = lambda i: pl.ds(pl.multiple_of(i * q, q), q)
+    _layer_greet(peers)
+    sent = []
+    for p in peers:
+        c = _layer_copy(x.at[rows(p)], r1.at[me], send_sems, recv_sems, 0, p, me)
+        c.start()
+        sent.append(c)
+    total = x[rows(me)]
+    for p in peers:
+        _layer_copy(x.at[rows(p)], r1.at[p], send_sems, recv_sems, 0, p, p).wait_recv()
+        total = total + r1[p]
+    total = total + bias[...]
+    pre_q[...] = total
+    feats[rows(me)] = jnp.maximum(total, 0.0).astype(feats.dtype)
+    for p in peers:
+        c = _layer_copy(feats.at[rows(me)], r2.at[me], send_sems, recv_sems, 1, p, me)
+        c.start()
+        sent.append(c)
+    for p in peers:
+        _layer_copy(feats.at[rows(p)], r2.at[p], send_sems, recv_sems, 1, p, p).wait_recv()
+        feats[rows(p)] = r2[p]
+    for c in sent:
+        c.wait_send()
+
+
+def layer_pre(x, bias):
     rows, cols = x.shape
-    half = rows // 2
+    q = rows // LAYERS
     return pl.pallas_call(
-        _layer_sum_kernel,
-        out_shape=jax.ShapeDtypeStruct((rows, cols), jnp.float32),
-        in_specs=[pl.BlockSpec(memory_space=pltpu.VMEM)],
+        _layer_pre_kernel,
+        out_shape=(jax.ShapeDtypeStruct((rows, cols), jnp.bfloat16),
+                   jax.ShapeDtypeStruct((q, cols), jnp.float32)),
+        in_specs=[pl.BlockSpec(memory_space=pltpu.VMEM)] * 2,
+        out_specs=(pl.BlockSpec(memory_space=pltpu.VMEM), pl.BlockSpec(memory_space=pltpu.VMEM)),
+        scratch_shapes=[
+            pltpu.VMEM((LAYERS, q, cols), jnp.float32),
+            pltpu.VMEM((LAYERS, q, cols), jnp.bfloat16),
+            pltpu.SemaphoreType.DMA((2, LAYERS)),
+            pltpu.SemaphoreType.DMA((2, LAYERS)),
+        ],
+        compiler_params=pltpu.CompilerParams(collective_id=1, has_side_effects=True),
+    )(x, bias)
+
+
+def _layer_grad_kernel(g, pre_q, margin_q, out, r1, r2, send_sems, recv_sems):
+    me, peers = _layer_peers()
+    q = g.shape[1] // LAYERS
+    lanes = lambda i: pl.ds(pl.multiple_of(i * q, q), q)
+    _layer_greet(peers)
+    sent = []
+    for p in peers:
+        c = _layer_copy(g.at[:, lanes(p)], r1.at[me], send_sems, recv_sems, 0, p, me)
+        c.start()
+        sent.append(c)
+    total = g[:, lanes(me)].astype(jnp.float32)
+    for p in peers:
+        _layer_copy(g.at[:, lanes(p)], r1.at[p], send_sems, recv_sems, 0, p, p).wait_recv()
+        total = total + r1[p].astype(jnp.float32)
+    grad = jnp.where(pre_q[...] > 0, total - MARGIN * margin_q[...], 0.0)
+    out[:, lanes(me)] = grad.astype(out.dtype)
+    for p in peers:
+        c = _layer_copy(out.at[:, lanes(me)], r2.at[me], send_sems, recv_sems, 1, p, me)
+        c.start()
+        sent.append(c)
+    for p in peers:
+        _layer_copy(out.at[:, lanes(p)], r2.at[p], send_sems, recv_sems, 1, p, p).wait_recv()
+        out[:, lanes(p)] = r2[p]
+    for c in sent:
+        c.wait_send()
+
+
+def layer_grad(g, pre_q, margin_q):
+    cols, rows = g.shape
+    q = rows // LAYERS
+    return pl.pallas_call(
+        _layer_grad_kernel,
+        out_shape=jax.ShapeDtypeStruct((cols, rows), jnp.bfloat16),
+        in_specs=[pl.BlockSpec(memory_space=pltpu.VMEM)] * 3,
         out_specs=pl.BlockSpec(memory_space=pltpu.VMEM),
         scratch_shapes=[
-            pltpu.VMEM((half, cols), x.dtype),
-            pltpu.VMEM((half, cols), jnp.float32),
-            pltpu.VMEM((half, cols), jnp.float32),
-            pltpu.SemaphoreType.DMA((3,)),
-            pltpu.SemaphoreType.DMA((3,)),
+            pltpu.VMEM((LAYERS, cols, q), jnp.bfloat16),
+            pltpu.VMEM((LAYERS, cols, q), jnp.bfloat16),
+            pltpu.SemaphoreType.DMA((2, LAYERS)),
+            pltpu.SemaphoreType.DMA((2, LAYERS)),
         ],
-        compiler_params=pltpu.CompilerParams(collective_id=collective_id, has_side_effects=True),
-    )(x)
+        compiler_params=pltpu.CompilerParams(collective_id=2, has_side_effects=True),
+    )(g, pre_q, margin_q)
 
 
 def local(inputs, clean_acts, enc_weight, enc_bias, dec_weight, dec_bias, pairing, targets):
@@ -235,8 +293,7 @@
     half = row_count // 2
     me = lax.axis_index("latent")
     partial_pre = jnp.einsum("rld,ldf->rf", inputs, enc_weight, preferred_element_type=jnp.float32)
-    preact = layer_sum(partial_pre, 1) + enc_bias
-    features = jnp.maximum(preact, 0.0).astype(jnp.bfloat16)
+    features, pre_q = layer_pre(partial_pre, enc_bias[None, :])
     dec4 = dec_weight[0].reshape(lat_count, RING, RING, chunk)
     recon_a = jnp.einsum("rf,fabd->badr", features[:half], dec4, preferred_element_type=jnp.float32)
     recon_b = jnp.einsum("rf,fabd->abdr", features[half:], dec4, preferred_element_type=jnp.float32)
@@ -250,8 +307,12 @@
         [error_a.reshape(d_model, half), error_b.reshape(d_model, half)], axis=1
     )
     partial_grad_t = jnp.dot(dec_weight[0], error_all, preferred_element_type=jnp.float32)
-    feat_grad_t = layer_sum(partial_grad_t.astype(jnp.bfloat16), 2)
-    row_ids = lax.axis_index("row") * row_count + jnp.arange(row_count, dtype=jnp.int32)
+    quarter = row_count // LAYERS
+    row_ids = (
+        lax.axis_index("row") * row_count
+        + lax.axis_index("layer") * quarter
+        + jnp.arange(quarter, dtype=jnp.int32)
+    )
     latent_ids = me * lat_count + jnp.arange(lat_count, dtype=jnp.int32)
     every_row = jnp.arange(all_rows, dtype=jnp.int32)
     pair_table_t = (
@@ -259,8 +320,8 @@
         - (pairing[:, None] == row_ids[None, :]).astype(jnp.float32)
     ).astype(jnp.bfloat16)
     target_hot_t = (latent_ids[:, None] == targets[None, :]).astype(jnp.bfloat16)
-    margin_t = jnp.dot(target_hot_t, pair_table_t, preferred_element_type=jnp.float32)
-    pre_grad_t = jnp.where(preact.T > 0, feat_grad_t - MARGIN * margin_t, 0.0).astype(jnp.bfloat16)
+    margin_q = jnp.dot(target_hot_t, pair_table_t, preferred_element_type=jnp.float32)
+    pre_grad_t = layer_grad(partial_grad_t.astype(jnp.bfloat16), pre_q.T, margin_q)
     enc4 = enc_weight[0].reshape(RING, RING, chunk, lat_count)
     input_a = jnp.einsum("abdf,fr->badr", enc4, pre_grad_t[:, :half], preferred_element_type=jnp.float32)
     input_b = jnp.einsum("abdf,fr->abdr", enc4, pre_grad_t[:, half:], preferred_element_type=jnp.float32)

time: 204 us -> 203 us (level)
  no operation moved by 1% of the time
where the time goes in v7:
time: 203 us; the launch traced here: 202 us
  Pallas kernels  159 us (78%)
  matrix products  33.2 us (16%)
  local copies, waits for them, and re-layouts  5.77 us (3%)
  other arithmetic  4.34 us (2%)
    pallas_call x2, Pallas kernels, latent_reduce(): pl.pallas_call(_reduce_kernel, out_shape=jax.ShapeDtypeStruct((2, h, c),...  70.5 us
    pallas_call x1, Pallas kernels, latent_gather(): pl.pallas_call(_gather_kernel, out_shape=(full, full), in_specs=[pl.Block...  32.6 us
    pallas_call x1, Pallas kernels, layer_pre(): pl.pallas_call(_layer_pre_kernel, out_shape=(jax.ShapeDtypeStruct((rows,...  31.7 us
    pallas_call x1, Pallas kernels, layer_grad(): pl.pallas_call(_layer_grad_kernel, out_shape=jax.ShapeDtypeStruct((cols,...  24.1 us
    dot_general x1, matrix products, local(): jnp.einsum('rld,ldf->rf', inputs, enc_weight, preferred_element_type=jnp....  7.86 us
    unnamed x2, matrix products  7.58 us
    dot_general x1, matrix products, local(): jnp.dot(dec_weight[0], error_all, preferred_element_type=jnp.float32)  7.57 us
    dot_general x1, matrix products, local(): jnp.einsum('abdf,fr->badr', enc4, pre_grad_t[:, :half], preferred_element...  5.69 us

profile of v7, /device:TPU:1, one launch (start us, length us, event | category | flops | bytes accessed | tf_op | source)
XLA Modules:
  0.0 202.5 jit_solution(7717992021087763656)
XLA Ops:
  0.0 1.1 constant_dynamic-slice_fusion
  1.2 0.1 copy.35
  1.3 0.3 reshape.38
  1.6 7.9 %fusion.6.x = f32[512,768]{1,0:T(8,128)} fusion(bf16[1,3584,768]{2,1,0:T(8,128)(2,1)} %param.10, bf16[512,1,3584]{2,0,1:T(8,128)(2,1)} %param.8), kind=kOutput, calls=%fused_computation.6 | convolution fusion | flops 2818572288 | bytes 10747904 | tf_op jit(solution)/shard_map/rld,ldf->rf/dot_general | solution.py:295
  9.5 0.6 broadcast_in_dim.2.bias
  10.0 31.7 %shard_map.82 = (bf16[512,768]{1,0:T(8,128)(2,1)}, f32[128,768]{1,0:T(8,128)}) custom-call(f32[512,768]{1,0:T(8,128)} %fusion.6.x, f32[1,768]{1,0:T(1,128)} %broadcast_in_dim.2.bias), custom_call_target="tpu_custom_call" | custom-call | tf_op jit(solution)/shard_map/pallas_call | solution.py:226
  41.8 5.2 %fusion.2 = f32[256,3584]{0,1:S(1)} fusion(bf16[1,768,3584]{2,1,0:T(8,128)(2,1)} %param.12, bf16[512,768]{1,0:T(8,128)(2,1)} %get-tuple-element.9), kind=kOutput, calls=%fused_computation.2 | convolution fusion | flops 1409286144 | bytes 9568256
  47.0 1.5 copy.44
  48.5 2.4 %fusion = f32[256,3584]{0,1:S(1)} fusion(bf16[1,768,3584]{2,1,0:T(8,128)(2,1)S(1)} %bitcast.61, bf16[512,768]{1,0:T(8,128)(2,1)S(1)} %copy-done.1), kind=kOutput, calls=%fused_computation | convolution fusion | flops 1409286144 | bytes 9568256
  50.9 1.5 convert_bitcast_fusion.2.xb
  52.4 37.2 %shard_map.83 = f32[2,224,256]{2,1,0:T(8,128)} custom-call(bf16[4,4,224,256]{3,2,1,0:T(8,128)(2,1)} %bitcast.64, bf16[4,4,224,256]{3,2,1,0:T(8,128)(2,1)} %convert_bitcast_fusion.2.xb), custom_call_target="tpu_custom_call" | custom-call | tf_op jit(solution)/shard_map/pallas_call | solution.py:92
  89.6 0.1 constant_dynamic-slice_fusion.1
  89.7 1.8 fusion.31.e
  91.5 32.6 %shard_map.84 = (bf16[4,4,224,256]{3,2,1,0:T(8,128)(2,1)}, bf16[4,4,224,256]{3,2,1,0:T(8,128)(2,1)}) custom-call(bf16[2,224,256]{2,1,0:T(8,128)(2,1)} %fusion.31.e), custom_call_target="tpu_custom_call" | custom-call | tf_op jit(solution)/shard_map/pallas_call | solution.py:159
  124.2 7.6 %fusion.26.g = bf16[768,512]{1,0:T(8,128)(2,1)} fusion(bf16[3584,256]{1,0:T(8,128)(2,1)} %bitcast.72, bf16[3584,256]{1,0:T(8,128)(2,1)} %bitcast.71, bf16[1,768,3584]{2,1,0:T(8,128)(2,1)} %param.12), kind=kOutput, calls=%fused_computation.24 | convolution fusion | flops 2826305536 | bytes 9961472 | tf_op jit(solution)/shard_map/dot_general | solution.py:309
  131.8 0.9 copy.28
  132.7 1.7 fusion.14.margin_q
  134.4 24.1 %shard_map.85 = bf16[768,512]{1,0:T(8,128)(2,1)} custom-call(bf16[768,512]{1,0:T(8,128)(2,1)} %fusion.26.g, f32[768,128]{1,0:T(8,128)} %bitcast.65, f32[768,128]{1,0:T(8,128)} %fusion.14.margin_q), custom_call_target="tpu_custom_call" | custom-call | tf_op jit(solution)/shard_map/pallas_call | solution.py:272
  158.5 5.7 %convert_bitcast_fusion.1.xa = bf16[4,4,224,256]{3,2,1,0:T(8,128)(2,1)} fusion(bf16[4,4,224,768]{3,2,1,0:T(8,128)(2,1)} %bitcast.67, bf16[768,512]{1,0:T(8,128)(2,1)} %shard_map.85), kind=kOutput, calls=%fused_computation.19 | convolution fusion | flops 1410203648 | bytes 7733248 | tf_op jit(solution)/shard_map/abdf,fr->badr/dot_general | solution.py:326
  164.3 2.8 %convert_bitcast_fusion.xb = bf16[4,4,224,256]{3,2,1,0:T(8,128)(2,1)} fusion(bf16[4,4,224,768]{3,2,1,0:T(8,128)(2,1)S(1)} %bitcast.70, bf16[768,512]{1,0:T(8,128)(2,1)S(1)} %copy-done.2), kind=kOutput, calls=%fused_computation.18 | convolution fusion | flops 1410203648 | bytes 7733248 | tf_op jit(solution)/shard_map/abdf,fr->abdr/dot_general | solution.py:327
  167.1 33.3 %shard_map.86 = f32[2,224,256]{2,1,0:T(8,128)} custom-call(bf16[4,4,224,256]{3,2,1,0:T(8,128)(2,1)} %convert_bitcast_fusion.1.xa, bf16[4,4,224,256]{3,2,1,0:T(8,128)(2,1)} %convert_bitcast_fusion.xb), custom_call_target="tpu_custom_call" | custom-call | tf_op jit(solution)/shard_map/pallas_call | solution.py:92
  200.4 1.0 convert_bitcast_fusion.3
  201.4 0.2 copy.30
  201.7 0.8 reshape.37
  (26 shorter events, 0.1 us)
Async XLA Ops:
  0.0 89.6 %copy-start = (f32[1,3584]{1,0:T(1,128)S(1)}, f32[1,3584]{1,0:T(1,128)}, u32[]{:S(2)}) copy-start(f32[1,3584]{1,0:T(1,128)} %param.13) | copy-start | bytes 43012
  1.6 7.9 %copy-start.4 = (f32[768]{0:T(1024)S(1)}, f32[768]{0:T(1024)}, u32[]{:S(2)}) copy-start(f32[768]{0:T(1024)} %param.11) | copy-start | bytes 9220
  10.0 38.5 %slice-start = ((s8[5505024]{0:T(1024)(128)(4,1)}), s8[1310720]{0:T(1024)(128)(4,1)S(1)}, s32[]{:S(2)}) async-start(s8[5505024]{0:T(1024)(128)(4,1)} %bitcast.60), calls=%async_computation | async-start | bytes 2621440
  41.8 6.7 %slice-start.1 = ((s8[5505024]{0:T(1024)(128)(4,1)}), s8[4194304]{0:T(1024)(128)(4,1)S(1)}, s32[]{:S(2)}) async-start(s8[5505024]{0:T(1024)(128)(4,1)} %bitcast.60), calls=%async_computation.1 | async-start | bytes 8388608
  47.0 1.5 copy-start.1
  124.2 7.6 %copy-start.3 = (f32[128,768]{1,0:T(8,128)S(1)}, f32[128,768]{1,0:T(8,128)}, u32[]{:S(2)}) copy-start(f32[128,768]{1,0:T(8,128)} %get-tuple-element.12) | copy-start | bytes 1179652
  124.2 8.5 %copy-start.5 = (s32[1024]{0:T(1024)S(1)}, s32[1024]{0:T(1024)}, u32[]{:S(2)}) copy-start(s32[1024]{0:T(1024)} %param.15) | copy-start | bytes 12292
  124.2 8.5 %copy-start.6 = (s32[1024]{0:T(1024)S(1)}, s32[1024]{0:T(1024)}, u32[]{:S(2)}) copy-start(s32[1024]{0:T(1024)} %param.14) | copy-start | bytes 12292
  134.4 29.9 %slice-start.2 = ((s8[5505024]{0:T(1024)(128)(4,1)}), s8[1310720]{0:T(1024)(128)(4,1)S(1)}, s32[]{:S(2)}) async-start(s8[5505024]{0:T(1024)(128)(4,1)} %bitcast.68), calls=%async_computation.2 | async-start | bytes 2621440
  158.5 5.7 %copy-start.2 = (bf16[768,512]{1,0:T(8,128)(2,1)S(1)}, bf16[768,512]{1,0:T(8,128)(2,1)}, u32[]{:S(2)}) copy-start(bf16[768,512]{1,0:T(8,128)(2,1)} %shard_map.85) | copy-start | bytes 2359300
  158.5 5.7 %slice-start.3 = ((s8[5505024]{0:T(1024)(128)(4,1)}), s8[4194304]{0:T(1024)(128)(4,1)S(1)}, s32[]{:S(2)}) async-start(s8[5505024]{0:T(1024)(128)(4,1)} %bitcast.68), calls=%async_computation.3 | async-start | bytes 8388608

commit v8 on v6

--- a/solution.py
+++ b/solution.py
@@ -8,6 +8,7 @@
 MARGIN = 16.0
 MESH = pl.DeviceIdType.MESH
 RING = 4
+LAYERS = 4
 
 
 def _latent_coords():
@@ -172,58 +173,116 @@
     )(e)
 
 
-def _layer_sum_kernel(x_ref, o_ref, recv_a, recv_b, recv_c, send_sems, recv_sems):
+def _layer_roles():
     me = lax.axis_index("layer")
-    core = me % 2
-    chip = me // 2
-    mate = me + 1 - 2 * core
-    far = me + 2 - 4 * chip
-    half = x_ref.shape[0] // 2
-    mine = pl.ds(pl.multiple_of(core * half, half), half)
-    other = pl.ds(pl.multiple_of((1 - core) * half, half), half)
-
+    mate = me + 1 - 2 * (me % 2)
+    far = (me + 2) % LAYERS
+    return me, mate, far, (mate + 2) % LAYERS
+
+
+def _layer_exchange(quarter, x, out, finish, ra, sb, rb, rc, rd, send_sems, recv_sems):
+    me, mate, far, mate_far = _layer_roles()
     barrier = pltpu.get_barrier_semaphore()
-    for peer in (mate, far):
-        pl.semaphore_signal(barrier, inc=1, device_id={"layer": peer}, device_id_type=MESH)
+    for p in (mate, far):
+        pl.semaphore_signal(barrier, inc=1, device_id={"layer": p}, device_id_type=MESH)
     pl.semaphore_wait(barrier, 2)
 
-    def send(src, dst, slot, peer):
+    def copy(src, dst, k, p):
         return pltpu.make_async_remote_copy(
-            src_ref=src, dst_ref=dst, send_sem=send_sems.at[slot], recv_sem=recv_sems.at[slot],
-            device_id={"layer": peer}, device_id_type=MESH,
+            src_ref=src, dst_ref=dst, send_sem=send_sems.at[k], recv_sem=recv_sems.at[k],
+            device_id={"layer": p}, device_id_type=MESH,
         )
 
-    step_a = send(x_ref.at[other], recv_a, 0, mate)
-    step_a.start()
-    step_a.wait()
-    o_ref[mine] = x_ref[mine].astype(jnp.float32) + recv_a[...].astype(jnp.float32)
-    step_b = send(o_ref.at[mine], recv_b, 1, far)
+    sent = [copy(quarter(x, mate), ra.at[0], 0, mate), copy(quarter(x, mate_far), ra.at[1], 1, mate)]
+    for c in sent:
+        c.start()
+    sent[0].wait_recv()
+    sent[1].wait_recv()
+    sb[...] = quarter(x, far)[...].astype(jnp.float32) + ra[1].astype(jnp.float32)
+    step_b = copy(sb, rb, 2, far)
     step_b.start()
-    step_b.wait()
-    o_ref[mine] = o_ref[mine] + recv_b[...]
-    step_c = send(o_ref.at[mine], recv_c, 2, mate)
+    own = quarter(x, me)[...].astype(jnp.float32) + ra[0].astype(jnp.float32)
+    step_b.wait_recv()
+    quarter(out, me)[...] = finish(own + rb[...])
+    step_c = copy(quarter(out, me), rc, 3, far)
     step_c.start()
-    step_c.wait()
-    o_ref[other] = recv_c[...]
-
-
-def layer_sum(x, collective_id):
+    step_c.wait_recv()
+    quarter(out, far)[...] = rc[...]
+    step_d = [copy(quarter(out, me), rd.at[0], 4, mate), copy(rc, rd.at[1], 5, mate)]
+    for c in step_d:
+        c.start()
+    for c in step_d:
+        c.wait_recv()
+    quarter(out, mate)[...] = rd[0]
+    quarter(out, mate_far)[...] = rd[1]
+    for c in sent + [step_b, step_c] + step_d:
+        c.wait_send()
+
+
+def _row_quarter(ref, i):
+    q = ref.shape[0] // LAYERS
+    return ref.at[pl.ds(pl.multiple_of(i * q, q), q)]
+
+
+def _lane_quarter(ref, i):
+    q = ref.shape[1] // LAYERS
+    return ref.at[:, pl.ds(pl.multiple_of(i * q, q), q)]
+
+
+def _layer_pre_kernel(x, bias, feats, pre_q, *scratch):
+    def finish(total):
+        pre = total + bias[...]
+        pre_q[...] = pre
+        return jnp.maximum(pre, 0.0).astype(feats.dtype)
+
+    _layer_exchange(_row_quarter, x, feats, finish, *scratch)
+
+
+def _layer_scratch(in_q, out_q, in_dtype):
+    return [
+        pltpu.VMEM((2,) + in_q, in_dtype),
+        pltpu.VMEM(in_q, jnp.float32),
+        pltpu.VMEM(in_q, jnp.float32),
+        pltpu.VMEM(out_q, jnp.bfloat16),
+        pltpu.VMEM((2,) + out_q, jnp.bfloat16),
+        pltpu.SemaphoreType.DMA((6,)),
+        pltpu.SemaphoreType.DMA((6,)),
+    ]
+
+
+def layer_pre(x, bias):
     rows, cols = x.shape
-    half = rows // 2
+    q = rows // LAYERS
     return pl.pallas_call(
-        _layer_sum_kernel,
-        out_shape=jax.ShapeDtypeStruct((rows, cols), jnp.float32),
-        in_specs=[pl.BlockSpec(memory_space=pltpu.VMEM)],
+        _layer_pre_kernel,
+        out_shape=(jax.ShapeDtypeStruct((rows, cols), jnp.bfloat16),
+                   jax.ShapeDtypeStruct((q, cols), jnp.float32)),
+        in_specs=[pl.BlockSpec(memory_space=pltpu.VMEM)] * 2,
+        out_specs=(pl.BlockSpec(memory_space=pltpu.VMEM), pl.BlockSpec(memory_space=pltpu.VMEM)),
+        scratch_shapes=_layer_scratch((q, cols), (q, cols), x.dtype),
+        compiler_params=pltpu.CompilerParams(collective_id=1, has_side_effects=True),
+    )(x, bias)
+
+
+def _layer_grad_kernel(g, pre_q, margin_q, out, *scratch):
+    def finish(total):
+        grad = jnp.where(pre_q[...] > 0, total - MARGIN * margin_q[...], 0.0)
+        return grad.astype(out.dtype)
+
+    _layer_exchange(_lane_quarter, g, out, finish, *scratch)
+
+
+def layer_grad(g, pre_q, margin_q):
+    cols, rows = g.shape
+    q = rows // LAYERS
+    return pl.pallas_call(
+        _layer_grad_kernel,
+        out_shape=jax.ShapeDtypeStruct((cols, rows), jnp.bfloat16),
+        in_specs=[pl.BlockSpec(memory_space=pltpu.VMEM)] * 3,
         out_specs=pl.BlockSpec(memory_space=pltpu.VMEM),
-        scratch_shapes=[
-            pltpu.VMEM((half, cols), x.dtype),
-            pltpu.VMEM((half, cols), jnp.float32),
-            pltpu.VMEM((half, cols), jnp.float32),
-            pltpu.SemaphoreType.DMA((3,)),
-            pltpu.SemaphoreType.DMA((3,)),
-        ],
-        compiler_params=pltpu.CompilerParams(collective_id=collective_id, has_side_effects=True),
-    )(x)
+        scratch_shapes=_layer_scratch((cols, q), (cols, q), g.dtype),
+        compiler_params=pltpu.CompilerParams(collective_id=2, has_side_effects=True),
+    )(g, pre_q, margin_q)
 
 
 def local(inputs, clean_acts, enc_weight, enc_bias, dec_weight, dec_bias, pairing, targets):
@@ -235,8 +294,7 @@
     half = row_count // 2
     me = lax.axis_index("latent")
     partial_pre = jnp.einsum("rld,ldf->rf", inputs, enc_weight, preferred_element_type=jnp.float32)
-    preact = layer_sum(partial_pre, 1) + enc_bias
-    features = jnp.maximum(preact, 0.0).astype(jnp.bfloat16)
+    features, pre_q = layer_pre(partial_pre, enc_bias[None, :])
     dec4 = dec_weight[0].reshape(lat_count, RING, RING, chunk)
     recon_a = jnp.einsum("rf,fabd->badr", features[:half], dec4, preferred_element_type=jnp.float32)
     recon_b = jnp.einsum("rf,fabd->abdr", features[half:], dec4, preferred_element_type=jnp.float32)
@@ -250,8 +308,12 @@
         [error_a.reshape(d_model, half), error_b.reshape(d_model, half)], axis=1
     )
     partial_grad_t = jnp.dot(dec_weight[0], error_all, preferred_element_type=jnp.float32)
-    feat_grad_t = layer_sum(partial_grad_t.astype(jnp.bfloat16), 2)
-    row_ids = lax.axis_index("row") * row_count + jnp.arange(row_count, dtype=jnp.int32)
+    quarter = row_count // LAYERS
+    row_ids = (
+        lax.axis_index("row") * row_count
+        + lax.axis_index("layer") * quarter
+        + jnp.arange(quarter, dtype=jnp.int32)
+    )
     latent_ids = me * lat_count + jnp.arange(lat_count, dtype=jnp.int32)
     every_row = jnp.arange(all_rows, dtype=jnp.int32)
     pair_table_t = (
@@ -259,8 +321,8 @@
         - (pairing[:, None] == row_ids[None, :]).astype(jnp.float32)
     ).astype(jnp.bfloat16)
     target_hot_t = (latent_ids[:, None] == targets[None, :]).astype(jnp.bfloat16)
-    margin_t = jnp.dot(target_hot_t, pair_table_t, preferred_element_type=jnp.float32)
-    pre_grad_t = jnp.where(preact.T > 0, feat_grad_t - MARGIN * margin_t, 0.0).astype(jnp.bfloat16)
+    margin_q = jnp.dot(target_hot_t, pair_table_t, preferred_element_type=jnp.float32)
+    pre_grad_t = layer_grad(partial_grad_t.astype(jnp.bfloat16), pre_q.T, margin_q)
     enc4 = enc_weight[0].reshape(RING, RING, chunk, lat_count)
     input_a = jnp.einsum("abdf,fr->badr", enc4, pre_grad_t[:, :half], preferred_element_type=jnp.float32)
     input_b = jnp.einsum("abdf,fr->abdr", enc4, pre_grad_t[:, half:], preferred_element_type=jnp.float32)

time: 204 us -> 198 us (0.971)
  Pallas kernels: 160 us -> 154 us
    pallas_call x2, Pallas kernels: 57.3 us -> 51.4 us  [the longest x1 26.1 us: layer_grad(): pl.pallas_call(_layer_grad_kernel, out_shape=jax.ShapeDtypeStruct((cols,...]
where the time goes in v8:
time: 198 us
  Pallas kernels  154 us (78%)
  matrix products  33.2 us (17%)
  local copies, waits for them, and re-layouts  5.77 us (3%)
  other arithmetic  4.34 us (2%)
    pallas_call x2, Pallas kernels, latent_reduce(): pl.pallas_call(_reduce_kernel, out_shape=jax.ShapeDtypeStruct((2, h, c),...  70.8 us
    pallas_call x1, Pallas kernels, latent_gather(): pl.pallas_call(_gather_kernel, out_shape=(full, full), in_specs=[pl.Block...  31.9 us
    pallas_call x1, Pallas kernels, layer_grad(): pl.pallas_call(_layer_grad_kernel, out_shape=jax.ShapeDtypeStruct((cols,...  26.1 us
    pallas_call x1, Pallas kernels, layer_pre(): pl.pallas_call(_layer_pre_kernel, out_shape=(jax.ShapeDtypeStruct((rows,...  25.3 us
    dot_general x1, matrix products, local(): jnp.einsum('rld,ldf->rf', inputs, enc_weight, preferred_element_type=jnp....  7.86 us
    unnamed x2, matrix products  7.58 us
    dot_general x1, matrix products, local(): jnp.dot(dec_weight[0], error_all, preferred_element_type=jnp.float32)  7.57 us
    dot_general x1, matrix products, local(): jnp.einsum('abdf,fr->badr', enc4, pre_grad_t[:, :half], preferred_element...  5.7 us

profile of v8, /device:TPU:1, one launch (start us, length us, event | category | flops | bytes accessed | tf_op | source)
XLA Modules:
  0.0 197.7 jit_solution(16176090852757889659)
XLA Ops:
  0.0 1.1 constant_dynamic-slice_fusion
  1.2 0.1 copy.35
  1.3 0.3 reshape.38
  1.6 7.9 %fusion.6.x = f32[512,768]{1,0:T(8,128)} fusion(bf16[1,3584,768]{2,1,0:T(8,128)(2,1)} %param.10, bf16[512,1,3584]{2,0,1:T(8,128)(2,1)} %param.8), kind=kOutput, calls=%fused_computation.6 | convolution fusion | flops 2818572288 | bytes 10747904 | tf_op jit(solution)/shard_map/rld,ldf->rf/dot_general | solution.py:296
  9.5 0.6 broadcast_in_dim.2.bias
  10.0 25.3 %shard_map.82 = (bf16[512,768]{1,0:T(8,128)(2,1)}, f32[128,768]{1,0:T(8,128)}) custom-call(f32[512,768]{1,0:T(8,128)} %fusion.6.x, f32[1,768]{1,0:T(1,128)} %broadcast_in_dim.2.bias), custom_call_target="tpu_custom_call" | custom-call | tf_op jit(solution)/shard_map/pallas_call | solution.py:256
  35.4 5.2 %fusion.2 = f32[256,3584]{0,1:S(1)} fusion(bf16[1,768,3584]{2,1,0:T(8,128)(2,1)} %param.12, bf16[512,768]{1,0:T(8,128)(2,1)} %get-tuple-element.9), kind=kOutput, calls=%fused_computation.2 | convolution fusion | flops 1409286144 | bytes 9568256
  40.6 1.5 copy.44
  42.1 2.4 %fusion = f32[256,3584]{0,1:S(1)} fusion(bf16[1,768,3584]{2,1,0:T(8,128)(2,1)S(1)} %bitcast.61, bf16[512,768]{1,0:T(8,128)(2,1)S(1)} %copy-done.1), kind=kOutput, calls=%fused_computation | convolution fusion | flops 1409286144 | bytes 9568256
  44.5 1.5 convert_bitcast_fusion.2.xb
  46.0 37.1 %shard_map.83 = f32[2,224,256]{2,1,0:T(8,128)} custom-call(bf16[4,4,224,256]{3,2,1,0:T(8,128)(2,1)} %bitcast.64, bf16[4,4,224,256]{3,2,1,0:T(8,128)(2,1)} %convert_bitcast_fusion.2.xb), custom_call_target="tpu_custom_call" | custom-call | tf_op jit(solution)/shard_map/pallas_call | solution.py:92
  83.0 0.1 constant_dynamic-slice_fusion.1
  83.1 1.8 fusion.31.e
  84.9 31.9 %shard_map.84 = (bf16[4,4,224,256]{3,2,1,0:T(8,128)(2,1)}, bf16[4,4,224,256]{3,2,1,0:T(8,128)(2,1)}) custom-call(bf16[2,224,256]{2,1,0:T(8,128)(2,1)} %fusion.31.e), custom_call_target="tpu_custom_call" | custom-call | tf_op jit(solution)/shard_map/pallas_call | solution.py:159
  116.9 7.6 %fusion.26.g = bf16[768,512]{1,0:T(8,128)(2,1)} fusion(bf16[3584,256]{1,0:T(8,128)(2,1)} %bitcast.72, bf16[3584,256]{1,0:T(8,128)(2,1)} %bitcast.71, bf16[1,768,3584]{2,1,0:T(8,128)(2,1)} %param.12), kind=kOutput, calls=%fused_computation.24 | convolution fusion | flops 2826305536 | bytes 9961472 | tf_op jit(solution)/shard_map/dot_general | solution.py:310
  124.5 0.9 copy.28
  125.4 1.7 fusion.14.margin_q
  127.1 26.1 %shard_map.85 = bf16[768,512]{1,0:T(8,128)(2,1)} custom-call(bf16[768,512]{1,0:T(8,128)(2,1)} %fusion.26.g, f32[768,128]{1,0:T(8,128)} %bitcast.65, f32[768,128]{1,0:T(8,128)} %fusion.14.margin_q), custom_call_target="tpu_custom_call" | custom-call | tf_op jit(solution)/shard_map/pallas_call | solution.py:278
  153.3 5.7 %convert_bitcast_fusion.1.xa = bf16[4,4,224,256]{3,2,1,0:T(8,128)(2,1)} fusion(bf16[4,4,224,768]{3,2,1,0:T(8,128)(2,1)} %bitcast.67, bf16[768,512]{1,0:T(8,128)(2,1)} %shard_map.85), kind=kOutput, calls=%fused_computation.19 | convolution fusion | flops 1410203648 | bytes 7733248 | tf_op jit(solution)/shard_map/abdf,fr->badr/dot_general | solution.py:327
  159.0 2.8 %convert_bitcast_fusion.xb = bf16[4,4,224,256]{3,2,1,0:T(8,128)(2,1)} fusion(bf16[4,4,224,768]{3,2,1,0:T(8,128)(2,1)S(1)} %bitcast.70, bf16[768,512]{1,0:T(8,128)(2,1)S(1)} %copy-done.2), kind=kOutput, calls=%fused_computation.18 | convolution fusion | flops 1410203648 | bytes 7733248 | tf_op jit(solution)/shard_map/abdf,fr->abdr/dot_general | solution.py:328
  161.8 33.7 %shard_map.86 = f32[2,224,256]{2,1,0:T(8,128)} custom-call(bf16[4,4,224,256]{3,2,1,0:T(8,128)(2,1)} %convert_bitcast_fusion.1.xa, bf16[4,4,224,256]{3,2,1,0:T(8,128)(2,1)} %convert_bitcast_fusion.xb), custom_call_target="tpu_custom_call" | custom-call | tf_op jit(solution)/shard_map/pallas_call | solution.py:92
  195.5 1.0 convert_bitcast_fusion.3
  196.6 0.2 copy.30
  196.8 0.8 reshape.37
  (26 shorter events, 0.1 us)
Async XLA Ops:
  0.0 83.0 %copy-start = (f32[1,3584]{1,0:T(1,128)S(1)}, f32[1,3584]{1,0:T(1,128)}, u32[]{:S(2)}) copy-start(f32[1,3584]{1,0:T(1,128)} %param.13) | copy-start | bytes 43012
  1.6 7.9 %copy-start.4 = (f32[768]{0:T(1024)S(1)}, f32[768]{0:T(1024)}, u32[]{:S(2)}) copy-start(f32[768]{0:T(1024)} %param.11) | copy-start | bytes 9220
  10.0 32.0 %slice-start = ((s8[5505024]{0:T(1024)(128)(4,1)}), s8[1310720]{0:T(1024)(128)(4,1)S(1)}, s32[]{:S(2)}) async-start(s8[5505024]{0:T(1024)(128)(4,1)} %bitcast.60), calls=%async_computation | async-start | bytes 2621440
  35.4 6.7 %slice-start.1 = ((s8[5505024]{0:T(1024)(128)(4,1)}), s8[4194304]{0:T(1024)(128)(4,1)S(1)}, s32[]{:S(2)}) async-start(s8[5505024]{0:T(1024)(128)(4,1)} %bitcast.60), calls=%async_computation.1 | async-start | bytes 8388608
  40.6 1.5 copy-start.1
  116.9 7.6 %copy-start.3 = (f32[128,768]{1,0:T(8,128)S(1)}, f32[128,768]{1,0:T(8,128)}, u32[]{:S(2)}) copy-start(f32[128,768]{1,0:T(8,128)} %get-tuple-element.12) | copy-start | bytes 1179652
  116.9 8.5 %copy-start.5 = (s32[1024]{0:T(1024)S(1)}, s32[1024]{0:T(1024)}, u32[]{:S(2)}) copy-start(s32[1024]{0:T(1024)} %param.15) | copy-start | bytes 12292
  116.9 8.5 %copy-start.6 = (s32[1024]{0:T(1024)S(1)}, s32[1024]{0:T(1024)}, u32[]{:S(2)}) copy-start(s32[1024]{0:T(1024)} %param.14) | copy-start | bytes 12292
  127.1 31.9 %slice-start.2 = ((s8[5505024]{0:T(1024)(128)(4,1)}), s8[1310720]{0:T(1024)(128)(4,1)S(1)}, s32[]{:S(2)}) async-start(s8[5505024]{0:T(1024)(128)(4,1)} %bitcast.68), calls=%async_computation.2 | async-start | bytes 2621440
  153.2 5.7 %copy-start.2 = (bf16[768,512]{1,0:T(8,128)(2,1)S(1)}, bf16[768,512]{1,0:T(8,128)(2,1)}, u32[]{:S(2)}) copy-start(bf16[768,512]{1,0:T(8,128)(2,1)} %shard_map.85) | copy-start | bytes 2359300
  153.3 5.7 %slice-start.3 = ((s8[5505024]{0:T(1024)(128)(4,1)}), s8[4194304]{0:T(1024)(128)(4,1)S(1)}, s32[]{:S(2)}) async-start(s8[5505024]{0:T(1024)(128)(4,1)} %bitcast.68), calls=%async_computation.3 | async-start | bytes 8388608

commit v9 on v8

--- a/solution.py
+++ b/solution.py
@@ -38,7 +38,7 @@
     peers_x = [(a + k) % RING for k in range(1, RING)]
     first = []
     for t in peers_z:
-        c = _copy(xa.at[t], r1a.at[b], send_sems.at[0, t], recv_sems.at[0, b], a * RING + t)
+        c = _copy(xa.at[:, t], r1a.at[b], send_sems.at[0, t], recv_sems.at[0, b], a * RING + t)
         c.start()
         first.append(c)
     for t in peers_x:
@@ -46,10 +46,10 @@
         c.start()
         first.append(c)
     for t in peers_z:
-        _copy(xa.at[t], r1a.at[t], send_sems.at[0, t], recv_sems.at[0, t], 0).wait_recv()
+        _copy(xa.at[:, t], r1a.at[t], send_sems.at[0, t], recv_sems.at[0, t], 0).wait_recv()
     for t in peers_x:
         _copy(xb.at[t], r1b.at[t], send_sems.at[1, t], recv_sems.at[1, t], 0).wait_recv()
-    sum_a = xa[b].astype(jnp.float32)
+    sum_a = xa[:, b].astype(jnp.float32)
     for t in peers_z:
         sum_a = sum_a + r1a[t].astype(jnp.float32)
     sum_b = xb[a].astype(jnp.float32)
@@ -70,7 +70,7 @@
         _copy(s1a.at[t], r2a.at[t], send_sems.at[2, t], recv_sems.at[2, t], 0).wait_recv()
     for t in peers_z:
         _copy(s1b.at[t], r2b.at[t], send_sems.at[3, t], recv_sems.at[3, t], 0).wait_recv()
-    own_a = xa[b, a].astype(jnp.float32)
+    own_a = xa[a, b].astype(jnp.float32)
     for t in peers_z:
         own_a = own_a + r1a[t, a].astype(jnp.float32)
     own_b = xb[a, b].astype(jnp.float32)
@@ -264,12 +264,50 @@
     )(x, bias)
 
 
-def _layer_grad_kernel(g, pre_q, margin_q, out, *scratch):
-    def finish(total):
-        grad = jnp.where(pre_q[...] > 0, total - MARGIN * margin_q[...], 0.0)
-        return grad.astype(out.dtype)
-
-    _layer_exchange(_lane_quarter, g, out, finish, *scratch)
+def _layer_peers():
+    me = lax.axis_index("layer")
+    return me, [(me + k) % LAYERS for k in range(1, LAYERS)]
+
+
+def _layer_greet(peers):
+    barrier = pltpu.get_barrier_semaphore()
+    for p in peers:
+        pl.semaphore_signal(barrier, inc=1, device_id={"layer": p}, device_id_type=MESH)
+    pl.semaphore_wait(barrier, LAYERS - 1)
+
+
+def _layer_copy(src, dst, send_sems, recv_sems, k, p, slot):
+    return pltpu.make_async_remote_copy(
+        src_ref=src, dst_ref=dst, send_sem=send_sems.at[k, p], recv_sem=recv_sems.at[k, slot],
+        device_id={"layer": p}, device_id_type=MESH,
+    )
+
+
+def _layer_grad_kernel(g, pre_q, margin_q, out, r1, r2, send_sems, recv_sems):
+    me, peers = _layer_peers()
+    q = g.shape[1] // LAYERS
+    lanes = lambda i: pl.ds(pl.multiple_of(i * q, q), q)
+    _layer_greet(peers)
+    sent = []
+    for p in peers:
+        c = _layer_copy(g.at[:, lanes(p)], r1.at[me], send_sems, recv_sems, 0, p, me)
+        c.start()
+        sent.append(c)
+    total = g[:, lanes(me)].astype(jnp.float32)
+    for p in peers:
+        _layer_copy(g.at[:, lanes(p)], r1.at[p], send_sems, recv_sems, 0, p, p).wait_recv()
+        total = total + r1[p].astype(jnp.float32)
+    grad = jnp.where(pre_q[...] > 0, total - MARGIN * margin_q[...], 0.0)
+    out[:, lanes(me)] = grad.astype(out.dtype)
+    for p in peers:
+        c = _layer_copy(out.at[:, lanes(me)], r2.at[me], send_sems, recv_sems, 1, p, me)
+        c.start()
+        sent.append(c)
+    for p in peers:
+        _layer_copy(out.at[:, lanes(p)], r2.at[p], send_sems, recv_sems, 1, p, p).wait_recv()
+        out[:, lanes(p)] = r2[p]
+    for c in sent:
+        c.wait_send()
 
 
 def layer_grad(g, pre_q, margin_q):
@@ -280,7 +318,12 @@
         out_shape=jax.ShapeDtypeStruct((cols, rows), jnp.bfloat16),
         in_specs=[pl.BlockSpec(memory_space=pltpu.VMEM)] * 3,
         out_specs=pl.BlockSpec(memory_space=pltpu.VMEM),
-        scratch_shapes=_layer_scratch((cols, q), (cols, q), g.dtype),
+        scratch_shapes=[
+            pltpu.VMEM((LAYERS, cols, q), jnp.bfloat16),
+            pltpu.VMEM((LAYERS, cols, q), jnp.bfloat16),
+            pltpu.SemaphoreType.DMA((2, LAYERS)),
+            pltpu.SemaphoreType.DMA((2, LAYERS)),
+        ],
         compiler_params=pltpu.CompilerParams(collective_id=2, has_side_effects=True),
     )(g, pre_q, margin_q)
 
@@ -296,7 +339,7 @@
     partial_pre = jnp.einsum("rld,ldf->rf", inputs, enc_weight, preferred_element_type=jnp.float32)
     features, pre_q = layer_pre(partial_pre, enc_bias[None, :])
     dec4 = dec_weight[0].reshape(lat_count, RING, RING, chunk)
-    recon_a = jnp.einsum("rf,fabd->badr", features[:half], dec4, preferred_element_type=jnp.float32)
+    recon_a = jnp.einsum("rf,fabd->abdr", features[:half], dec4, preferred_element_type=jnp.float32)
     recon_b = jnp.einsum("rf,fabd->abdr", features[half:], dec4, preferred_element_type=jnp.float32)
     recon_sum = latent_reduce(recon_a.astype(jnp.bfloat16), recon_b.astype(jnp.bfloat16), 3)
     bias_part = lax.dynamic_slice_in_dim(dec_bias[0], me * chunk, chunk)
@@ -324,7 +367,7 @@
     margin_q = jnp.dot(target_hot_t, pair_table_t, preferred_element_type=jnp.float32)
     pre_grad_t = layer_grad(partial_grad_t.astype(jnp.bfloat16), pre_q.T, margin_q)
     enc4 = enc_weight[0].reshape(RING, RING, chunk, lat_count)
-    input_a = jnp.einsum("abdf,fr->badr", enc4, pre_grad_t[:, :half], preferred_element_type=jnp.float32)
+    input_a = jnp.einsum("abdf,fr->abdr", enc4, pre_grad_t[:, :half], preferred_element_type=jnp.float32)
     input_b = jnp.einsum("abdf,fr->abdr", enc4, pre_grad_t[:, half:], preferred_element_type=jnp.float32)
     total = latent_reduce(input_a.astype(jnp.bfloat16), input_b.astype(jnp.bfloat16), 5)
     return jnp.swapaxes(total.astype(jnp.bfloat16), 1, 2).reshape(row_count, 1, chunk)

time: 198 us -> 196 us (0.990)
  no operation moved by 1% of the time
where the time goes in v9:
time: 196 us
  Pallas kernels  153 us (78%)
  matrix products  33.2 us (17%)
  other arithmetic  5.16 us (3%)
  local copies, waits for them, and re-layouts  4.28 us (2%)
    pallas_call x2, Pallas kernels, latent_reduce(): pl.pallas_call(_reduce_kernel, out_shape=jax.ShapeDtypeStruct((2, h, c),...  70.4 us
    pallas_call x1, Pallas kernels, latent_gather(): pl.pallas_call(_gather_kernel, out_shape=(full, full), in_specs=[pl.Block...  31.9 us
    pallas_call x1, Pallas kernels, layer_pre(): pl.pallas_call(_layer_pre_kernel, out_shape=(jax.ShapeDtypeStruct((rows,...  25.3 us
    pallas_call x1, Pallas kernels, layer_grad(): pl.pallas_call(_layer_grad_kernel, out_shape=jax.ShapeDtypeStruct((cols,...  25.1 us
    dot_general x1, matrix products, local(): jnp.einsum('rld,ldf->rf', inputs, enc_weight, preferred_element_type=jnp....  7.86 us
    dot_general x1, matrix products, local(): jnp.dot(dec_weight[0], error_all, preferred_element_type=jnp.float32)  7.56 us
    unnamed x2, matrix products  7.55 us
    dot_general x1, matrix products, local(): jnp.einsum('abdf,fr->abdr', enc4, pre_grad_t[:, :half], preferred_element...  5.69 us

profile of v9, /device:TPU:1, one launch (start us, length us, event | category | flops | bytes accessed | tf_op | source)
XLA Modules:
  0.0 195.6 jit_solution(3962519262876088146)
XLA Ops:
  0.0 1.1 constant_dynamic-slice_fusion
  1.2 0.1 copy.28
  1.3 0.3 reshape.38
  1.6 7.9 %fusion.6.x = f32[512,768]{1,0:T(8,128)} fusion(bf16[1,3584,768]{2,1,0:T(8,128)(2,1)} %param.10, bf16[512,1,3584]{2,0,1:T(8,128)(2,1)} %param.8), kind=kOutput, calls=%fused_computation.6 | convolution fusion | flops 2818572288 | bytes 10747904 | tf_op jit(solution)/shard_map/rld,ldf->rf/dot_general | solution.py:339
  9.5 0.6 broadcast_in_dim.2.bias
  10.0 25.3 %shard_map.82 = (bf16[512,768]{1,0:T(8,128)(2,1)}, f32[128,768]{1,0:T(8,128)}) custom-call(f32[512,768]{1,0:T(8,128)} %fusion.6.x, f32[1,768]{1,0:T(1,128)} %broadcast_in_dim.2.bias), custom_call_target="tpu_custom_call" | custom-call | tf_op jit(solution)/shard_map/pallas_call | solution.py:256
  35.4 0.0 slice-start.1
  35.4 5.2 %fusion = f32[256,3584]{0,1:S(1)} fusion(bf16[1,768,3584]{2,1,0:T(8,128)(2,1)} %param.12, bf16[512,768]{1,0:T(8,128)(2,1)} %get-tuple-element.9), kind=kOutput, calls=%fused_computation | convolution fusion | flops 1409286144 | bytes 9568256
  40.6 2.4 %fusion.2 = f32[256,3584]{0,1:S(1)} fusion(bf16[1,768,3584]{2,1,0:T(8,128)(2,1)S(1)} %bitcast.63, bf16[512,768]{1,0:T(8,128)(2,1)S(1)} %copy-done.1), kind=kOutput, calls=%fused_computation.2 | convolution fusion | flops 1409286144 | bytes 9568256
  43.0 2.3 %convert_bitcast_fusion.2 = (bf16[4,4,224,256]{3,2,1,0:T(8,128)(2,1)}, bf16[4,4,224,256]{3,2,1,0:T(8,128)(2,1)}) fusion(f32[256,4,4,224]{0,3,2,1:T(8,128)S(1)} %bitcast.64, f32[256,4,4,224]{0,3,2,1:T(8,128)S(1)} %bitcast.65), kind=kLoop, calls=%fused_computation.16 | loop fusion | flops 1835008 | bytes 11010048 | tf_op jit(solution)/shard_map/convert_element_type | solution.py:344
  45.3 37.1 %shard_map.83 = f32[2,224,256]{2,1,0:T(8,128)} custom-call(bf16[4,4,224,256]{3,2,1,0:T(8,128)(2,1)} %get-tuple-element.14.xa, bf16[4,4,224,256]{3,2,1,0:T(8,128)(2,1)} %get-tuple-element.13.xb), custom_call_target="tpu_custom_call" | custom-call | tf_op jit(solution)/shard_map/pallas_call | solution.py:92
  82.4 0.1 constant_dynamic-slice_fusion.1
  82.5 1.8 fusion.26.e
  84.3 31.9 %shard_map.84 = (bf16[4,4,224,256]{3,2,1,0:T(8,128)(2,1)}, bf16[4,4,224,256]{3,2,1,0:T(8,128)(2,1)}) custom-call(bf16[2,224,256]{2,1,0:T(8,128)(2,1)} %fusion.26.e), custom_call_target="tpu_custom_call" | custom-call | tf_op jit(solution)/shard_map/pallas_call | solution.py:159
  116.2 7.6 %fusion.21.g = bf16[768,512]{1,0:T(8,128)(2,1)} fusion(bf16[3584,256]{1,0:T(8,128)(2,1)} %bitcast.73, bf16[3584,256]{1,0:T(8,128)(2,1)} %bitcast.72, bf16[1,768,3584]{2,1,0:T(8,128)(2,1)} %param.12), kind=kOutput, calls=%fused_computation.21 | convolution fusion | flops 2826305536 | bytes 9961472 | tf_op jit(solution)/shard_map/dot_general | solution.py:353
  123.8 0.9 copy.23
  124.7 1.7 fusion.12.margin_q
  126.4 25.1 %shard_map.85 = bf16[768,512]{1,0:T(8,128)(2,1)} custom-call(bf16[768,512]{1,0:T(8,128)(2,1)} %fusion.21.g, f32[768,128]{1,0:T(8,128)} %bitcast.66, f32[768,128]{1,0:T(8,128)} %fusion.12.margin_q), custom_call_target="tpu_custom_call" | custom-call | tf_op jit(solution)/shard_map/pallas_call | solution.py:316
  151.6 5.7 %convert_bitcast_fusion.1.xa = bf16[4,4,224,256]{3,2,1,0:T(8,128)(2,1)} fusion(bf16[4,4,224,768]{3,2,1,0:T(8,128)(2,1)} %bitcast.68, bf16[768,512]{1,0:T(8,128)(2,1)} %shard_map.85), kind=kOutput, calls=%fused_computation.15 | convolution fusion | flops 1410203648 | bytes 7733248 | tf_op jit(solution)/shard_map/abdf,fr->abdr/dot_general | solution.py:370
  157.3 2.8 %convert_bitcast_fusion.xb = bf16[4,4,224,256]{3,2,1,0:T(8,128)(2,1)} fusion(bf16[4,4,224,768]{3,2,1,0:T(8,128)(2,1)S(1)} %bitcast.71, bf16[768,512]{1,0:T(8,128)(2,1)S(1)} %copy-done.2), kind=kOutput, calls=%fused_computation.14 | convolution fusion | flops 1410203648 | bytes 7733248 | tf_op jit(solution)/shard_map/abdf,fr->abdr/dot_general | solution.py:371
  160.1 33.3 %shard_map.86 = f32[2,224,256]{2,1,0:T(8,128)} custom-call(bf16[4,4,224,256]{3,2,1,0:T(8,128)(2,1)} %convert_bitcast_fusion.1.xa, bf16[4,4,224,256]{3,2,1,0:T(8,128)(2,1)} %convert_bitcast_fusion.xb), custom_call_target="tpu_custom_call" | custom-call | tf_op jit(solution)/shard_map/pallas_call | solution.py:92
  193.4 1.0 convert_bitcast_fusion.4
  194.5 0.2 copy.24
  194.7 0.8 reshape.37
  (25 shorter events, 0.1 us)
Async XLA Ops:
  0.0 82.4 %copy-start = (f32[1,3584]{1,0:T(1,128)S(1)}, f32[1,3584]{1,0:T(1,128)}, u32[]{:S(2)}) copy-start(f32[1,3584]{1,0:T(1,128)} %param.13) | copy-start | bytes 43012
  1.6 7.9 %copy-start.4 = (f32[768]{0:T(1024)S(1)}, f32[768]{0:T(1024)}, u32[]{:S(2)}) copy-start(f32[768]{0:T(1024)} %param.11) | copy-start | bytes 9220
  10.0 30.6 %slice-start = ((s8[5505024]{0:T(1024)(128)(4,1)}), s8[1310720]{0:T(1024)(128)(4,1)S(1)}, s32[]{:S(2)}) async-start(s8[5505024]{0:T(1024)(128)(4,1)} %bitcast.62), calls=%async_computation | async-start | bytes 2621440
  35.4 5.2 %slice-start.1 = ((s8[5505024]{0:T(1024)(128)(4,1)}), s8[4194304]{0:T(1024)(128)(4,1)S(1)}, s32[]{:S(2)}) async-start(s8[5505024]{0:T(1024)(128)(4,1)} %bitcast.62), calls=%async_computation.1 | async-start | bytes 8388608
  35.4 5.2 %copy-start.1 = (bf16[512,768]{1,0:T(8,128)(2,1)S(1)}, bf16[512,768]{1,0:T(8,128)(2,1)}, u32[]{:S(2)}) copy-start(bf16[512,768]{1,0:T(8,128)(2,1)} %get-tuple-element.9) | copy-start | bytes 2359300
  116.2 7.6 %copy-start.3 = (f32[128,768]{1,0:T(8,128)S(1)}, f32[128,768]{1,0:T(8,128)}, u32[]{:S(2)}) copy-start(f32[128,768]{1,0:T(8,128)} %get-tuple-element.12) | copy-start | bytes 1179652
  116.2 8.5 %copy-start.5 = (s32[1024]{0:T(1024)S(1)}, s32[1024]{0:T(1024)}, u32[]{:S(2)}) copy-start(s32[1024]{0:T(1024)} %param.15) | copy-start | bytes 12292
  116.2 8.5 %copy-start.6 = (s32[1024]{0:T(1024)S(1)}, s32[1024]{0:T(1024)}, u32[]{:S(2)}) copy-start(s32[1024]{0:T(1024)} %param.14) | copy-start | bytes 12292
  126.4 30.9 %slice-start.2 = ((s8[5505024]{0:T(1024)(128)(4,1)}), s8[1310720]{0:T(1024)(128)(4,1)S(1)}, s32[]{:S(2)}) async-start(s8[5505024]{0:T(1024)(128)(4,1)} %bitcast.69), calls=%async_computation.2 | async-start | bytes 2621440
  151.6 5.7 %copy-start.2 = (bf16[768,512]{1,0:T(8,128)(2,1)S(1)}, bf16[768,512]{1,0:T(8,128)(2,1)}, u32[]{:S(2)}) copy-start(bf16[768,512]{1,0:T(8,128)(2,1)} %shard_map.85) | copy-start | bytes 2359300
  151.6 5.7 %slice-start.3 = ((s8[5505024]{0:T(1024)(128)(4,1)}), s8[4194304]{0:T(1024)(128)(4,1)S(1)}, s32[]{:S(2)}) async-start(s8[5505024]{0:T(1024)(128)(4,1)} %bitcast.69), calls=%async_computation.3 | async-start | bytes 8388608

commit v10 on v9

--- a/solution.py
+++ b/solution.py
@@ -106,6 +106,97 @@
         ],
         compiler_params=pltpu.CompilerParams(collective_id=collective_id, has_side_effects=True),
     )(xa, xb)
+
+
+def _reduce_mm_kernel(w, v, out, xa, xb, r1a, r1b, s1a, s1b, r2a, r2b, send_sems, recv_sems):
+    a, b = _latent_coords()
+    _greet(a, b)
+    h = v.shape[1] // 2
+    peers_z = [(b + k) % RING for k in range(1, RING)]
+    peers_x = [(a + k) % RING for k in range(1, RING)]
+
+    def fill(dst, i, j, half):
+        prod = jnp.dot(w[i, j], v[:, half * h:(half + 1) * h], preferred_element_type=jnp.float32)
+        dst[i, j] = prod.astype(dst.dtype)
+
+    first = []
+    for kz, kx in zip(peers_z, peers_x):
+        for i in range(RING):
+            fill(xa, i, kz, 0)
+        c = _copy(xa.at[:, kz], r1a.at[b], send_sems.at[0, kz], recv_sems.at[0, b], a * RING + kz)
+        c.start()
+        first.append(c)
+        for j in range(RING):
+            fill(xb, kx, j, 1)
+        c = _copy(xb.at[kx], r1b.at[a], send_sems.at[1, kx], recv_sems.at[1, a], kx * RING + b)
+        c.start()
+        first.append(c)
+    for i in range(RING):
+        fill(xa, i, b, 0)
+    for j in range(RING):
+        fill(xb, a, j, 1)
+    for t in peers_z:
+        _copy(xa.at[:, t], r1a.at[t], send_sems.at[0, t], recv_sems.at[0, t], 0).wait_recv()
+    for t in peers_x:
+        _copy(xb.at[t], r1b.at[t], send_sems.at[1, t], recv_sems.at[1, t], 0).wait_recv()
+    sum_a = xa[:, b].astype(jnp.float32)
+    for t in peers_z:
+        sum_a = sum_a + r1a[t].astype(jnp.float32)
+    sum_b = xb[a].astype(jnp.float32)
+    for t in peers_x:
+        sum_b = sum_b + r1b[t].astype(jnp.float32)
+    s1a[...] = sum_a.astype(s1a.dtype)
+    s1b[...] = sum_b.astype(s1b.dtype)
+    second = []
+    for t in peers_x:
+        c = _copy(s1a.at[t], r2a.at[a], send_sems.at[2, t], recv_sems.at[2, a], t * RING + b)
+        c.start()
+        second.append(c)
+    for t in peers_z:
+        c = _copy(s1b.at[t], r2b.at[b], send_sems.at[3, t], recv_sems.at[3, b], a * RING + t)
+        c.start()
+        second.append(c)
+    for t in peers_x:
+        _copy(s1a.at[t], r2a.at[t], send_sems.at[2, t], recv_sems.at[2, t], 0).wait_recv()
+    for t in peers_z:
+        _copy(s1b.at[t], r2b.at[t], send_sems.at[3, t], recv_sems.at[3, t], 0).wait_recv()
+    own_a = xa[a, b].astype(jnp.float32)
+    own_b = xb[a, b].astype(jnp.float32)
+    for k in range(1, RING):
+        own_a = own_a + r1a[(b + k) % RING, a].astype(jnp.float32)
+        own_b = own_b + r1b[(a + k) % RING, b].astype(jnp.float32)
+    for k in range(1, RING):
+        own_a = own_a + r2a[(a + k) % RING].astype(jnp.float32)
+        own_b = own_b + r2b[(b + k) % RING].astype(jnp.float32)
+    out[0] = own_a
+    out[1] = own_b
+    for c in first + second:
+        c.wait_send()
+
+
+def latent_reduce_mm(w, v, collective_id):
+    n, _, d, _ = w.shape
+    h = v.shape[1] // 2
+    dt = w.dtype
+    return pl.pallas_call(
+        _reduce_mm_kernel,
+        out_shape=jax.ShapeDtypeStruct((2, d, h), jnp.float32),
+        in_specs=[pl.BlockSpec(memory_space=pltpu.VMEM)] * 2,
+        out_specs=pl.BlockSpec(memory_space=pltpu.VMEM),
+        scratch_shapes=[
+            pltpu.VMEM((n, n, d, h), dt),
+            pltpu.VMEM((n, n, d, h), dt),
+            pltpu.VMEM((n, n, d, h), dt),
+            pltpu.VMEM((n, n, d, h), dt),
+            pltpu.VMEM((n, d, h), dt),
+            pltpu.VMEM((n, d, h), dt),
+            pltpu.VMEM((n, d, h), dt),
+            pltpu.VMEM((n, d, h), dt),
+            pltpu.SemaphoreType.DMA((4, n)),
+            pltpu.SemaphoreType.DMA((4, n)),
+        ],
+        compiler_params=pltpu.CompilerParams(collective_id=collective_id, has_side_effects=True),
+    )(w, v)
 
 
 def _gather_kernel(e, oa, ob, g1a, g1b, ga, gb, send_sems, recv_sems):
@@ -367,9 +458,7 @@
     margin_q = jnp.dot(target_hot_t, pair_table_t, preferred_element_type=jnp.float32)
     pre_grad_t = layer_grad(partial_grad_t.astype(jnp.bfloat16), pre_q.T, margin_q)
     enc4 = enc_weight[0].reshape(RING, RING, chunk, lat_count)
-    input_a = jnp.einsum("abdf,fr->abdr", enc4, pre_grad_t[:, :half], preferred_element_type=jnp.float32)
-    input_b = jnp.einsum("abdf,fr->abdr", enc4, pre_grad_t[:, half:], preferred_element_type=jnp.float32)
-    total = latent_reduce(input_a.astype(jnp.bfloat16), input_b.astype(jnp.bfloat16), 5)
+    total = latent_reduce_mm(enc4, pre_grad_t, 5)
     return jnp.swapaxes(total.astype(jnp.bfloat16), 1, 2).reshape(row_count, 1, chunk)
 
 

time: 196 us -> 190 us (0.969)
  matrix products: 33.2 us -> 24.7 us
  Pallas kernels: 153 us -> 155 us
    pallas_call x0 -> x1, Pallas kernels: none -> 35.8 us  [latent_reduce_mm(): pl.pallas_call(_reduce_mm_kernel, out_shape=jax.ShapeDtypeStruct((2, d, h...]
    pallas_call x2 -> x1, Pallas kernels: 70.4 us -> 37.1 us  [latent_reduce(): pl.pallas_call(_reduce_kernel, out_shape=jax.ShapeDtypeStruct((2, h, c),...]
    dot_general x2 -> x0, matrix products: 8.52 us -> none  [the longest x1 5.69 us: local(): jnp.einsum('abdf,fr->abdr', enc4, pre_grad_t[:, :half], preferred_element...]
where the time goes in v10:
time: 190 us; the launch traced here: 189 us
  Pallas kernels  155 us (82%)
  matrix products  24.7 us (13%)
  other arithmetic  5.16 us (3%)
  local copies, waits for them, and re-layouts  4.26 us (2%)
    pallas_call x1, Pallas kernels, latent_reduce(): pl.pallas_call(_reduce_kernel, out_shape=jax.ShapeDtypeStruct((2, h, c),...  37.1 us
    pallas_call x1, Pallas kernels, latent_reduce_mm(): pl.pallas_call(_reduce_mm_kernel, out_shape=jax.ShapeDtypeStruct((2, d, h...  35.8 us
    pallas_call x1, Pallas kernels, latent_gather(): pl.pallas_call(_gather_kernel, out_shape=(full, full), in_specs=[pl.Block...  31.9 us
    pallas_call x1, Pallas kernels, layer_pre(): pl.pallas_call(_layer_pre_kernel, out_shape=(jax.ShapeDtypeStruct((rows,...  25.3 us
    pallas_call x1, Pallas kernels, layer_grad(): pl.pallas_call(_layer_grad_kernel, out_shape=jax.ShapeDtypeStruct((cols,...  25 us
    dot_general x1, matrix products, local(): jnp.einsum('rld,ldf->rf', inputs, enc_weight, preferred_element_type=jnp....  7.85 us
    dot_general x1, matrix products, local(): jnp.dot(dec_weight[0], error_all, preferred_element_type=jnp.float32)  7.55 us
    unnamed x2, matrix products  7.55 us

profile of v10, /device:TPU:1, one launch (start us, length us, event | category | flops | bytes accessed | tf_op | source)
XLA Modules:
  0.0 189.4 jit_solution(6428826781385805867)
XLA Ops:
  0.0 1.1 constant_dynamic-slice_fusion
  1.2 0.1 copy.26
  1.3 0.3 reshape.38
  1.6 0.0 copy-start.3
  1.6 7.9 %fusion.6.x = f32[512,768]{1,0:T(8,128)} fusion(bf16[1,3584,768]{2,1,0:T(8,128)(2,1)} %param.10, bf16[512,1,3584]{2,0,1:T(8,128)(2,1)} %param.8), kind=kOutput, calls=%fused_computation.6 | convolution fusion | flops 2818572288 | bytes 10747904 | tf_op jit(solution)/shard_map/rld,ldf->rf/dot_general | solution.py:430
  9.5 0.6 broadcast_in_dim.2.bias
  10.0 25.3 %shard_map.82 = (bf16[512,768]{1,0:T(8,128)(2,1)}, f32[128,768]{1,0:T(8,128)}) custom-call(f32[512,768]{1,0:T(8,128)} %fusion.6.x, f32[1,768]{1,0:T(1,128)} %broadcast_in_dim.2.bias), custom_call_target="tpu_custom_call" | custom-call | tf_op jit(solution)/shard_map/pallas_call | solution.py:347
  35.4 0.0 slice-start.1
  35.4 5.2 %fusion = f32[256,3584]{0,1:S(1)} fusion(bf16[1,768,3584]{2,1,0:T(8,128)(2,1)} %param.12, bf16[512,768]{1,0:T(8,128)(2,1)} %get-tuple-element.9), kind=kOutput, calls=%fused_computation | convolution fusion | flops 1409286144 | bytes 9568256
  40.6 2.4 %fusion.2 = f32[256,3584]{0,1:S(1)} fusion(bf16[1,768,3584]{2,1,0:T(8,128)(2,1)S(1)} %bitcast.47, bf16[512,768]{1,0:T(8,128)(2,1)S(1)} %copy-done.1), kind=kOutput, calls=%fused_computation.2 | convolution fusion | flops 1409286144 | bytes 9568256
  43.0 2.3 %convert_bitcast_fusion = (bf16[4,4,224,256]{3,2,1,0:T(8,128)(2,1)}, bf16[4,4,224,256]{3,2,1,0:T(8,128)(2,1)}) fusion(f32[256,4,4,224]{0,3,2,1:T(8,128)S(1)} %bitcast.48, f32[256,4,4,224]{0,3,2,1:T(8,128)S(1)} %bitcast.49), kind=kLoop, calls=%fused_computation.14 | loop fusion | flops 1835008 | bytes 11010048 | tf_op jit(solution)/shard_map/convert_element_type | solution.py:435
  45.3 37.1 %shard_map.83 = f32[2,224,256]{2,1,0:T(8,128)} custom-call(bf16[4,4,224,256]{3,2,1,0:T(8,128)(2,1)} %get-tuple-element.14.xa, bf16[4,4,224,256]{3,2,1,0:T(8,128)(2,1)} %get-tuple-element.13.xb), custom_call_target="tpu_custom_call" | custom-call | tf_op jit(solution)/shard_map/pallas_call | solution.py:92
  82.4 0.1 constant_dynamic-slice_fusion.1
  82.5 1.8 fusion.26.e
  84.3 31.9 %shard_map.84 = (bf16[4,4,224,256]{3,2,1,0:T(8,128)(2,1)}, bf16[4,4,224,256]{3,2,1,0:T(8,128)(2,1)}) custom-call(bf16[2,224,256]{2,1,0:T(8,128)(2,1)} %fusion.26.e), custom_call_target="tpu_custom_call" | custom-call | tf_op jit(solution)/shard_map/pallas_call | solution.py:250
  116.2 0.0 copy-start.5
  116.2 7.6 %fusion.21.g = bf16[768,512]{1,0:T(8,128)(2,1)} fusion(bf16[3584,256]{1,0:T(8,128)(2,1)} %bitcast.54, bf16[3584,256]{1,0:T(8,128)(2,1)} %bitcast.53, bf16[1,768,3584]{2,1,0:T(8,128)(2,1)} %param.12), kind=kOutput, calls=%fused_computation.19 | convolution fusion | flops 2826305536 | bytes 9961472 | tf_op jit(solution)/shard_map/dot_general | solution.py:444
  123.8 0.9 copy.23
  124.7 1.7 fusion.12.margin_q
  126.4 25.0 %shard_map.85.v = bf16[768,512]{1,0:T(8,128)(2,1)} custom-call(bf16[768,512]{1,0:T(8,128)(2,1)} %fusion.21.g, f32[768,128]{1,0:T(8,128)} %bitcast.51, f32[768,128]{1,0:T(8,128)} %fusion.12.margin_q), custom_call_target="tpu_custom_call" | custom-call | tf_op jit(solution)/shard_map/pallas_call | solution.py:407
  151.5 35.8 %shard_map.86 = f32[2,224,256]{2,1,0:T(8,128)} custom-call(bf16[4,4,224,768]{3,2,1,0:T(8,128)(2,1)} %bitcast.50, bf16[768,512]{1,0:T(8,128)(2,1)} %shard_map.85.v), custom_call_target="tpu_custom_call" | custom-call | tf_op jit(solution)/shard_map/pallas_call | solution.py:181
  187.3 1.0 convert_bitcast_fusion.2
  188.4 0.2 copy.24
  188.6 0.8 reshape.37
  (16 shorter events, 0.0 us)
Async XLA Ops:
  0.0 82.4 %copy-start = (f32[1,3584]{1,0:T(1,128)S(1)}, f32[1,3584]{1,0:T(1,128)}, u32[]{:S(2)}) copy-start(f32[1,3584]{1,0:T(1,128)} %param.13) | copy-start | bytes 43012
  1.6 7.9 %copy-start.3 = (f32[768]{0:T(1024)S(1)}, f32[768]{0:T(1024)}, u32[]{:S(2)}) copy-start(f32[768]{0:T(1024)} %param.11) | copy-start | bytes 9220
  10.0 30.6 %slice-start = ((s8[5505024]{0:T(1024)(128)(4,1)}), s8[1310720]{0:T(1024)(128)(4,1)S(1)}, s32[]{:S(2)}) async-start(s8[5505024]{0:T(1024)(128)(4,1)} %bitcast.46), calls=%async_computation | async-start | bytes 2621440
  35.4 5.2 %slice-start.1 = ((s8[5505024]{0:T(1024)(128)(4,1)}), s8[4194304]{0:T(1024)(128)(4,1)S(1)}, s32[]{:S(2)}) async-start(s8[5505024]{0:T(1024)(128)(4,1)} %bitcast.46), calls=%async_computation.1 | async-start | bytes 8388608
  35.4 5.2 %copy-start.1 = (bf16[512,768]{1,0:T(8,128)(2,1)S(1)}, bf16[512,768]{1,0:T(8,128)(2,1)}, u32[]{:S(2)}) copy-start(bf16[512,768]{1,0:T(8,128)(2,1)} %get-tuple-element.9) | copy-start | bytes 2359300
  116.2 7.6 %copy-start.2 = (f32[128,768]{1,0:T(8,128)S(1)}, f32[128,768]{1,0:T(8,128)}, u32[]{:S(2)}) copy-start(f32[128,768]{1,0:T(8,128)} %get-tuple-element.12) | copy-start | bytes 1179652
  116.2 8.5 %copy-start.4 = (s32[1024]{0:T(1024)S(1)}, s32[1024]{0:T(1024)}, u32[]{:S(2)}) copy-start(s32[1024]{0:T(1024)} %param.15) | copy-start | bytes 12292
  116.2 8.5 %copy-start.5 = (s32[1024]{0:T(1024)S(1)}, s32[1024]{0:T(1024)}, u32[]{:S(2)}) copy-start(s32[1024]{0:T(1024)} %param.14) | copy-start | bytes 12292

commit v11 on v10

--- a/solution.py
+++ b/solution.py
@@ -264,6 +264,63 @@
     )(e)
 
 
+def _gather_mm_kernel(e, w, out, g1, gx, acc, send_sems, recv_sems):
+    a, b = _latent_coords()
+    _greet(a, b)
+    peers_z = [(b + k) % RING for k in range(1, RING)]
+    peers_x = [(a + k) % RING for k in range(1, RING)]
+    halves, n, d, r = g1.shape
+    group = n * d
+
+    def add_group(block, i):
+        cols = w[:, pl.ds(pl.multiple_of(i * group, 128), group)]
+        for h in range(halves):
+            part = jnp.dot(cols, block[h].reshape(group, r), preferred_element_type=jnp.float32)
+            acc[:, h * r:(h + 1) * r] += part
+
+    sent = []
+    for t in peers_z:
+        c = _copy(e, g1.at[:, b], send_sems.at[0, t], recv_sems.at[0, b], a * RING + t)
+        c.start()
+        sent.append(c)
+    g1[:, b] = e[...]
+    for t in peers_z:
+        _copy(e, g1.at[:, t], send_sems.at[0, t], recv_sems.at[0, t], 0).wait_recv()
+    for t in peers_x:
+        c = _copy(g1, gx.at[a], send_sems.at[1, t], recv_sems.at[1, a], t * RING + b)
+        c.start()
+        sent.append(c)
+    acc[...] = jnp.zeros_like(acc)
+    add_group(g1, a)
+    for t in peers_x:
+        _copy(g1, gx.at[t], send_sems.at[1, t], recv_sems.at[1, t], 0).wait_recv()
+        add_group(gx.at[t], t)
+    out[...] = acc[...].astype(out.dtype)
+    for c in sent:
+        c.wait_send()
+
+
+def latent_gather_mm(e, w, collective_id):
+    halves, d, r = e.shape
+    n = RING
+    f = w.shape[0]
+    dt = e.dtype
+    return pl.pallas_call(
+        _gather_mm_kernel,
+        out_shape=jax.ShapeDtypeStruct((f, halves * r), jnp.bfloat16),
+        in_specs=[pl.BlockSpec(memory_space=pltpu.VMEM)] * 2,
+        out_specs=pl.BlockSpec(memory_space=pltpu.VMEM),
+        scratch_shapes=[
+            pltpu.VMEM((halves, n, d, r), dt),
+            pltpu.VMEM((n, halves, n, d, r), dt),
+            pltpu.VMEM((f, halves * r), jnp.float32),
+            pltpu.SemaphoreType.DMA((2, n)),
+            pltpu.SemaphoreType.DMA((2, n)),
+        ],
+        compiler_params=pltpu.CompilerParams(collective_id=collective_id, has_side_effects=True),
+    )(e, w)
+
+
 def _layer_roles():
     me = lax.axis_index("layer")
     mate = me + 1 - 2 * (me % 2)
@@ -437,11 +494,7 @@
     clean_part = lax.dynamic_slice_in_dim(clean_acts[:, 0, :], me * chunk, chunk, axis=1)
     clean_t = jnp.swapaxes(clean_part.reshape(2, half, chunk), 1, 2).astype(jnp.float32)
     recon_error = (recon_sum + bias_part[:, None] - clean_t).astype(jnp.bfloat16)
-    error_a, error_b = latent_gather(recon_error, 4)
-    error_all = jnp.concatenate(
-        [error_a.reshape(d_model, half), error_b.reshape(d_model, half)], axis=1
-    )
-    partial_grad_t = jnp.dot(dec_weight[0], error_all, preferred_element_type=jnp.float32)
+    partial_grad_t = latent_gather_mm(recon_error, dec_weight[0], 4)
     quarter = row_count // LAYERS
     row_ids = (
         lax.axis_index("row") * row_count
@@ -456,7 +509,7 @@
     ).astype(jnp.bfloat16)
     target_hot_t = (latent_ids[:, None] == targets[None, :]).astype(jnp.bfloat16)
     margin_q = jnp.dot(target_hot_t, pair_table_t, preferred_element_type=jnp.float32)
-    pre_grad_t = layer_grad(partial_grad_t.astype(jnp.bfloat16), pre_q.T, margin_q)
+    pre_grad_t = layer_grad(partial_grad_t, pre_q.T, margin_q)
     enc4 = enc_weight[0].reshape(RING, RING, chunk, lat_count)
     total = latent_reduce_mm(enc4, pre_grad_t, 5)
     return jnp.swapaxes(total.astype(jnp.bfloat16), 1, 2).reshape(row_count, 1, chunk)

time: 190 us -> 209 us (1.10)
  Pallas kernels: 155 us -> 182 us
  matrix products: 24.7 us -> 17 us
    pallas_call x1, Pallas kernels: 31.9 us -> 58.8 us  [latent_gather_mm(): pl.pallas_call(_gather_mm_kernel, out_shape=jax.ShapeDtypeStruct((f, halv...]
    dot_general x1 -> x0, matrix products: 7.55 us -> none  [local(): jnp.dot(dec_weight[0], error_all, preferred_element_type=jnp.float32)]
where the time goes in v11:
time: 209 us
  Pallas kernels  182 us (87%)
  matrix products  17 us (8%)
  other arithmetic  5.22 us (2%)
  local copies, waits for them, and re-layouts  4.25 us (2%)
    pallas_call x1, Pallas kernels, latent_gather_mm(): pl.pallas_call(_gather_mm_kernel, out_shape=jax.ShapeDtypeStruct((f, halv...  58.8 us
    pallas_call x1, Pallas kernels, latent_reduce(): pl.pallas_call(_reduce_kernel, out_shape=jax.ShapeDtypeStruct((2, h, c),...  37.1 us
    pallas_call x1, Pallas kernels, latent_reduce_mm(): pl.pallas_call(_reduce_mm_kernel, out_shape=jax.ShapeDtypeStruct((2, d, h...  37 us
    pallas_call x1, Pallas kernels, layer_pre(): pl.pallas_call(_layer_pre_kernel, out_shape=(jax.ShapeDtypeStruct((rows,...  25.3 us
    pallas_call x1, Pallas kernels, layer_grad(): pl.pallas_call(_layer_grad_kernel, out_shape=jax.ShapeDtypeStruct((cols,...  24.1 us
    dot_general x1, matrix products, local(): jnp.einsum('rld,ldf->rf', inputs, enc_weight, preferred_element_type=jnp....  7.84 us
    unnamed x2, matrix products  7.54 us

profile of v11, /device:TPU:1, one launch (start us, length us, event | category | flops | bytes accessed | tf_op | source)
XLA Modules:
  0.0 209.0 jit_solution(2124030377997163936)
XLA Ops:
  0.0 1.1 constant_dynamic-slice_fusion
  1.2 0.1 copy.22
  1.3 0.3 reshape.30
  1.6 0.0 copy-start.3
  1.6 7.8 %fusion.x = f32[512,768]{1,0:T(8,128)} fusion(bf16[1,3584,768]{2,1,0:T(8,128)(2,1)} %param.10, bf16[512,1,3584]{2,0,1:T(8,128)(2,1)} %param.8), kind=kOutput, calls=%fused_computation | convolution fusion | flops 2818572288 | bytes 10747904 | tf_op jit(solution)/shard_map/rld,ldf->rf/dot_general | solution.py:487
  9.4 0.0 copy-done.3
  9.4 0.6 broadcast_in_dim.2.bias
  10.0 25.3 %shard_map.82 = (bf16[512,768]{1,0:T(8,128)(2,1)}, f32[128,768]{1,0:T(8,128)}) custom-call(f32[512,768]{1,0:T(8,128)} %fusion.x, f32[1,768]{1,0:T(1,128)} %broadcast_in_dim.2.bias), custom_call_target="tpu_custom_call" | custom-call | tf_op jit(solution)/shard_map/pallas_call | solution.py:404
  35.3 0.0 slice-start.1
  35.4 5.2 %fusion.8 = f32[256,3584]{0,1:S(1)} fusion(bf16[512,768]{1,0:T(8,128)(2,1)} %get-tuple-element.7, bf16[1,768,3584]{2,1,0:T(8,128)(2,1)} %param.12), kind=kOutput, calls=%fused_computation.13 | convolution fusion | flops 1409286144 | bytes 9568256
  40.6 0.0 slice-done
  40.6 2.4 %fusion.10 = f32[256,3584]{0,1:S(1)} fusion(bf16[512,768]{1,0:T(8,128)(2,1)S(1)} %copy-done.1, bf16[1,768,3584]{2,1,0:T(8,128)(2,1)S(1)} %bitcast.38), kind=kOutput, calls=%fused_computation.15 | convolution fusion | flops 1409286144 | bytes 9568256
  43.0 2.3 %convert_bitcast_fusion = (bf16[4,4,224,256]{3,2,1,0:T(8,128)(2,1)}, bf16[4,4,224,256]{3,2,1,0:T(8,128)(2,1)}) fusion(f32[256,4,4,224]{0,3,2,1:T(8,128)S(1)} %bitcast.39, f32[256,4,4,224]{0,3,2,1:T(8,128)S(1)} %bitcast.40), kind=kLoop, calls=%fused_computation.5 | loop fusion | flops 1835008 | bytes 11010048 | tf_op jit(solution)/shard_map/convert_element_type | solution.py:492
  45.3 37.1 %shard_map.83 = f32[2,224,256]{2,1,0:T(8,128)} custom-call(bf16[4,4,224,256]{3,2,1,0:T(8,128)(2,1)} %get-tuple-element.10.xa, bf16[4,4,224,256]{3,2,1,0:T(8,128)(2,1)} %get-tuple-element.9.xb), custom_call_target="tpu_custom_call" | custom-call | tf_op jit(solution)/shard_map/pallas_call | solution.py:92
  82.3 0.1 constant_dynamic-slice_fusion.1
  82.4 1.9 fusion.7.e
  84.3 58.8 %shard_map.84.g = bf16[768,512]{1,0:T(8,128)(2,1)} custom-call(bf16[2,224,256]{2,1,0:T(8,128)(2,1)} %fusion.7.e, bf16[768,3584]{1,0:T(8,128)(2,1)} %bitcast.36), custom_call_target="tpu_custom_call" | custom-call | tf_op jit(solution)/shard_map/pallas_call | solution.py:308
  143.1 0.9 copy.20
  144.1 1.7 fusion.3.margin_q
  145.7 24.1 %shard_map.85.v = bf16[768,512]{1,0:T(8,128)(2,1)} custom-call(bf16[768,512]{1,0:T(8,128)(2,1)} %shard_map.84.g, f32[768,128]{1,0:T(8,128)} %bitcast.42, f32[768,128]{1,0:T(8,128)} %fusion.3.margin_q), custom_call_target="tpu_custom_call" | custom-call | tf_op jit(solution)/shard_map/pallas_call | solution.py:464
  169.9 37.0 %shard_map.86 = f32[2,224,256]{2,1,0:T(8,128)} custom-call(bf16[4,4,224,768]{3,2,1,0:T(8,128)(2,1)} %bitcast.41, bf16[768,512]{1,0:T(8,128)(2,1)} %shard_map.85.v), custom_call_target="tpu_custom_call" | custom-call | tf_op jit(solution)/shard_map/pallas_call | solution.py:181
  206.9 1.0 convert_bitcast_fusion.2
  207.9 0.2 copy.21
  208.2 0.8 reshape.29
  (15 shorter events, 0.0 us)
Async XLA Ops:
  0.0 82.3 %copy-start = (f32[1,3584]{1,0:T(1,128)S(1)}, f32[1,3584]{1,0:T(1,128)}, u32[]{:S(2)}) copy-start(f32[1,3584]{1,0:T(1,128)} %param.13) | copy-start | bytes 43012
  1.6 7.9 %copy-start.3 = (f32[768]{0:T(1024)S(1)}, f32[768]{0:T(1024)}, u32[]{:S(2)}) copy-start(f32[768]{0:T(1024)} %param.11) | copy-start | bytes 9220
  10.0 30.5 %slice-start = ((s8[5505024]{0:T(1024)(128)(4,1)}), s8[1310720]{0:T(1024)(128)(4,1)S(1)}, s32[]{:S(2)}) async-start(s8[5505024]{0:T(1024)(128)(4,1)} %bitcast.37), calls=%async_computation | async-start | bytes 2621440
  35.3 5.2 %slice-start.1 = ((s8[5505024]{0:T(1024)(128)(4,1)}), s8[4194304]{0:T(1024)(128)(4,1)S(1)}, s32[]{:S(2)}) async-start(s8[5505024]{0:T(1024)(128)(4,1)} %bitcast.37), calls=%async_computation.1 | async-start | bytes 8388608
  35.3 5.2 %copy-start.1 = (bf16[512,768]{1,0:T(8,128)(2,1)S(1)}, bf16[512,768]{1,0:T(8,128)(2,1)}, u32[]{:S(2)}) copy-start(bf16[512,768]{1,0:T(8,128)(2,1)} %get-tuple-element.7) | copy-start | bytes 2359300
  82.4 60.7 %copy-start.2 = (f32[128,768]{1,0:T(8,128)S(1)}, f32[128,768]{1,0:T(8,128)}, u32[]{:S(2)}) copy-start(f32[128,768]{1,0:T(8,128)} %get-tuple-element.8) | copy-start | bytes 1179652
  84.3 59.8 %copy-start.4 = (s32[1024]{0:T(1024)S(1)}, s32[1024]{0:T(1024)}, u32[]{:S(2)}) copy-start(s32[1024]{0:T(1024)} %param.15) | copy-start | bytes 12292
  84.3 59.8 %copy-start.5 = (s32[1024]{0:T(1024)S(1)}, s32[1024]{0:T(1024)}, u32[]{:S(2)}) copy-start(s32[1024]{0:T(1024)} %param.14) | copy-start | bytes 12292

commit v12 on v10

--- a/solution.py
+++ b/solution.py
@@ -271,7 +271,7 @@
     return me, mate, far, (mate + 2) % LAYERS
 
 
-def _layer_exchange(quarter, x, out, finish, ra, sb, rb, rc, rd, send_sems, recv_sems):
+def _layer_exchange(quarter, x, out, finish, produce, ra, sb, rb, rc, rd, send_sems, recv_sems):
     me, mate, far, mate_far = _layer_roles()
     barrier = pltpu.get_barrier_semaphore()
     for p in (mate, far):
@@ -284,9 +284,13 @@
             device_id={"layer": p}, device_id_type=MESH,
         )
 
+    produce(mate)
+    produce(mate_far)
     sent = [copy(quarter(x, mate), ra.at[0], 0, mate), copy(quarter(x, mate_far), ra.at[1], 1, mate)]
     for c in sent:
         c.start()
+    produce(far)
+    produce(me)
     sent[0].wait_recv()
     sent[1].wait_recv()
     sb[...] = quarter(x, far)[...].astype(jnp.float32) + ra[1].astype(jnp.float32)
@@ -320,13 +324,18 @@
     return ref.at[:, pl.ds(pl.multiple_of(i * q, q), q)]
 
 
-def _layer_pre_kernel(x, bias, feats, pre_q, *scratch):
+def _layer_pre_kernel(inp, w, bias, feats, pre_q, x, *scratch):
     def finish(total):
         pre = total + bias[...]
         pre_q[...] = pre
         return jnp.maximum(pre, 0.0).astype(feats.dtype)
 
-    _layer_exchange(_row_quarter, x, feats, finish, *scratch)
+    def produce(i):
+        _row_quarter(x, i)[...] = jnp.dot(
+            _row_quarter(inp, i)[...], w[...], preferred_element_type=jnp.float32
+        )
+
+    _layer_exchange(_row_quarter, x, feats, finish, produce, *scratch)
 
 
 def _layer_scratch(in_q, out_q, in_dtype):
@@ -341,18 +350,19 @@
     ]
 
 
-def layer_pre(x, bias):
-    rows, cols = x.shape
+def layer_pre(inp, w, bias):
+    rows, cols = inp.shape[0], w.shape[1]
     q = rows // LAYERS
     return pl.pallas_call(
         _layer_pre_kernel,
         out_shape=(jax.ShapeDtypeStruct((rows, cols), jnp.bfloat16),
                    jax.ShapeDtypeStruct((q, cols), jnp.float32)),
-        in_specs=[pl.BlockSpec(memory_space=pltpu.VMEM)] * 2,
+        in_specs=[pl.BlockSpec(memory_space=pltpu.VMEM)] * 3,
         out_specs=(pl.BlockSpec(memory_space=pltpu.VMEM), pl.BlockSpec(memory_space=pltpu.VMEM)),
-        scratch_shapes=_layer_scratch((q, cols), (q, cols), x.dtype),
+        scratch_shapes=[pltpu.VMEM((rows, cols), jnp.float32)]
+        + _layer_scratch((q, cols), (q, cols), jnp.float32),
         compiler_params=pltpu.CompilerParams(collective_id=1, has_side_effects=True),
-    )(x, bias)
+    )(inp, w, bias)
 
 
 def _layer_peers():
@@ -427,8 +437,7 @@
     chunk = d_model // (RING * RING)
     half = row_count // 2
     me = lax.axis_index("latent")
-    partial_pre = jnp.einsum("rld,ldf->rf", inputs, enc_weight, preferred_element_type=jnp.float32)
-    features, pre_q = layer_pre(partial_pre, enc_bias[None, :])
+    features, pre_q = layer_pre(inputs[:, 0, :], enc_weight[0], enc_bias[None, :])
     dec4 = dec_weight[0].reshape(lat_count, RING, RING, chunk)
     recon_a = jnp.einsum("rf,fabd->abdr", features[:half], dec4, preferred_element_type=jnp.float32)
     recon_b = jnp.einsum("rf,fabd->abdr", features[half:], dec4, preferred_element_type=jnp.float32)

time: 190 us -> 187 us (0.984)
  matrix products: 24.7 us -> 16.8 us
  Pallas kernels: 155 us -> 159 us
    dot_general x1 -> x0, matrix products: 7.85 us -> none  [local(): jnp.einsum('rld,ldf->rf', inputs, enc_weight, preferred_element_type=jnp....]
    pallas_call x1, Pallas kernels: 25.3 us -> 29.7 us  [layer_pre(): pl.pallas_call(_layer_pre_kernel, out_shape=(jax.ShapeDtypeStruct((rows,...]
where the time goes in v12:
time: 187 us; the launch traced here: 186 us
  Pallas kernels  159 us (85%)
  matrix products  16.8 us (9%)
  other arithmetic  5.17 us (3%)
  local copies, waits for them, and re-layouts  4.94 us (3%)
    pallas_call x1, Pallas kernels, latent_reduce(): pl.pallas_call(_reduce_kernel, out_shape=jax.ShapeDtypeStruct((2, h, c),...  37.1 us
    pallas_call x1, Pallas kernels, latent_reduce_mm(): pl.pallas_call(_reduce_mm_kernel, out_shape=jax.ShapeDtypeStruct((2, d, h...  35.7 us
    pallas_call x1, Pallas kernels, latent_gather(): pl.pallas_call(_gather_kernel, out_shape=(full, full), in_specs=[pl.Block...  31.9 us
    pallas_call x1, Pallas kernels, layer_pre(): pl.pallas_call(_layer_pre_kernel, out_shape=(jax.ShapeDtypeStruct((rows,...  29.7 us
    pallas_call x1, Pallas kernels, layer_grad(): pl.pallas_call(_layer_grad_kernel, out_shape=jax.ShapeDtypeStruct((cols,...  25 us
    dot_general x1, matrix products, local(): jnp.dot(dec_weight[0], error_all, preferred_element_type=jnp.float32)  7.73 us
    unnamed x2, matrix products  7.55 us

profile of v12, /device:TPU:1, one launch (start us, length us, event | category | flops | bytes accessed | tf_op | source)
XLA Modules:
  0.0 186.4 jit_solution(6021122705327558227)
XLA Ops:
  0.0 1.1 constant_dynamic-slice_fusion
  1.2 0.1 copy.26
  1.3 0.3 reshape.30
  1.6 1.3 broadcast_in_dim.2.bias
  2.9 29.7 %shard_map.82 = (bf16[512,768]{1,0:T(8,128)(2,1)}, f32[128,768]{1,0:T(8,128)}) custom-call(bf16[512,3584]{1,0:T(8,128)(2,1)} %bitcast.48, bf16[3584,768]{1,0:T(8,128)(2,1)} %bitcast.44, f32[1,768]{1,0:T(1,128)} %broadcast_in_dim.2.bias), custom_call_target="tpu_custom_call" | custom-call | tf_op jit(solution)/shard_map/pallas_call | solution.py:356
  32.5 0.0 slice-start.1
  32.6 5.2 %fusion = f32[256,3584]{0,1:S(1)} fusion(bf16[1,768,3584]{2,1,0:T(8,128)(2,1)} %param.12, bf16[512,768]{1,0:T(8,128)(2,1)} %get-tuple-element.9), kind=kOutput, calls=%fused_computation | convolution fusion | flops 1409286144 | bytes 9568256
  37.8 0.0 slice-done
  37.8 2.4 %fusion.2 = f32[256,3584]{0,1:S(1)} fusion(bf16[1,768,3584]{2,1,0:T(8,128)(2,1)S(1)} %bitcast.43, bf16[512,768]{1,0:T(8,128)(2,1)S(1)} %copy-done.1), kind=kOutput, calls=%fused_computation.2 | convolution fusion | flops 1409286144 | bytes 9568256
  40.2 2.3 %convert_bitcast_fusion = (bf16[4,4,224,256]{3,2,1,0:T(8,128)(2,1)}, bf16[4,4,224,256]{3,2,1,0:T(8,128)(2,1)}) fusion(f32[256,4,4,224]{0,3,2,1:T(8,128)S(1)} %bitcast.46, f32[256,4,4,224]{0,3,2,1:T(8,128)S(1)} %bitcast.47), kind=kLoop, calls=%fused_computation.11 | loop fusion | flops 1835008 | bytes 11010048 | tf_op jit(solution)/shard_map/convert_element_type | solution.py:444
  42.5 37.1 %shard_map.83 = f32[2,224,256]{2,1,0:T(8,128)} custom-call(bf16[4,4,224,256]{3,2,1,0:T(8,128)(2,1)} %get-tuple-element.14.xa, bf16[4,4,224,256]{3,2,1,0:T(8,128)(2,1)} %get-tuple-element.13.xb), custom_call_target="tpu_custom_call" | custom-call | tf_op jit(solution)/shard_map/pallas_call | solution.py:92
  79.5 0.1 constant_dynamic-slice_fusion.1
  79.6 1.8 fusion.23.e
  81.4 31.9 %shard_map.84 = (bf16[4,4,224,256]{3,2,1,0:T(8,128)(2,1)}, bf16[4,4,224,256]{3,2,1,0:T(8,128)(2,1)}) custom-call(bf16[2,224,256]{2,1,0:T(8,128)(2,1)} %fusion.23.e), custom_call_target="tpu_custom_call" | custom-call | tf_op jit(solution)/shard_map/pallas_call | solution.py:250
  113.4 0.0 copy-start.3
  113.4 0.0 copy-start.4
  113.4 7.7 %fusion.18.g = bf16[768,512]{1,0:T(8,128)(2,1)} fusion(bf16[3584,256]{1,0:T(8,128)(2,1)} %bitcast.52, bf16[3584,256]{1,0:T(8,128)(2,1)} %bitcast.51, bf16[1,768,3584]{2,1,0:T(8,128)(2,1)} %param.12), kind=kOutput, calls=%fused_computation.16 | convolution fusion | flops 2826305536 | bytes 9961472 | tf_op jit(solution)/shard_map/dot_general | solution.py:453
  121.1 0.9 copy.23
  122.1 1.5 fusion.9.margin_q
  123.6 25.0 %shard_map.85.v = bf16[768,512]{1,0:T(8,128)(2,1)} custom-call(bf16[768,512]{1,0:T(8,128)(2,1)} %fusion.18.g, f32[768,128]{1,0:T(8,128)} %bitcast.49, f32[768,128]{1,0:T(8,128)} %fusion.9.margin_q), custom_call_target="tpu_custom_call" | custom-call | tf_op jit(solution)/shard_map/pallas_call | solution.py:417
  148.6 35.7 %shard_map.86 = f32[2,224,256]{2,1,0:T(8,128)} custom-call(bf16[4,4,224,768]{3,2,1,0:T(8,128)(2,1)} %bitcast.45, bf16[768,512]{1,0:T(8,128)(2,1)} %shard_map.85.v), custom_call_target="tpu_custom_call" | custom-call | tf_op jit(solution)/shard_map/pallas_call | solution.py:181
  184.3 1.0 convert_bitcast_fusion.2
  185.3 0.2 copy.24
  185.6 0.8 reshape.29
  (13 shorter events, 0.0 us)
Async XLA Ops:
  0.0 79.5 %copy-start = (f32[1,3584]{1,0:T(1,128)S(1)}, f32[1,3584]{1,0:T(1,128)}, u32[]{:S(2)}) copy-start(f32[1,3584]{1,0:T(1,128)} %param.13) | copy-start | bytes 43012
  2.9 34.9 %slice-start = ((s8[5505024]{0:T(1024)(128)(4,1)}), s8[1310720]{0:T(1024)(128)(4,1)S(1)}, s32[]{:S(2)}) async-start(s8[5505024]{0:T(1024)(128)(4,1)} %bitcast.42), calls=%async_computation | async-start | bytes 2621440
  32.5 5.2 %slice-start.1 = ((s8[5505024]{0:T(1024)(128)(4,1)}), s8[4194304]{0:T(1024)(128)(4,1)S(1)}, s32[]{:S(2)}) async-start(s8[5505024]{0:T(1024)(128)(4,1)} %bitcast.42), calls=%async_computation.1 | async-start | bytes 8388608
  32.5 5.2 %copy-start.1 = (bf16[512,768]{1,0:T(8,128)(2,1)S(1)}, bf16[512,768]{1,0:T(8,128)(2,1)}, u32[]{:S(2)}) copy-start(bf16[512,768]{1,0:T(8,128)(2,1)} %get-tuple-element.9) | copy-start | bytes 2359300
  113.4 7.8 %copy-start.2 = (f32[128,768]{1,0:T(8,128)S(1)}, f32[128,768]{1,0:T(8,128)}, u32[]{:S(2)}) copy-start(f32[128,768]{1,0:T(8,128)} %get-tuple-element.12) | copy-start | bytes 1179652
  113.4 8.7 %copy-start.3 = (s32[1024]{0:T(1024)S(1)}, s32[1024]{0:T(1024)}, u32[]{:S(2)}) copy-start(s32[1024]{0:T(1024)} %param.15) | copy-start | bytes 12292
  113.4 8.7 %copy-start.4 = (s32[1024]{0:T(1024)S(1)}, s32[1024]{0:T(1024)}, u32[]{:S(2)}) copy-start(s32[1024]{0:T(1024)} %param.14) | copy-start | bytes 12292

commit v13 on v12

--- a/solution.py
+++ b/solution.py
@@ -384,22 +384,33 @@
     )
 
 
-def _layer_grad_kernel(g, pre_q, margin_q, out, r1, r2, send_sems, recv_sems):
+def _layer_grad_mm_kernel(ea, eb, w, pre_q, margin_q, out, gq, r1, r2, send_sems, recv_sems):
     me, peers = _layer_peers()
-    q = g.shape[1] // LAYERS
+    q = out.shape[1] // LAYERS
     lanes = lambda i: pl.ds(pl.multiple_of(i * q, q), q)
     _layer_greet(peers)
-    sent = []
+    per_half = ea.shape[1] // q
+
+    def first(i):
+        return _layer_copy(gq.at[i], r1.at[me], send_sems, recv_sems, 0, i, me)
+
+    for i in range(LAYERS):
+        src = ea if i < per_half else eb
+        lo = (i % per_half) * q
+        part = jnp.dot(w[...], src[:, lo:lo + q], preferred_element_type=jnp.float32)
+        gq[i] = part.astype(gq.dtype)
+
+        @pl.when(i != me)
+        def _():
+            first(i).start()
+
+    total = gq[me].astype(jnp.float32)
     for p in peers:
-        c = _layer_copy(g.at[:, lanes(p)], r1.at[me], send_sems, recv_sems, 0, p, me)
-        c.start()
-        sent.append(c)
-    total = g[:, lanes(me)].astype(jnp.float32)
-    for p in peers:
-        _layer_copy(g.at[:, lanes(p)], r1.at[p], send_sems, recv_sems, 0, p, p).wait_recv()
+        _layer_copy(gq.at[p], r1.at[p], send_sems, recv_sems, 0, p, p).wait_recv()
         total = total + r1[p].astype(jnp.float32)
     grad = jnp.where(pre_q[...] > 0, total - MARGIN * margin_q[...], 0.0)
     out[:, lanes(me)] = grad.astype(out.dtype)
+    sent = []
     for p in peers:
         c = _layer_copy(out.at[:, lanes(me)], r2.at[me], send_sems, recv_sems, 1, p, me)
         c.start()
@@ -409,24 +420,29 @@
         out[:, lanes(p)] = r2[p]
     for c in sent:
         c.wait_send()
-
-
-def layer_grad(g, pre_q, margin_q):
-    cols, rows = g.shape
+    for i in range(LAYERS):
+        @pl.when(i != me)
+        def _():
+            first(i).wait_send()
+
+
+def layer_grad_mm(ea, eb, w, pre_q, margin_q):
+    cols, rows = w.shape[0], ea.shape[1] + eb.shape[1]
     q = rows // LAYERS
     return pl.pallas_call(
-        _layer_grad_kernel,
+        _layer_grad_mm_kernel,
         out_shape=jax.ShapeDtypeStruct((cols, rows), jnp.bfloat16),
-        in_specs=[pl.BlockSpec(memory_space=pltpu.VMEM)] * 3,
+        in_specs=[pl.BlockSpec(memory_space=pltpu.VMEM)] * 5,
         out_specs=pl.BlockSpec(memory_space=pltpu.VMEM),
         scratch_shapes=[
+            pltpu.VMEM((LAYERS, cols, q), jnp.bfloat16),
             pltpu.VMEM((LAYERS, cols, q), jnp.bfloat16),
             pltpu.VMEM((LAYERS, cols, q), jnp.bfloat16),
             pltpu.SemaphoreType.DMA((2, LAYERS)),
             pltpu.SemaphoreType.DMA((2, LAYERS)),
         ],
         compiler_params=pltpu.CompilerParams(collective_id=2, has_side_effects=True),
-    )(g, pre_q, margin_q)
+    )(ea, eb, w, pre_q, margin_q)
 
 
 def local(inputs, clean_acts, enc_weight, enc_bias, dec_weight, dec_bias, pairing, targets):
@@ -447,10 +463,6 @@
     clean_t = jnp.swapaxes(clean_part.reshape(2, half, chunk), 1, 2).astype(jnp.float32)
     recon_error = (recon_sum + bias_part[:, None] - clean_t).astype(jnp.bfloat16)
     error_a, error_b = latent_gather(recon_error, 4)
-    error_all = jnp.concatenate(
-        [error_a.reshape(d_model, half), error_b.reshape(d_model, half)], axis=1
-    )
-    partial_grad_t = jnp.dot(dec_weight[0], error_all, preferred_element_type=jnp.float32)
     quarter = row_count // LAYERS
     row_ids = (
         lax.axis_index("row") * row_count
@@ -465,7 +477,9 @@
     ).astype(jnp.bfloat16)
     target_hot_t = (latent_ids[:, None] == targets[None, :]).astype(jnp.bfloat16)
     margin_q = jnp.dot(target_hot_t, pair_table_t, preferred_element_type=jnp.float32)
-    pre_grad_t = layer_grad(partial_grad_t.astype(jnp.bfloat16), pre_q.T, margin_q)
+    pre_grad_t = layer_grad_mm(
+        error_a.reshape(d_model, half), error_b.reshape(d_model, half), dec_weight[0], pre_q.T, margin_q
+    )
     enc4 = enc_weight[0].reshape(RING, RING, chunk, lat_count)
     total = latent_reduce_mm(enc4, pre_grad_t, 5)
     return jnp.swapaxes(total.astype(jnp.bfloat16), 1, 2).reshape(row_count, 1, chunk)

time: 187 us -> 190 us (1.016)
  Pallas kernels: 159 us -> 171 us
  matrix products: 16.8 us -> 9.04 us
    pallas_call x1, Pallas kernels: 25 us -> 34.7 us  [layer_grad_mm(): pl.pallas_call(_layer_grad_mm_kernel, out_shape=jax.ShapeDtypeStruct((col...]
    dot_general x1 -> x0, matrix products: 7.73 us -> none  [local(): jnp.dot(dec_weight[0], error_all, preferred_element_type=jnp.float32)]
where the time goes in v13:
time: 190 us
  Pallas kernels  171 us (90%)
  matrix products  9.04 us (5%)
  other arithmetic  5.17 us (3%)
  local copies, waits for them, and re-layouts  4.93 us (3%)
    pallas_call x1, Pallas kernels, latent_reduce_mm(): pl.pallas_call(_reduce_mm_kernel, out_shape=jax.ShapeDtypeStruct((2, d, h...  37.3 us
    pallas_call x1, Pallas kernels, latent_reduce(): pl.pallas_call(_reduce_kernel, out_shape=jax.ShapeDtypeStruct((2, h, c),...  37.1 us
    pallas_call x1, Pallas kernels, layer_grad_mm(): pl.pallas_call(_layer_grad_mm_kernel, out_shape=jax.ShapeDtypeStruct((col...  34.7 us
    pallas_call x1, Pallas kernels, latent_gather(): pl.pallas_call(_gather_kernel, out_shape=(full, full), in_specs=[pl.Block...  31.9 us
    pallas_call x1, Pallas kernels, layer_pre(): pl.pallas_call(_layer_pre_kernel, out_shape=(jax.ShapeDtypeStruct((rows,...  29.7 us
    unnamed x2, matrix products  7.55 us

profile of v13, /device:TPU:1, one launch (start us, length us, event | category | flops | bytes accessed | tf_op | source)
XLA Modules:
  0.0 190.0 jit_solution(11203463415526328272)
XLA Ops:
  0.0 0.0 copy-start
  0.0 1.1 constant_dynamic-slice_fusion
  1.2 0.1 copy.22
  1.3 0.3 reshape.30
  1.6 1.3 broadcast_in_dim.2.bias
  2.9 29.7 %shard_map.82 = (bf16[512,768]{1,0:T(8,128)(2,1)}, f32[128,768]{1,0:T(8,128)}) custom-call(bf16[512,3584]{1,0:T(8,128)(2,1)} %bitcast.41, bf16[3584,768]{1,0:T(8,128)(2,1)} %bitcast.37, f32[1,768]{1,0:T(1,128)} %broadcast_in_dim.2.bias), custom_call_target="tpu_custom_call" | custom-call | tf_op jit(solution)/shard_map/pallas_call | solution.py:356
  32.5 0.0 slice-start.1
  32.6 0.0 copy-start.1
  32.6 5.2 %fusion.5 = f32[256,3584]{0,1:S(1)} fusion(bf16[512,768]{1,0:T(8,128)(2,1)} %get-tuple-element.9, bf16[1,768,3584]{2,1,0:T(8,128)(2,1)} %param.12), kind=kOutput, calls=%fused_computation.10 | convolution fusion | flops 1409286144 | bytes 9568256
  37.8 0.0 slice-done
  37.8 2.4 %fusion.7 = f32[256,3584]{0,1:S(1)} fusion(bf16[512,768]{1,0:T(8,128)(2,1)S(1)} %copy-done.1, bf16[1,768,3584]{2,1,0:T(8,128)(2,1)S(1)} %bitcast.36), kind=kOutput, calls=%fused_computation.12 | convolution fusion | flops 1409286144 | bytes 9568256
  40.2 2.3 %convert_bitcast_fusion = (bf16[4,4,224,256]{3,2,1,0:T(8,128)(2,1)}, bf16[4,4,224,256]{3,2,1,0:T(8,128)(2,1)}) fusion(f32[256,4,4,224]{0,3,2,1:T(8,128)S(1)} %bitcast.39, f32[256,4,4,224]{0,3,2,1:T(8,128)S(1)} %bitcast.40), kind=kLoop, calls=%fused_computation.2 | loop fusion | flops 1835008 | bytes 11010048 | tf_op jit(solution)/shard_map/convert_element_type | solution.py:460
  42.5 37.1 %shard_map.83 = f32[2,224,256]{2,1,0:T(8,128)} custom-call(bf16[4,4,224,256]{3,2,1,0:T(8,128)(2,1)} %get-tuple-element.14.xa, bf16[4,4,224,256]{3,2,1,0:T(8,128)(2,1)} %get-tuple-element.13.xb), custom_call_target="tpu_custom_call" | custom-call | tf_op jit(solution)/shard_map/pallas_call | solution.py:92
  79.6 0.0 copy-done
  79.6 0.1 constant_dynamic-slice_fusion.1
  79.7 1.8 fusion.4.e
  81.5 31.9 %shard_map.84 = (bf16[4,4,224,256]{3,2,1,0:T(8,128)(2,1)}, bf16[4,4,224,256]{3,2,1,0:T(8,128)(2,1)}) custom-call(bf16[2,224,256]{2,1,0:T(8,128)(2,1)} %fusion.4.e), custom_call_target="tpu_custom_call" | custom-call | tf_op jit(solution)/shard_map/pallas_call | solution.py:250
  113.4 0.9 copy.20
  114.4 1.5 fusion.margin_q
  115.9 34.7 %shard_map.85.v = bf16[768,512]{1,0:T(8,128)(2,1)} custom-call(bf16[3584,256]{1,0:T(8,128)(2,1)} %bitcast.42, bf16[3584,256]{1,0:T(8,128)(2,1)} %bitcast.43, bf16[768,3584]{1,0:T(8,128)(2,1)} %bitcast.34, f32[768,128]{1,0:T(8,128)} %bitcast.44, f32[768,128]{1,0:T(8,128)} %fusion.margin_q), custom_call_target="tpu_custom_call" | custom-call | tf_op jit(solution)/shard_map/pallas_call | solution.py:432
  150.6 37.3 %shard_map.86 = f32[2,224,256]{2,1,0:T(8,128)} custom-call(bf16[4,4,224,768]{3,2,1,0:T(8,128)(2,1)} %bitcast.38, bf16[768,512]{1,0:T(8,128)(2,1)} %shard_map.85.v), custom_call_target="tpu_custom_call" | custom-call | tf_op jit(solution)/shard_map/pallas_call | solution.py:181
  187.9 1.0 convert_bitcast_fusion.2
  188.9 0.2 copy.21
  189.2 0.8 reshape.29
  (12 shorter events, 0.0 us)
Async XLA Ops:
  0.0 79.6 %copy-start = (f32[1,3584]{1,0:T(1,128)S(1)}, f32[1,3584]{1,0:T(1,128)}, u32[]{:S(2)}) copy-start(f32[1,3584]{1,0:T(1,128)} %param.13) | copy-start | bytes 43012
  2.9 34.9 %slice-start = ((s8[5505024]{0:T(1024)(128)(4,1)}), s8[1310720]{0:T(1024)(128)(4,1)S(1)}, s32[]{:S(2)}) async-start(s8[5505024]{0:T(1024)(128)(4,1)} %bitcast.35), calls=%async_computation | async-start | bytes 2621440
  32.5 5.2 %slice-start.1 = ((s8[5505024]{0:T(1024)(128)(4,1)}), s8[4194304]{0:T(1024)(128)(4,1)S(1)}, s32[]{:S(2)}) async-start(s8[5505024]{0:T(1024)(128)(4,1)} %bitcast.35), calls=%async_computation.1 | async-start | bytes 8388608
  32.6 5.2 %copy-start.1 = (bf16[512,768]{1,0:T(8,128)(2,1)S(1)}, bf16[512,768]{1,0:T(8,128)(2,1)}, u32[]{:S(2)}) copy-start(bf16[512,768]{1,0:T(8,128)(2,1)} %get-tuple-element.9) | copy-start | bytes 2359300
  42.5 71.0 %copy-start.2 = (f32[128,768]{1,0:T(8,128)S(1)}, f32[128,768]{1,0:T(8,128)}, u32[]{:S(2)}) copy-start(f32[128,768]{1,0:T(8,128)} %get-tuple-element.12) | copy-start | bytes 1179652
  42.5 71.9 %copy-start.3 = (s32[1024]{0:T(1024)S(1)}, s32[1024]{0:T(1024)}, u32[]{:S(2)}) copy-start(s32[1024]{0:T(1024)} %param.15) | copy-start | bytes 12292
  42.5 71.9 %copy-start.4 = (s32[1024]{0:T(1024)S(1)}, s32[1024]{0:T(1024)}, u32[]{:S(2)}) copy-start(s32[1024]{0:T(1024)} %param.14) | copy-start | bytes 12292

commit v14 on v12

--- a/solution.py
+++ b/solution.py
@@ -31,7 +31,10 @@
     )
 
 
-def _reduce_kernel(xa, xb, out, r1a, r1b, s1a, s1b, r2a, r2b, send_sems, recv_sems):
+def _reduce_kernel(x, out, r1a, r1b, s1a, s1b, r2a, r2b, send_sems, recv_sems):
+    h = x.shape[-1] // 2
+    xa = x.at[:, :, :, pl.ds(0, h)]
+    xb = x.at[:, :, :, pl.ds(h, h)]
     a, b = _latent_coords()
     _greet(a, b)
     peers_z = [(b + k) % RING for k in range(1, RING)]
@@ -86,13 +89,14 @@
         c.wait_send()
 
 
-def latent_reduce(xa, xb, collective_id):
-    n, _, h, c = xa.shape
-    dt = xa.dtype
+def latent_reduce(x, collective_id):
+    n, _, h, c = x.shape
+    c = c // 2
+    dt = x.dtype
     return pl.pallas_call(
         _reduce_kernel,
         out_shape=jax.ShapeDtypeStruct((2, h, c), jnp.float32),
-        in_specs=[pl.BlockSpec(memory_space=pltpu.VMEM)] * 2,
+        in_specs=[pl.BlockSpec(memory_space=pltpu.VMEM)],
         out_specs=pl.BlockSpec(memory_space=pltpu.VMEM),
         scratch_shapes=[
             pltpu.VMEM((n, n, h, c), dt),
@@ -105,7 +109,7 @@
             pltpu.SemaphoreType.DMA((4, n)),
         ],
         compiler_params=pltpu.CompilerParams(collective_id=collective_id, has_side_effects=True),
-    )(xa, xb)
+    )(x)
 
 
 def _reduce_mm_kernel(w, v, out, xa, xb, r1a, r1b, s1a, s1b, r2a, r2b, send_sems, recv_sems):
@@ -437,11 +441,10 @@
     chunk = d_model // (RING * RING)
     half = row_count // 2
     me = lax.axis_index("latent")
-    features, pre_q = layer_pre(inputs[:, 0, :], enc_weight[0], enc_bias[None, :])
+    features, pre_q = layer_pre(inputs[:, 0, :], enc_weight[0], enc_bias.reshape(1, lat_count))
     dec4 = dec_weight[0].reshape(lat_count, RING, RING, chunk)
-    recon_a = jnp.einsum("rf,fabd->abdr", features[:half], dec4, preferred_element_type=jnp.float32)
-    recon_b = jnp.einsum("rf,fabd->abdr", features[half:], dec4, preferred_element_type=jnp.float32)
-    recon_sum = latent_reduce(recon_a.astype(jnp.bfloat16), recon_b.astype(jnp.bfloat16), 3)
+    recon_part = jnp.einsum("rf,fabd->abdr", features, dec4, preferred_element_type=jnp.float32)
+    recon_sum = latent_reduce(recon_part.astype(jnp.bfloat16), 3)
     bias_part = lax.dynamic_slice_in_dim(dec_bias[0], me * chunk, chunk)
     clean_part = lax.dynamic_slice_in_dim(clean_acts[:, 0, :], me * chunk, chunk, axis=1)
     clean_t = jnp.swapaxes(clean_part.reshape(2, half, chunk), 1, 2).astype(jnp.float32)

time: 187 us -> 184 us (0.984)
  matrix products: 16.8 us -> 14.5 us
    pallas_call x1, Pallas kernels: 31.9 us -> 34 us  [latent_gather(): pl.pallas_call(_gather_kernel, out_shape=(full, full), in_specs=[pl.Block...]
    unnamed x2 -> x1, matrix products: 7.55 us -> 5.47 us
    pallas_call x1, Pallas kernels: 25 us -> 22.9 us  [layer_grad(): pl.pallas_call(_layer_grad_kernel, out_shape=jax.ShapeDtypeStruct((cols,...]
where the time goes in v14:
time: 184 us
  Pallas kernels  159 us (86%)
  matrix products  14.5 us (8%)
  other arithmetic  5.17 us (3%)
  local copies, waits for them, and re-layouts  4.92 us (3%)
    pallas_call x1, Pallas kernels, latent_reduce(): pl.pallas_call(_reduce_kernel, out_shape=jax.ShapeDtypeStruct((2, h, c),...  37.1 us
    pallas_call x1, Pallas kernels, latent_reduce_mm(): pl.pallas_call(_reduce_mm_kernel, out_shape=jax.ShapeDtypeStruct((2, d, h...  35.7 us
    pallas_call x1, Pallas kernels, latent_gather(): pl.pallas_call(_gather_kernel, out_shape=(full, full), in_specs=[pl.Block...  34 us
    pallas_call x1, Pallas kernels, layer_pre(): pl.pallas_call(_layer_pre_kernel, out_shape=(jax.ShapeDtypeStruct((rows,...  29.6 us
    pallas_call x1, Pallas kernels, layer_grad(): pl.pallas_call(_layer_grad_kernel, out_shape=jax.ShapeDtypeStruct((cols,...  22.9 us
    dot_general x1, matrix products, local(): jnp.dot(dec_weight[0], error_all, preferred_element_type=jnp.float32)  7.56 us
    unnamed x1, matrix products  5.47 us

profile of v14, /device:TPU:1, one launch (start us, length us, event | category | flops | bytes accessed | tf_op | source)
XLA Modules:
  0.0 184.0 jit_solution(16828597505513637169)
XLA Ops:
  0.0 0.0 copy-start
  0.0 1.1 constant_dynamic-slice_fusion
  1.2 0.1 copy.25
  1.3 0.3 reshape.34
  1.6 1.3 reshape.30.bias
  2.9 29.6 %shard_map.82 = (bf16[512,768]{1,0:T(8,128)(2,1)}, f32[128,768]{1,0:T(8,128)}) custom-call(bf16[512,3584]{1,0:T(8,128)(2,1)} %bitcast.39, bf16[3584,768]{1,0:T(8,128)(2,1)} %bitcast.36, f32[1,768]{1,0:T(1,128)} %reshape.30.bias), custom_call_target="tpu_custom_call" | custom-call | tf_op jit(solution)/shard_map/pallas_call | solution.py:360
  32.4 5.5 %fusion = f32[512,3584]{0,1:S(1)} fusion(bf16[512,768]{1,0:T(8,128)(2,1)} %get-tuple-element.9, bf16[1,768,3584]{2,1,0:T(8,128)(2,1)} %param.12), kind=kOutput, calls=%fused_computation | convolution fusion | flops 2818572288 | bytes 13631488
  37.9 2.3 %convert_bitcast_fusion.x = bf16[4,4,224,512]{3,2,1,0:T(8,128)(2,1)} fusion(f32[512,4,4,224]{0,3,2,1:T(8,128)S(1)} %bitcast.38), kind=kLoop, calls=%fused_computation.7 | loop fusion | flops 1835008 | bytes 11010048 | tf_op jit(solution)/shard_map/convert_element_type | solution.py:447
  40.2 37.1 %shard_map.83 = f32[2,224,256]{2,1,0:T(8,128)} custom-call(bf16[4,4,224,512]{3,2,1,0:T(8,128)(2,1)} %convert_bitcast_fusion.x), custom_call_target="tpu_custom_call" | custom-call | tf_op jit(solution)/shard_map/pallas_call | solution.py:96
  77.3 0.0 copy-done
  77.3 0.1 constant_dynamic-slice_fusion.1
  77.4 1.8 fusion.21.e
  79.2 34.0 %shard_map.84 = (bf16[4,4,224,256]{3,2,1,0:T(8,128)(2,1)}, bf16[4,4,224,256]{3,2,1,0:T(8,128)(2,1)}) custom-call(bf16[2,224,256]{2,1,0:T(8,128)(2,1)} %fusion.21.e), custom_call_target="tpu_custom_call" | custom-call | tf_op jit(solution)/shard_map/pallas_call | solution.py:254
  113.2 0.0 copy-start.1
  113.2 0.0 copy-start.2
  113.2 0.0 copy-start.3
  113.2 7.6 %fusion.16.g = bf16[768,512]{1,0:T(8,128)(2,1)} fusion(bf16[3584,256]{1,0:T(8,128)(2,1)} %bitcast.43, bf16[3584,256]{1,0:T(8,128)(2,1)} %bitcast.42, bf16[1,768,3584]{2,1,0:T(8,128)(2,1)} %param.12), kind=kOutput, calls=%fused_computation.13 | convolution fusion | flops 2826305536 | bytes 9961472 | tf_op jit(solution)/shard_map/dot_general | solution.py:456
  120.8 0.9 copy.22
  121.7 1.5 fusion.7.margin_q
  123.2 22.9 %shard_map.85.v = bf16[768,512]{1,0:T(8,128)(2,1)} custom-call(bf16[768,512]{1,0:T(8,128)(2,1)} %fusion.16.g, f32[768,128]{1,0:T(8,128)} %bitcast.40, f32[768,128]{1,0:T(8,128)} %fusion.7.margin_q), custom_call_target="tpu_custom_call" | custom-call | tf_op jit(solution)/shard_map/pallas_call | solution.py:421
  146.2 35.7 %shard_map.86 = f32[2,224,256]{2,1,0:T(8,128)} custom-call(bf16[4,4,224,768]{3,2,1,0:T(8,128)(2,1)} %bitcast.37, bf16[768,512]{1,0:T(8,128)(2,1)} %shard_map.85.v), custom_call_target="tpu_custom_call" | custom-call | tf_op jit(solution)/shard_map/pallas_call | solution.py:185
  181.9 1.0 convert_bitcast_fusion.1
  182.9 0.2 copy.23
  183.2 0.8 reshape.33
  (5 shorter events, 0.0 us)
Async XLA Ops:
  0.0 77.3 %copy-start = (f32[1,3584]{1,0:T(1,128)S(1)}, f32[1,3584]{1,0:T(1,128)}, u32[]{:S(2)}) copy-start(f32[1,3584]{1,0:T(1,128)} %param.13) | copy-start | bytes 43012
  113.2 7.6 %copy-start.1 = (f32[128,768]{1,0:T(8,128)S(1)}, f32[128,768]{1,0:T(8,128)}, u32[]{:S(2)}) copy-start(f32[128,768]{1,0:T(8,128)} %get-tuple-element.12) | copy-start | bytes 1179652
  113.2 8.5 %copy-start.2 = (s32[1024]{0:T(1024)S(1)}, s32[1024]{0:T(1024)}, u32[]{:S(2)}) copy-start(s32[1024]{0:T(1024)} %param.15) | copy-start | bytes 12292
  113.2 8.5 %copy-start.3 = (s32[1024]{0:T(1024)S(1)}, s32[1024]{0:T(1024)}, u32[]{:S(2)}) copy-start(s32[1024]{0:T(1024)} %param.14) | copy-start | bytes 12292

commit v15 on v14

--- a/solution.py
+++ b/solution.py
@@ -443,8 +443,8 @@
     me = lax.axis_index("latent")
     features, pre_q = layer_pre(inputs[:, 0, :], enc_weight[0], enc_bias.reshape(1, lat_count))
     dec4 = dec_weight[0].reshape(lat_count, RING, RING, chunk)
-    recon_part = jnp.einsum("rf,fabd->abdr", features, dec4, preferred_element_type=jnp.float32)
-    recon_sum = latent_reduce(recon_part.astype(jnp.bfloat16), 3)
+    recon_part = jnp.einsum("rf,fabd->abdr", features, dec4, preferred_element_type=jnp.bfloat16)
+    recon_sum = latent_reduce(recon_part, 3)
     bias_part = lax.dynamic_slice_in_dim(dec_bias[0], me * chunk, chunk)
     clean_part = lax.dynamic_slice_in_dim(clean_acts[:, 0, :], me * chunk, chunk, axis=1)
     clean_t = jnp.swapaxes(clean_part.reshape(2, half, chunk), 1, 2).astype(jnp.float32)

time: 184 us -> 184 us (level)
  other arithmetic: 5.17 us -> 2.87 us
  matrix products: 14.5 us -> 16.7 us
    convert_element_type x1 -> x0, other arithmetic: 2.3 us -> none  [local(): recon_sum = latent_reduce(recon_part.astype(jnp.bfloat16), 3)]
    unnamed x1, matrix products: 5.47 us -> 7.67 us
where the time goes in v15:
time: 184 us
  Pallas kernels  159 us (86%)
  matrix products  16.7 us (9%)
  local copies, waits for them, and re-layouts  4.92 us (3%)
  other arithmetic  2.87 us (2%)
    pallas_call x1, Pallas kernels, latent_reduce(): pl.pallas_call(_reduce_kernel, out_shape=jax.ShapeDtypeStruct((2, h, c),...  37.1 us
    pallas_call x1, Pallas kernels, latent_reduce_mm(): pl.pallas_call(_reduce_mm_kernel, out_shape=jax.ShapeDtypeStruct((2, d, h...  35.9 us
    pallas_call x1, Pallas kernels, latent_gather(): pl.pallas_call(_gather_kernel, out_shape=(full, full), in_specs=[pl.Block...  34 us
    pallas_call x1, Pallas kernels, layer_pre(): pl.pallas_call(_layer_pre_kernel, out_shape=(jax.ShapeDtypeStruct((rows,...  29.6 us
    pallas_call x1, Pallas kernels, layer_grad(): pl.pallas_call(_layer_grad_kernel, out_shape=jax.ShapeDtypeStruct((cols,...  22.9 us
    unnamed x1, matrix products  7.67 us
    dot_general x1, matrix products, local(): jnp.dot(dec_weight[0], error_all, preferred_element_type=jnp.float32)  7.56 us

profile of v15, /device:TPU:1, one launch (start us, length us, event | category | flops | bytes accessed | tf_op | source)
XLA Modules:
  0.0 184.1 jit_solution(3401284733221990696)
XLA Ops:
  0.0 0.0 copy-start
  0.0 1.1 constant_dynamic-slice_fusion
  1.2 0.1 copy.25
  1.3 0.3 reshape.34
  1.6 1.3 reshape.30.bias
  2.9 29.6 %shard_map.82 = (bf16[512,768]{1,0:T(8,128)(2,1)}, f32[128,768]{1,0:T(8,128)}) custom-call(bf16[512,3584]{1,0:T(8,128)(2,1)} %bitcast.38, bf16[3584,768]{1,0:T(8,128)(2,1)} %bitcast.36, f32[1,768]{1,0:T(1,128)} %reshape.30.bias), custom_call_target="tpu_custom_call" | custom-call | tf_op jit(solution)/shard_map/pallas_call | solution.py:360
  32.5 7.7 %fusion = bf16[512,3584]{0,1} fusion(bf16[512,768]{1,0:T(8,128)(2,1)} %get-tuple-element.9, bf16[1,768,3584]{2,1,0:T(8,128)(2,1)} %param.12), kind=kOutput, calls=%fused_computation | convolution fusion | flops 2818572288 | bytes 9961472
  40.1 37.1 %shard_map.83 = f32[2,224,256]{2,1,0:T(8,128)} custom-call(bf16[4,4,224,512]{3,2,1,0:T(8,128)(2,1)} %bitcast.39), custom_call_target="tpu_custom_call" | custom-call | tf_op jit(solution)/shard_map/pallas_call | solution.py:96
  77.2 0.0 copy-done
  77.2 0.1 constant_dynamic-slice_fusion.1
  77.3 1.8 fusion.21.e
  79.1 34.0 %shard_map.84 = (bf16[4,4,224,256]{3,2,1,0:T(8,128)(2,1)}, bf16[4,4,224,256]{3,2,1,0:T(8,128)(2,1)}) custom-call(bf16[2,224,256]{2,1,0:T(8,128)(2,1)} %fusion.21.e), custom_call_target="tpu_custom_call" | custom-call | tf_op jit(solution)/shard_map/pallas_call | solution.py:254
  113.1 0.0 copy-start.1
  113.1 0.0 copy-start.2
  113.1 0.0 copy-start.3
  113.2 7.6 %fusion.16.g = bf16[768,512]{1,0:T(8,128)(2,1)} fusion(bf16[3584,256]{1,0:T(8,128)(2,1)} %bitcast.43, bf16[3584,256]{1,0:T(8,128)(2,1)} %bitcast.42, bf16[1,768,3584]{2,1,0:T(8,128)(2,1)} %param.12), kind=kOutput, calls=%fused_computation.12 | convolution fusion | flops 2826305536 | bytes 9961472 | tf_op jit(solution)/shard_map/dot_general | solution.py:456
  120.7 0.9 copy.22
  121.6 0.0 copy-done.2
  121.7 1.5 fusion.7.margin_q
  123.2 22.9 %shard_map.85.v = bf16[768,512]{1,0:T(8,128)(2,1)} custom-call(bf16[768,512]{1,0:T(8,128)(2,1)} %fusion.16.g, f32[768,128]{1,0:T(8,128)} %bitcast.40, f32[768,128]{1,0:T(8,128)} %fusion.7.margin_q), custom_call_target="tpu_custom_call" | custom-call | tf_op jit(solution)/shard_map/pallas_call | solution.py:421
  146.1 35.9 %shard_map.86 = f32[2,224,256]{2,1,0:T(8,128)} custom-call(bf16[4,4,224,768]{3,2,1,0:T(8,128)(2,1)} %bitcast.37, bf16[768,512]{1,0:T(8,128)(2,1)} %shard_map.85.v), custom_call_target="tpu_custom_call" | custom-call | tf_op jit(solution)/shard_map/pallas_call | solution.py:185
  182.0 1.0 convert_bitcast_fusion
  183.1 0.2 copy.23
  183.3 0.8 reshape.33
  (4 shorter events, 0.0 us)
Async XLA Ops:
  0.0 77.2 %copy-start = (f32[1,3584]{1,0:T(1,128)S(1)}, f32[1,3584]{1,0:T(1,128)}, u32[]{:S(2)}) copy-start(f32[1,3584]{1,0:T(1,128)} %param.13) | copy-start | bytes 43012
  113.1 7.6 %copy-start.1 = (f32[128,768]{1,0:T(8,128)S(1)}, f32[128,768]{1,0:T(8,128)}, u32[]{:S(2)}) copy-start(f32[128,768]{1,0:T(8,128)} %get-tuple-element.12) | copy-start | bytes 1179652
  113.1 8.5 %copy-start.2 = (s32[1024]{0:T(1024)S(1)}, s32[1024]{0:T(1024)}, u32[]{:S(2)}) copy-start(s32[1024]{0:T(1024)} %param.15) | copy-start | bytes 12292
  113.1 8.5 %copy-start.3 = (s32[1024]{0:T(1024)S(1)}, s32[1024]{0:T(1024)}, u32[]{:S(2)}) copy-start(s32[1024]{0:T(1024)} %param.14) | copy-start | bytes 12292

commit v16 on v14

--- a/solution.py
+++ b/solution.py
@@ -330,7 +330,7 @@
 
 def _layer_pre_kernel(inp, w, bias, feats, pre_q, x, *scratch):
     def finish(total):
-        pre = total + bias[...]
+        pre = total + bias[...].reshape(1, -1)
         pre_q[...] = pre
         return jnp.maximum(pre, 0.0).astype(feats.dtype)
 
@@ -441,7 +441,7 @@
     chunk = d_model // (RING * RING)
     half = row_count // 2
     me = lax.axis_index("latent")
-    features, pre_q = layer_pre(inputs[:, 0, :], enc_weight[0], enc_bias.reshape(1, lat_count))
+    features, pre_q = layer_pre(inputs[:, 0, :], enc_weight[0], enc_bias)
     dec4 = dec_weight[0].reshape(lat_count, RING, RING, chunk)
     recon_part = jnp.einsum("rf,fabd->abdr", features, dec4, preferred_element_type=jnp.float32)
     recon_sum = latent_reduce(recon_part.astype(jnp.bfloat16), 3)

time: 184 us -> 183 us (level)
  no operation moved by 1% of the time
where the time goes in v16:
time: 183 us
  Pallas kernels  159 us (87%)
  matrix products  14.5 us (8%)
  other arithmetic  5.17 us (3%)
  local copies, waits for them, and re-layouts  3.65 us (2%)
    pallas_call x1, Pallas kernels, latent_reduce(): pl.pallas_call(_reduce_kernel, out_shape=jax.ShapeDtypeStruct((2, h, c),...  37.1 us
    pallas_call x1, Pallas kernels, latent_reduce_mm(): pl.pallas_call(_reduce_mm_kernel, out_shape=jax.ShapeDtypeStruct((2, d, h...  35.7 us
    pallas_call x1, Pallas kernels, latent_gather(): pl.pallas_call(_gather_kernel, out_shape=(full, full), in_specs=[pl.Block...  34 us
    pallas_call x1, Pallas kernels, layer_pre(): pl.pallas_call(_layer_pre_kernel, out_shape=(jax.ShapeDtypeStruct((rows,...  29.6 us
    pallas_call x1, Pallas kernels, layer_grad(): pl.pallas_call(_layer_grad_kernel, out_shape=jax.ShapeDtypeStruct((cols,...  22.9 us
    dot_general x1, matrix products, local(): jnp.dot(dec_weight[0], error_all, preferred_element_type=jnp.float32)  7.56 us
    unnamed x1, matrix products  5.47 us

profile of v16, /device:TPU:1, one launch (start us, length us, event | category | flops | bytes accessed | tf_op | source)
XLA Modules:
  0.0 182.8 jit_solution(2719443672170107614)
XLA Ops:
  0.0 0.0 copy-start
  0.0 1.1 constant_dynamic-slice_fusion
  1.2 0.1 copy.25
  1.3 0.3 reshape.30
  1.6 29.6 %shard_map.82 = (bf16[512,768]{1,0:T(8,128)(2,1)}, f32[128,768]{1,0:T(8,128)}) custom-call(bf16[512,3584]{1,0:T(8,128)(2,1)} %bitcast.39, bf16[3584,768]{1,0:T(8,128)(2,1)} %bitcast.36, f32[768]{0:T(1024)} %bias.1), custom_call_target="tpu_custom_call" | custom-call | tf_op jit(solution)/shard_map/pallas_call | solution.py:360
  31.2 5.5 %fusion = f32[512,3584]{0,1:S(1)} fusion(bf16[512,768]{1,0:T(8,128)(2,1)} %get-tuple-element.9, bf16[1,768,3584]{2,1,0:T(8,128)(2,1)} %param.12), kind=kOutput, calls=%fused_computation | convolution fusion | flops 2818572288 | bytes 13631488
  36.7 2.3 %convert_bitcast_fusion.x = bf16[4,4,224,512]{3,2,1,0:T(8,128)(2,1)} fusion(f32[512,4,4,224]{0,3,2,1:T(8,128)S(1)} %bitcast.38), kind=kLoop, calls=%fused_computation.7 | loop fusion | flops 1835008 | bytes 11010048 | tf_op jit(solution)/shard_map/convert_element_type | solution.py:447
  39.0 37.1 %shard_map.83 = f32[2,224,256]{2,1,0:T(8,128)} custom-call(bf16[4,4,224,512]{3,2,1,0:T(8,128)(2,1)} %convert_bitcast_fusion.x), custom_call_target="tpu_custom_call" | custom-call | tf_op jit(solution)/shard_map/pallas_call | solution.py:96
  76.1 0.0 copy-done
  76.1 0.1 constant_dynamic-slice_fusion.1
  76.2 1.8 fusion.21.e
  78.0 34.0 %shard_map.84 = (bf16[4,4,224,256]{3,2,1,0:T(8,128)(2,1)}, bf16[4,4,224,256]{3,2,1,0:T(8,128)(2,1)}) custom-call(bf16[2,224,256]{2,1,0:T(8,128)(2,1)} %fusion.21.e), custom_call_target="tpu_custom_call" | custom-call | tf_op jit(solution)/shard_map/pallas_call | solution.py:254
  112.0 0.0 copy-start.1
  112.0 0.0 copy-start.2
  112.0 0.0 copy-start.3
  112.0 7.6 %fusion.16.g = bf16[768,512]{1,0:T(8,128)(2,1)} fusion(bf16[3584,256]{1,0:T(8,128)(2,1)} %bitcast.43, bf16[3584,256]{1,0:T(8,128)(2,1)} %bitcast.42, bf16[1,768,3584]{2,1,0:T(8,128)(2,1)} %param.12), kind=kOutput, calls=%fused_computation.13 | convolution fusion | flops 2826305536 | bytes 9961472 | tf_op jit(solution)/shard_map/dot_general | solution.py:456
  119.6 0.0 copy-done.1
  119.6 0.9 copy.22
  120.5 1.5 fusion.7.margin_q
  122.0 22.9 %shard_map.85.v = bf16[768,512]{1,0:T(8,128)(2,1)} custom-call(bf16[768,512]{1,0:T(8,128)(2,1)} %fusion.16.g, f32[768,128]{1,0:T(8,128)} %bitcast.40, f32[768,128]{1,0:T(8,128)} %fusion.7.margin_q), custom_call_target="tpu_custom_call" | custom-call | tf_op jit(solution)/shard_map/pallas_call | solution.py:421
  145.0 35.7 %shard_map.86 = f32[2,224,256]{2,1,0:T(8,128)} custom-call(bf16[4,4,224,768]{3,2,1,0:T(8,128)(2,1)} %bitcast.37, bf16[768,512]{1,0:T(8,128)(2,1)} %shard_map.85.v), custom_call_target="tpu_custom_call" | custom-call | tf_op jit(solution)/shard_map/pallas_call | solution.py:185
  180.7 1.0 convert_bitcast_fusion.1
  181.7 0.2 copy.23
  182.0 0.8 reshape.29
  (4 shorter events, 0.0 us)
Async XLA Ops:
  0.0 76.1 %copy-start = (f32[1,3584]{1,0:T(1,128)S(1)}, f32[1,3584]{1,0:T(1,128)}, u32[]{:S(2)}) copy-start(f32[1,3584]{1,0:T(1,128)} %param.13) | copy-start | bytes 43012
  112.0 7.6 %copy-start.1 = (f32[128,768]{1,0:T(8,128)S(1)}, f32[128,768]{1,0:T(8,128)}, u32[]{:S(2)}) copy-start(f32[128,768]{1,0:T(8,128)} %get-tuple-element.12) | copy-start | bytes 1179652
  112.0 8.5 %copy-start.2 = (s32[1024]{0:T(1024)S(1)}, s32[1024]{0:T(1024)}, u32[]{:S(2)}) copy-start(s32[1024]{0:T(1024)} %param.15) | copy-start | bytes 12292
  112.0 8.5 %copy-start.3 = (s32[1024]{0:T(1024)S(1)}, s32[1024]{0:T(1024)}, u32[]{:S(2)}) copy-start(s32[1024]{0:T(1024)} %param.14) | copy-start | bytes 12292

commit v17 on v16

--- a/solution.py
+++ b/solution.py
@@ -203,7 +203,7 @@
     )(w, v)
 
 
-def _gather_kernel(e, oa, ob, g1a, g1b, ga, gb, send_sems, recv_sems):
+def _gather_kernel(e, oa, ob, g1a, g1b, send_sems, recv_sems):
     a, b = _latent_coords()
     _greet(a, b)
     peers_z = [(b + k) % RING for k in range(1, RING)]
@@ -225,23 +225,20 @@
         _copy(e.at[1], g1b.at[t], send_sems.at[1, t], recv_sems.at[1, t], 0).wait_recv()
     second = []
     for t in peers_x:
-        c = _copy(g1a, ga.at[a], send_sems.at[2, t], recv_sems.at[2, a], t * RING + b)
-        c.start()
-        second.append(c)
-    for t in peers_z:
-        c = _copy(g1b, gb.at[b], send_sems.at[3, t], recv_sems.at[3, b], a * RING + t)
+        c = _copy(g1a, oa.at[a], send_sems.at[2, t], recv_sems.at[2, a], t * RING + b)
+        c.start()
+        second.append(c)
+    for t in peers_z:
+        c = _copy(g1b, ob.at[:, b], send_sems.at[3, t], recv_sems.at[3, b], a * RING + t)
         c.start()
         second.append(c)
     oa[a] = g1a[...]
     for j in range(RING):
         ob[j, b] = g1b[j]
     for t in peers_x:
-        _copy(g1a, ga.at[t], send_sems.at[2, t], recv_sems.at[2, t], 0).wait_recv()
-        oa[t] = ga[t]
-    for t in peers_z:
-        _copy(g1b, gb.at[t], send_sems.at[3, t], recv_sems.at[3, t], 0).wait_recv()
-        for j in range(RING):
-            ob[j, t] = gb[t, j]
+        _copy(g1a, oa.at[t], send_sems.at[2, t], recv_sems.at[2, t], 0).wait_recv()
+    for t in peers_z:
+        _copy(g1b, ob.at[:, t], send_sems.at[3, t], recv_sems.at[3, t], 0).wait_recv()
     for c in first + second:
         c.wait_send()
 
@@ -259,8 +256,6 @@
         scratch_shapes=[
             pltpu.VMEM((n, h, c), dt),
             pltpu.VMEM((n, h, c), dt),
-            pltpu.VMEM((n, n, h, c), dt),
-            pltpu.VMEM((n, n, h, c), dt),
             pltpu.SemaphoreType.DMA((4, n)),
             pltpu.SemaphoreType.DMA((4, n)),
         ],

time: 183 us -> 183 us (level)
  no operation moved by 1% of the time
where the time goes in v17:
time: 183 us
  Pallas kernels  159 us (87%)
  matrix products  14.5 us (8%)
  other arithmetic  5.17 us (3%)
  local copies, waits for them, and re-layouts  3.65 us (2%)
    pallas_call x1, Pallas kernels, latent_reduce(): pl.pallas_call(_reduce_kernel, out_shape=jax.ShapeDtypeStruct((2, h, c),...  37.1 us
    pallas_call x1, Pallas kernels, latent_reduce_mm(): pl.pallas_call(_reduce_mm_kernel, out_shape=jax.ShapeDtypeStruct((2, d, h...  35.6 us
    pallas_call x1, Pallas kernels, latent_gather(): pl.pallas_call(_gather_kernel, out_shape=(full, full), in_specs=[pl.Block...  34 us
    pallas_call x1, Pallas kernels, layer_pre(): pl.pallas_call(_layer_pre_kernel, out_shape=(jax.ShapeDtypeStruct((rows,...  29.6 us
    pallas_call x1, Pallas kernels, layer_grad(): pl.pallas_call(_layer_grad_kernel, out_shape=jax.ShapeDtypeStruct((cols,...  22.9 us
    dot_general x1, matrix products, local(): jnp.dot(dec_weight[0], error_all, preferred_element_type=jnp.float32)  7.56 us
    unnamed x1, matrix products  5.47 us

profile of v17, /device:TPU:1, one launch (start us, length us, event | category | flops | bytes accessed | tf_op | source)
XLA Modules:
  0.0 182.7 jit_solution(10501732129812239376)
XLA Ops:
  0.0 0.0 copy-start
  0.0 1.1 constant_dynamic-slice_fusion
  1.2 0.1 copy.25
  1.3 0.3 reshape.30
  1.6 29.6 %shard_map.82 = (bf16[512,768]{1,0:T(8,128)(2,1)}, f32[128,768]{1,0:T(8,128)}) custom-call(bf16[512,3584]{1,0:T(8,128)(2,1)} %bitcast.39, bf16[3584,768]{1,0:T(8,128)(2,1)} %bitcast.36, f32[768]{0:T(1024)} %bias.1), custom_call_target="tpu_custom_call" | custom-call | tf_op jit(solution)/shard_map/pallas_call | solution.py:355
  31.2 5.5 %fusion = f32[512,3584]{0,1:S(1)} fusion(bf16[512,768]{1,0:T(8,128)(2,1)} %get-tuple-element.9, bf16[1,768,3584]{2,1,0:T(8,128)(2,1)} %param.12), kind=kOutput, calls=%fused_computation | convolution fusion | flops 2818572288 | bytes 13631488
  36.7 2.3 %convert_bitcast_fusion.x = bf16[4,4,224,512]{3,2,1,0:T(8,128)(2,1)} fusion(f32[512,4,4,224]{0,3,2,1:T(8,128)S(1)} %bitcast.38), kind=kLoop, calls=%fused_computation.7 | loop fusion | flops 1835008 | bytes 11010048 | tf_op jit(solution)/shard_map/convert_element_type | solution.py:442
  39.0 37.1 %shard_map.83 = f32[2,224,256]{2,1,0:T(8,128)} custom-call(bf16[4,4,224,512]{3,2,1,0:T(8,128)(2,1)} %convert_bitcast_fusion.x), custom_call_target="tpu_custom_call" | custom-call | tf_op jit(solution)/shard_map/pallas_call | solution.py:96
  76.1 0.0 copy-done
  76.1 0.1 constant_dynamic-slice_fusion.1
  76.2 1.8 fusion.21.e
  78.0 34.0 %shard_map.84 = (bf16[4,4,224,256]{3,2,1,0:T(8,128)(2,1)}, bf16[4,4,224,256]{3,2,1,0:T(8,128)(2,1)}) custom-call(bf16[2,224,256]{2,1,0:T(8,128)(2,1)} %fusion.21.e), custom_call_target="tpu_custom_call" | custom-call | tf_op jit(solution)/shard_map/pallas_call | solution.py:251
  112.0 0.0 copy-start.1
  112.0 0.0 copy-start.2
  112.0 0.0 copy-start.3
  112.0 7.6 %fusion.16.g = bf16[768,512]{1,0:T(8,128)(2,1)} fusion(bf16[3584,256]{1,0:T(8,128)(2,1)} %bitcast.43, bf16[3584,256]{1,0:T(8,128)(2,1)} %bitcast.42, bf16[1,768,3584]{2,1,0:T(8,128)(2,1)} %param.12), kind=kOutput, calls=%fused_computation.13 | convolution fusion | flops 2826305536 | bytes 9961472 | tf_op jit(solution)/shard_map/dot_general | solution.py:451
  119.6 0.0 copy-done.1
  119.6 0.9 copy.22
  120.5 1.5 fusion.7.margin_q
  122.0 22.9 %shard_map.85.v = bf16[768,512]{1,0:T(8,128)(2,1)} custom-call(bf16[768,512]{1,0:T(8,128)(2,1)} %fusion.16.g, f32[768,128]{1,0:T(8,128)} %bitcast.40, f32[768,128]{1,0:T(8,128)} %fusion.7.margin_q), custom_call_target="tpu_custom_call" | custom-call | tf_op jit(solution)/shard_map/pallas_call | solution.py:416
  145.0 35.6 %shard_map.86 = f32[2,224,256]{2,1,0:T(8,128)} custom-call(bf16[4,4,224,768]{3,2,1,0:T(8,128)(2,1)} %bitcast.37, bf16[768,512]{1,0:T(8,128)(2,1)} %shard_map.85.v), custom_call_target="tpu_custom_call" | custom-call | tf_op jit(solution)/shard_map/pallas_call | solution.py:185
  180.5 1.0 convert_bitcast_fusion.1
  181.6 0.2 copy.23
  181.8 0.8 reshape.29
  (4 shorter events, 0.0 us)
Async XLA Ops:
  0.0 76.1 %copy-start = (f32[1,3584]{1,0:T(1,128)S(1)}, f32[1,3584]{1,0:T(1,128)}, u32[]{:S(2)}) copy-start(f32[1,3584]{1,0:T(1,128)} %param.13) | copy-start | bytes 43012
  112.0 7.6 %copy-start.1 = (f32[128,768]{1,0:T(8,128)S(1)}, f32[128,768]{1,0:T(8,128)}, u32[]{:S(2)}) copy-start(f32[128,768]{1,0:T(8,128)} %get-tuple-element.12) | copy-start | bytes 1179652
  112.0 8.5 %copy-start.2 = (s32[1024]{0:T(1024)S(1)}, s32[1024]{0:T(1024)}, u32[]{:S(2)}) copy-start(s32[1024]{0:T(1024)} %param.15) | copy-start | bytes 12292
  112.0 8.5 %copy-start.3 = (s32[1024]{0:T(1024)S(1)}, s32[1024]{0:T(1024)}, u32[]{:S(2)}) copy-start(s32[1024]{0:T(1024)} %param.14) | copy-start | bytes 12292

commit v18 on v16

--- a/solution.py
+++ b/solution.py
@@ -31,7 +31,7 @@
     )
 
 
-def _reduce_kernel(x, out, r1a, r1b, s1a, s1b, r2a, r2b, send_sems, recv_sems):
+def _reduce_kernel(x, bias, clean, out, r1a, r1b, s1a, s1b, r2a, r2b, send_sems, recv_sems):
     h = x.shape[-1] // 2
     xa = x.at[:, :, :, pl.ds(0, h)]
     xb = x.at[:, :, :, pl.ds(h, h)]
@@ -83,20 +83,20 @@
         own_a = own_a + r2a[t].astype(jnp.float32)
     for t in peers_z:
         own_b = own_b + r2b[t].astype(jnp.float32)
-    out[0] = own_a
-    out[1] = own_b
+    out[0] = (own_a + bias[...] - clean[0].astype(jnp.float32)).astype(out.dtype)
+    out[1] = (own_b + bias[...] - clean[1].astype(jnp.float32)).astype(out.dtype)
     for c in first + second:
         c.wait_send()
 
 
-def latent_reduce(x, collective_id):
+def latent_reduce(x, bias, clean, collective_id):
     n, _, h, c = x.shape
     c = c // 2
     dt = x.dtype
     return pl.pallas_call(
         _reduce_kernel,
-        out_shape=jax.ShapeDtypeStruct((2, h, c), jnp.float32),
-        in_specs=[pl.BlockSpec(memory_space=pltpu.VMEM)],
+        out_shape=jax.ShapeDtypeStruct((2, h, c), jnp.bfloat16),
+        in_specs=[pl.BlockSpec(memory_space=pltpu.VMEM)] * 3,
         out_specs=pl.BlockSpec(memory_space=pltpu.VMEM),
         scratch_shapes=[
             pltpu.VMEM((n, n, h, c), dt),
@@ -109,7 +109,7 @@
             pltpu.SemaphoreType.DMA((4, n)),
         ],
         compiler_params=pltpu.CompilerParams(collective_id=collective_id, has_side_effects=True),
-    )(x)
+    )(x, bias, clean)
 
 
 def _reduce_mm_kernel(w, v, out, xa, xb, r1a, r1b, s1a, s1b, r2a, r2b, send_sems, recv_sems):
@@ -444,11 +444,10 @@
     features, pre_q = layer_pre(inputs[:, 0, :], enc_weight[0], enc_bias)
     dec4 = dec_weight[0].reshape(lat_count, RING, RING, chunk)
     recon_part = jnp.einsum("rf,fabd->abdr", features, dec4, preferred_element_type=jnp.float32)
-    recon_sum = latent_reduce(recon_part.astype(jnp.bfloat16), 3)
     bias_part = lax.dynamic_slice_in_dim(dec_bias[0], me * chunk, chunk)
     clean_part = lax.dynamic_slice_in_dim(clean_acts[:, 0, :], me * chunk, chunk, axis=1)
-    clean_t = jnp.swapaxes(clean_part.reshape(2, half, chunk), 1, 2).astype(jnp.float32)
-    recon_error = (recon_sum + bias_part[:, None] - clean_t).astype(jnp.bfloat16)
+    clean_t = jnp.swapaxes(clean_part.reshape(2, half, chunk), 1, 2)
+    recon_error = latent_reduce(recon_part.astype(jnp.bfloat16), bias_part[:, None], clean_t, 3)
     error_a, error_b = latent_gather(recon_error, 4)
     error_all = jnp.concatenate(
         [error_a.reshape(d_model, half), error_b.reshape(d_model, half)], axis=1

time: 183 us -> 182 us (level)
    convert_element_type x2 -> x1, other arithmetic: 4.12 us -> 2.3 us  [local(): recon_part.astype(jnp.bfloat16)]
where the time goes in v18:
time: 182 us
  Pallas kernels  159 us (87%)
  matrix products  14.5 us (8%)
  local copies, waits for them, and re-layouts  4.84 us (3%)
  other arithmetic  3.35 us (2%)
    pallas_call x1, Pallas kernels, latent_reduce(): pl.pallas_call(_reduce_kernel, out_shape=jax.ShapeDtypeStruct((2, h, c),...  37.1 us
    pallas_call x1, Pallas kernels, latent_reduce_mm(): pl.pallas_call(_reduce_mm_kernel, out_shape=jax.ShapeDtypeStruct((2, d, h...  35.7 us
    pallas_call x1, Pallas kernels, latent_gather(): pl.pallas_call(_gather_kernel, out_shape=(full, full), in_specs=[pl.Block...  34.1 us
    pallas_call x1, Pallas kernels, layer_pre(): pl.pallas_call(_layer_pre_kernel, out_shape=(jax.ShapeDtypeStruct((rows,...  29.6 us
    pallas_call x1, Pallas kernels, layer_grad(): pl.pallas_call(_layer_grad_kernel, out_shape=jax.ShapeDtypeStruct((cols,...  22.9 us
    dot_general x1, matrix products, local(): jnp.dot(dec_weight[0], error_all, preferred_element_type=jnp.float32)  7.56 us
    unnamed x1, matrix products  5.47 us

profile of v18, /device:TPU:1, one launch (start us, length us, event | category | flops | bytes accessed | tf_op | source)
XLA Modules:
  0.0 182.2 jit_solution(2860337574022072458)
XLA Ops:
  0.0 0.0 copy-start
  0.0 29.6 %shard_map.82 = (bf16[512,768]{1,0:T(8,128)(2,1)}, f32[128,768]{1,0:T(8,128)}) custom-call(bf16[512,3584]{1,0:T(8,128)(2,1)} %bitcast.36, bf16[3584,768]{1,0:T(8,128)(2,1)} %bitcast.33, f32[768]{0:T(1024)} %bias.1), custom_call_target="tpu_custom_call" | custom-call | tf_op jit(solution)/shard_map/pallas_call | solution.py:360
  29.6 5.5 %fusion = f32[512,3584]{0,1:S(1)} fusion(bf16[512,768]{1,0:T(8,128)(2,1)} %get-tuple-element.9, bf16[1,768,3584]{2,1,0:T(8,128)(2,1)} %param.12), kind=kOutput, calls=%fused_computation | convolution fusion | flops 2818572288 | bytes 13631488
  35.1 2.3 %convert_bitcast_fusion.x = bf16[4,4,224,512]{3,2,1,0:T(8,128)(2,1)} fusion(f32[512,4,4,224]{0,3,2,1:T(8,128)S(1)} %bitcast.35), kind=kLoop, calls=%fused_computation.7 | loop fusion | flops 1835008 | bytes 11010048 | tf_op jit(solution)/shard_map/convert_element_type | solution.py:450
  37.4 0.0 copy-done
  37.4 0.1 dynamic-slice_bitcast_fusion
  37.4 0.8 copy.15.bias
  38.2 1.1 constant_dynamic-slice_fusion
  39.4 0.8 copy.14
  40.2 37.1 %shard_map.83.e = bf16[2,224,256]{2,1,0:T(8,128)(2,1)} custom-call(bf16[4,4,224,512]{3,2,1,0:T(8,128)(2,1)} %convert_bitcast_fusion.x, f32[224,1]{1,0:T(8,128)} %copy.15.bias, bf16[2,224,256]{2,1,0:T(8,128)(2,1)} %bitcast.39), custom_call_target="tpu_custom_call" | custom-call | tf_op jit(solution)/shard_map/pallas_call | solution.py:96
  77.3 34.1 %shard_map.84 = (bf16[4,4,224,256]{3,2,1,0:T(8,128)(2,1)}, bf16[4,4,224,256]{3,2,1,0:T(8,128)(2,1)}) custom-call(bf16[2,224,256]{2,1,0:T(8,128)(2,1)} %shard_map.83.e), custom_call_target="tpu_custom_call" | custom-call | tf_op jit(solution)/shard_map/pallas_call | solution.py:254
  111.4 0.0 copy-start.1
  111.4 0.0 copy-start.2
  111.4 0.0 copy-start.3
  111.5 7.6 %fusion.16.g = bf16[768,512]{1,0:T(8,128)(2,1)} fusion(bf16[3584,256]{1,0:T(8,128)(2,1)} %bitcast.41, bf16[3584,256]{1,0:T(8,128)(2,1)} %bitcast.40, bf16[1,768,3584]{2,1,0:T(8,128)(2,1)} %param.12), kind=kOutput, calls=%fused_computation.13 | convolution fusion | flops 2826305536 | bytes 9961472 | tf_op jit(solution)/shard_map/dot_general | solution.py:455
  119.0 0.0 copy-done.1
  119.0 0.9 copy.17
  119.9 0.0 copy-done.3
  120.0 1.5 fusion.7.margin_q
  121.5 22.9 %shard_map.85.v = bf16[768,512]{1,0:T(8,128)(2,1)} custom-call(bf16[768,512]{1,0:T(8,128)(2,1)} %fusion.16.g, f32[768,128]{1,0:T(8,128)} %bitcast.37, f32[768,128]{1,0:T(8,128)} %fusion.7.margin_q), custom_call_target="tpu_custom_call" | custom-call | tf_op jit(solution)/shard_map/pallas_call | solution.py:421
  144.4 35.7 %shard_map.86 = f32[2,224,256]{2,1,0:T(8,128)} custom-call(bf16[4,4,224,768]{3,2,1,0:T(8,128)(2,1)} %bitcast.34, bf16[768,512]{1,0:T(8,128)(2,1)} %shard_map.85.v), custom_call_target="tpu_custom_call" | custom-call | tf_op jit(solution)/shard_map/pallas_call | solution.py:185
  180.1 1.0 convert_bitcast_fusion.1
  181.1 0.2 copy.18
  181.4 0.8 reshape.29
  (3 shorter events, 0.0 us)
Async XLA Ops:
  0.0 37.4 %copy-start = (f32[1,3584]{1,0:T(1,128)S(1)}, f32[1,3584]{1,0:T(1,128)}, u32[]{:S(2)}) copy-start(f32[1,3584]{1,0:T(1,128)} %param.13) | copy-start | bytes 43012
  111.4 7.6 %copy-start.1 = (f32[128,768]{1,0:T(8,128)S(1)}, f32[128,768]{1,0:T(8,128)}, u32[]{:S(2)}) copy-start(f32[128,768]{1,0:T(8,128)} %get-tuple-element.12) | copy-start | bytes 1179652
  111.4 8.5 %copy-start.2 = (s32[1024]{0:T(1024)S(1)}, s32[1024]{0:T(1024)}, u32[]{:S(2)}) copy-start(s32[1024]{0:T(1024)} %param.15) | copy-start | bytes 12292
  111.4 8.5 %copy-start.3 = (s32[1024]{0:T(1024)S(1)}, s32[1024]{0:T(1024)}, u32[]{:S(2)}) copy-start(s32[1024]{0:T(1024)} %param.14) | copy-start | bytes 12292

commit v19 on v18

--- a/solution.py
+++ b/solution.py
@@ -31,23 +31,34 @@
     )
 
 
-def _reduce_kernel(x, bias, clean, out, r1a, r1b, s1a, s1b, r2a, r2b, send_sems, recv_sems):
+def _reduce_kernel(x, bias, clean, out, xs, r1a, r1b, s1a, s1b, r2a, r2b, send_sems, recv_sems):
     h = x.shape[-1] // 2
-    xa = x.at[:, :, :, pl.ds(0, h)]
-    xb = x.at[:, :, :, pl.ds(h, h)]
+    xa = xs.at[:, :, :, pl.ds(0, h)]
+    xb = xs.at[:, :, :, pl.ds(h, h)]
     a, b = _latent_coords()
     _greet(a, b)
     peers_z = [(b + k) % RING for k in range(1, RING)]
     peers_x = [(a + k) % RING for k in range(1, RING)]
+    def round_a(j):
+        for i in range(RING):
+            xs[i, j, :, 0:h] = x[i, j, :, 0:h].astype(xs.dtype)
+
+    def round_b(i):
+        for j in range(RING):
+            xs[i, j, :, h:2 * h] = x[i, j, :, h:2 * h].astype(xs.dtype)
+
     first = []
-    for t in peers_z:
-        c = _copy(xa.at[:, t], r1a.at[b], send_sems.at[0, t], recv_sems.at[0, b], a * RING + t)
+    for tz, tx in zip(peers_z, peers_x):
+        round_a(tz)
+        c = _copy(xa.at[:, tz], r1a.at[b], send_sems.at[0, tz], recv_sems.at[0, b], a * RING + tz)
         c.start()
         first.append(c)
-    for t in peers_x:
-        c = _copy(xb.at[t], r1b.at[a], send_sems.at[1, t], recv_sems.at[1, a], t * RING + b)
+        round_b(tx)
+        c = _copy(xb.at[tx], r1b.at[a], send_sems.at[1, tx], recv_sems.at[1, a], tx * RING + b)
         c.start()
         first.append(c)
+    round_a(b)
+    round_b(a)
     for t in peers_z:
         _copy(xa.at[:, t], r1a.at[t], send_sems.at[0, t], recv_sems.at[0, t], 0).wait_recv()
     for t in peers_x:
@@ -92,13 +103,14 @@
 def latent_reduce(x, bias, clean, collective_id):
     n, _, h, c = x.shape
     c = c // 2
-    dt = x.dtype
+    dt = jnp.bfloat16
     return pl.pallas_call(
         _reduce_kernel,
         out_shape=jax.ShapeDtypeStruct((2, h, c), jnp.bfloat16),
         in_specs=[pl.BlockSpec(memory_space=pltpu.VMEM)] * 3,
         out_specs=pl.BlockSpec(memory_space=pltpu.VMEM),
         scratch_shapes=[
+            pltpu.VMEM((n, n, h, 2 * c), dt),
             pltpu.VMEM((n, n, h, c), dt),
             pltpu.VMEM((n, n, h, c), dt),
             pltpu.VMEM((n, h, c), dt),
@@ -447,7 +459,7 @@
     bias_part = lax.dynamic_slice_in_dim(dec_bias[0], me * chunk, chunk)
     clean_part = lax.dynamic_slice_in_dim(clean_acts[:, 0, :], me * chunk, chunk, axis=1)
     clean_t = jnp.swapaxes(clean_part.reshape(2, half, chunk), 1, 2)
-    recon_error = latent_reduce(recon_part.astype(jnp.bfloat16), bias_part[:, None], clean_t, 3)
+    recon_error = latent_reduce(recon_part, bias_part[:, None], clean_t, 3)
     error_a, error_b = latent_gather(recon_error, 4)
     error_all = jnp.concatenate(
         [error_a.reshape(d_model, half), error_b.reshape(d_model, half)], axis=1

time: 182 us -> 185 us (1.016)
  matrix products: 14.5 us -> 17.9 us
  other arithmetic: 3.35 us -> 1.05 us
  Pallas kernels: 159 us -> 161 us
    unnamed x1, matrix products: 5.47 us -> 8.82 us
    convert_element_type x1 -> x0, other arithmetic: 2.3 us -> none  [local(): recon_part.astype(jnp.bfloat16)]
where the time goes in v19:
time: 185 us
  Pallas kernels  161 us (87%)
  matrix products  17.9 us (10%)
  local copies, waits for them, and re-layouts  4.82 us (3%)
    pallas_call x1, Pallas kernels, latent_reduce(): pl.pallas_call(_reduce_kernel, out_shape=jax.ShapeDtypeStruct((2, h, c),...  38.3 us
    pallas_call x1, Pallas kernels, latent_reduce_mm(): pl.pallas_call(_reduce_mm_kernel, out_shape=jax.ShapeDtypeStruct((2, d, h...  35.9 us
    pallas_call x1, Pallas kernels, latent_gather(): pl.pallas_call(_gather_kernel, out_shape=(full, full), in_specs=[pl.Block...  34.1 us
    pallas_call x1, Pallas kernels, layer_pre(): pl.pallas_call(_layer_pre_kernel, out_shape=(jax.ShapeDtypeStruct((rows,...  29.6 us
    pallas_call x1, Pallas kernels, layer_grad(): pl.pallas_call(_layer_grad_kernel, out_shape=jax.ShapeDtypeStruct((cols,...  22.9 us
    unnamed x1, matrix products  8.82 us
    dot_general x1, matrix products, local(): jnp.dot(dec_weight[0], error_all, preferred_element_type=jnp.float32)  7.56 us

profile of v19, /device:TPU:1, one launch (start us, length us, event | category | flops | bytes accessed | tf_op | source)
XLA Modules:
  0.0 184.7 jit_solution(10077109306095054931)
XLA Ops:
  0.0 0.0 copy-start
  0.0 29.6 %shard_map.82 = (bf16[512,768]{1,0:T(8,128)(2,1)}, f32[128,768]{1,0:T(8,128)}) custom-call(bf16[512,3584]{1,0:T(8,128)(2,1)} %bitcast.36, bf16[3584,768]{1,0:T(8,128)(2,1)} %bitcast.33, f32[768]{0:T(1024)} %bias.1), custom_call_target="tpu_custom_call" | custom-call | tf_op jit(solution)/shard_map/pallas_call | solution.py:372
  29.6 8.8 %fusion = f32[512,3584]{0,1} fusion(bf16[512,768]{1,0:T(8,128)(2,1)} %get-tuple-element.9, bf16[1,768,3584]{2,1,0:T(8,128)(2,1)} %param.12), kind=kOutput, calls=%fused_computation | convolution fusion | flops 2818572288 | bytes 13631488
  38.5 0.0 copy-done
  38.5 0.1 dynamic-slice_bitcast_fusion
  38.5 0.8 copy.15.bias
  39.3 1.1 constant_dynamic-slice_fusion
  40.5 0.8 copy.14
  41.3 38.3 %shard_map.83.e = bf16[2,224,256]{2,1,0:T(8,128)(2,1)} custom-call(f32[4,4,224,512]{3,2,1,0:T(8,128)} %bitcast.35, f32[224,1]{1,0:T(8,128)} %copy.15.bias, bf16[2,224,256]{2,1,0:T(8,128)(2,1)} %bitcast.39), custom_call_target="tpu_custom_call" | custom-call | tf_op jit(solution)/shard_map/pallas_call | solution.py:107
  79.6 34.1 %shard_map.84 = (bf16[4,4,224,256]{3,2,1,0:T(8,128)(2,1)}, bf16[4,4,224,256]{3,2,1,0:T(8,128)(2,1)}) custom-call(bf16[2,224,256]{2,1,0:T(8,128)(2,1)} %shard_map.83.e), custom_call_target="tpu_custom_call" | custom-call | tf_op jit(solution)/shard_map/pallas_call | solution.py:266
  113.8 0.0 copy-start.1
  113.8 0.0 copy-start.2
  113.8 0.0 copy-start.3
  113.8 7.6 %fusion.16.g = bf16[768,512]{1,0:T(8,128)(2,1)} fusion(bf16[3584,256]{1,0:T(8,128)(2,1)} %bitcast.41, bf16[3584,256]{1,0:T(8,128)(2,1)} %bitcast.40, bf16[1,768,3584]{2,1,0:T(8,128)(2,1)} %param.12), kind=kOutput, calls=%fused_computation.12 | convolution fusion | flops 2826305536 | bytes 9961472 | tf_op jit(solution)/shard_map/dot_general | solution.py:467
  121.4 0.0 copy-done.1
  121.4 0.9 copy.17
  122.3 0.0 copy-done.2
  122.3 0.0 copy-done.3
  122.3 1.5 fusion.7.margin_q
  123.8 22.9 %shard_map.85.v = bf16[768,512]{1,0:T(8,128)(2,1)} custom-call(bf16[768,512]{1,0:T(8,128)(2,1)} %fusion.16.g, f32[768,128]{1,0:T(8,128)} %bitcast.37, f32[768,128]{1,0:T(8,128)} %fusion.7.margin_q), custom_call_target="tpu_custom_call" | custom-call | tf_op jit(solution)/shard_map/pallas_call | solution.py:433
  146.7 35.9 %shard_map.86 = f32[2,224,256]{2,1,0:T(8,128)} custom-call(bf16[4,4,224,768]{3,2,1,0:T(8,128)(2,1)} %bitcast.34, bf16[768,512]{1,0:T(8,128)(2,1)} %shard_map.85.v), custom_call_target="tpu_custom_call" | custom-call | tf_op jit(solution)/shard_map/pallas_call | solution.py:197
  182.6 1.0 convert_bitcast_fusion
  183.6 0.2 copy.18
  183.9 0.8 reshape.29
  (2 shorter events, 0.0 us)
Async XLA Ops:
  0.0 38.5 %copy-start = (f32[1,3584]{1,0:T(1,128)S(1)}, f32[1,3584]{1,0:T(1,128)}, u32[]{:S(2)}) copy-start(f32[1,3584]{1,0:T(1,128)} %param.13) | copy-start | bytes 43012
  113.8 7.6 %copy-start.1 = (f32[128,768]{1,0:T(8,128)S(1)}, f32[128,768]{1,0:T(8,128)}, u32[]{:S(2)}) copy-start(f32[128,768]{1,0:T(8,128)} %get-tuple-element.12) | copy-start | bytes 1179652
  113.8 8.5 %copy-start.2 = (s32[1024]{0:T(1024)S(1)}, s32[1024]{0:T(1024)}, u32[]{:S(2)}) copy-start(s32[1024]{0:T(1024)} %param.15) | copy-start | bytes 12292
  113.8 8.5 %copy-start.3 = (s32[1024]{0:T(1024)S(1)}, s32[1024]{0:T(1024)}, u32[]{:S(2)}) copy-start(s32[1024]{0:T(1024)} %param.14) | copy-start | bytes 12292

commit v20 on v18

--- a/solution.py
+++ b/solution.py
@@ -203,7 +203,7 @@
     )(w, v)
 
 
-def _gather_kernel(e, oa, ob, g1a, g1b, ga, gb, send_sems, recv_sems):
+def _gather_kernel(e, targets, pairing, oa, ob, margin, g1a, g1b, ga, gb, send_sems, recv_sems):
     a, b = _latent_coords()
     _greet(a, b)
     peers_z = [(b + k) % RING for k in range(1, RING)]
@@ -233,6 +233,18 @@
         c.start()
         second.append(c)
     oa[a] = g1a[...]
+    f, q = margin.shape
+    n_rows = pairing.shape[0]
+    lat0 = lax.axis_index("latent") * f
+    row0 = lax.axis_index("row") * (LAYERS * q) + lax.axis_index("layer") * q
+    lat_ids = lat0 + lax.broadcasted_iota(jnp.int32, (f, n_rows), 0)
+    target_hot = (lat_ids == targets[...]).astype(jnp.bfloat16)
+    row_ids = row0 + lax.broadcasted_iota(jnp.int32, (n_rows, q), 1)
+    every_row = lax.broadcasted_iota(jnp.int32, (n_rows, q), 0)
+    pair_table = (
+        (every_row == row_ids).astype(jnp.float32) - (pairing[...] == row_ids).astype(jnp.float32)
+    ).astype(jnp.bfloat16)
+    margin[...] = jnp.dot(target_hot, pair_table, preferred_element_type=jnp.float32)
     for j in range(RING):
         ob[j, b] = g1b[j]
     for t in peers_x:
@@ -246,16 +258,16 @@
         c.wait_send()
 
 
-def latent_gather(e, collective_id):
+def latent_gather(e, targets, pairing, lat_count, collective_id):
     _, h, c = e.shape
     n = RING
     dt = e.dtype
     full = jax.ShapeDtypeStruct((n, n, h, c), dt)
     return pl.pallas_call(
         _gather_kernel,
-        out_shape=(full, full),
-        in_specs=[pl.BlockSpec(memory_space=pltpu.VMEM)],
-        out_specs=(pl.BlockSpec(memory_space=pltpu.VMEM), pl.BlockSpec(memory_space=pltpu.VMEM)),
+        out_shape=(full, full, jax.ShapeDtypeStruct((lat_count, 2 * c // LAYERS), jnp.float32)),
+        in_specs=[pl.BlockSpec(memory_space=pltpu.VMEM)] * 3,
+        out_specs=(pl.BlockSpec(memory_space=pltpu.VMEM),) * 3,
         scratch_shapes=[
             pltpu.VMEM((n, h, c), dt),
             pltpu.VMEM((n, h, c), dt),
@@ -265,7 +277,7 @@
             pltpu.SemaphoreType.DMA((4, n)),
         ],
         compiler_params=pltpu.CompilerParams(collective_id=collective_id, has_side_effects=True),
-    )(e)
+    )(e, targets, pairing)
 
 
 def _layer_roles():
@@ -448,25 +460,13 @@
     clean_part = lax.dynamic_slice_in_dim(clean_acts[:, 0, :], me * chunk, chunk, axis=1)
     clean_t = jnp.swapaxes(clean_part.reshape(2, half, chunk), 1, 2)
     recon_error = latent_reduce(recon_part.astype(jnp.bfloat16), bias_part[:, None], clean_t, 3)
-    error_a, error_b = latent_gather(recon_error, 4)
+    error_a, error_b, margin_q = latent_gather(
+        recon_error, targets.reshape(1, all_rows), pairing.reshape(all_rows, 1), lat_count, 4
+    )
     error_all = jnp.concatenate(
         [error_a.reshape(d_model, half), error_b.reshape(d_model, half)], axis=1
     )
     partial_grad_t = jnp.dot(dec_weight[0], error_all, preferred_element_type=jnp.float32)
-    quarter = row_count // LAYERS
-    row_ids = (
-        lax.axis_index("row") * row_count
-        + lax.axis_index("layer") * quarter
-        + jnp.arange(quarter, dtype=jnp.int32)
-    )
-    latent_ids = me * lat_count + jnp.arange(lat_count, dtype=jnp.int32)
-    every_row = jnp.arange(all_rows, dtype=jnp.int32)
-    pair_table_t = (
-        (every_row[:, None] == row_ids[None, :]).astype(jnp.float32)
-        - (pairing[:, None] == row_ids[None, :]).astype(jnp.float32)
-    ).astype(jnp.bfloat16)
-    target_hot_t = (latent_ids[:, None] == targets[None, :]).astype(jnp.bfloat16)
-    margin_q = jnp.dot(target_hot_t, pair_table_t, preferred_element_type=jnp.float32)
     pre_grad_t = layer_grad(partial_grad_t.astype(jnp.bfloat16), pre_q.T, margin_q)
     enc4 = enc_weight[0].reshape(RING, RING, chunk, lat_count)
     total = latent_reduce_mm(enc4, pre_grad_t, 5)

time: 182 us -> 182 us (level)
  no operation moved by 1% of the time
where the time goes in v20:
time: 182 us
  Pallas kernels  160 us (88%)
  matrix products  13 us (7%)
  local copies, waits for them, and re-layouts  5.85 us (3%)
  other arithmetic  3.34 us (2%)
    pallas_call x1, Pallas kernels, latent_reduce(): pl.pallas_call(_reduce_kernel, out_shape=jax.ShapeDtypeStruct((2, h, c),...  37.1 us
    pallas_call x1, Pallas kernels, latent_reduce_mm(): pl.pallas_call(_reduce_mm_kernel, out_shape=jax.ShapeDtypeStruct((2, d, h...  35.7 us
    pallas_call x1, Pallas kernels, latent_gather(): pl.pallas_call(_gather_kernel, out_shape=(full, full, jax.ShapeDtypeStruc...  34.4 us
    pallas_call x1, Pallas kernels, layer_pre(): pl.pallas_call(_layer_pre_kernel, out_shape=(jax.ShapeDtypeStruct((rows,...  29.6 us
    pallas_call x1, Pallas kernels, layer_grad(): pl.pallas_call(_layer_grad_kernel, out_shape=jax.ShapeDtypeStruct((cols,...  22.9 us
    dot_general x1, matrix products, local(): jnp.dot(dec_weight[0], error_all, preferred_element_type=jnp.float32)  7.57 us
    unnamed x1, matrix products  5.47 us

profile of v20, /device:TPU:1, one launch (start us, length us, event | category | flops | bytes accessed | tf_op | source)
XLA Modules:
  0.0 182.0 jit_solution(17738889754153622773)
XLA Ops:
  0.0 0.0 copy-start
  0.0 29.6 %shard_map.82 = (bf16[512,768]{1,0:T(8,128)(2,1)}, f32[128,768]{1,0:T(8,128)}) custom-call(bf16[512,3584]{1,0:T(8,128)(2,1)} %bitcast.38, bf16[3584,768]{1,0:T(8,128)(2,1)} %bitcast.35, f32[768]{0:T(1024)} %bias.1), custom_call_target="tpu_custom_call" | custom-call | tf_op jit(solution)/shard_map/pallas_call | solution.py:372
  29.6 5.5 %fusion = f32[512,3584]{0,1:S(1)} fusion(bf16[512,768]{1,0:T(8,128)(2,1)} %get-tuple-element.10, bf16[1,768,3584]{2,1,0:T(8,128)(2,1)} %param.12), kind=kOutput, calls=%fused_computation | convolution fusion | flops 2818572288 | bytes 13631488
  35.1 2.3 %convert_bitcast_fusion.x = bf16[4,4,224,512]{3,2,1,0:T(8,128)(2,1)} fusion(f32[512,4,4,224]{0,3,2,1:T(8,128)S(1)} %bitcast.37), kind=kLoop, calls=%fused_computation.7 | loop fusion | flops 1835008 | bytes 11010048 | tf_op jit(solution)/shard_map/convert_element_type | solution.py:462
  37.4 0.0 copy-start.2
  37.4 0.0 copy-done
  37.4 0.1 dynamic-slice_bitcast_fusion
  37.4 0.8 copy.15.bias
  38.2 1.1 constant_dynamic-slice_fusion
  39.4 0.8 copy.14
  40.2 37.1 %shard_map.83.e = bf16[2,224,256]{2,1,0:T(8,128)(2,1)} custom-call(bf16[4,4,224,512]{3,2,1,0:T(8,128)(2,1)} %convert_bitcast_fusion.x, f32[224,1]{1,0:T(8,128)} %copy.15.bias, bf16[2,224,256]{2,1,0:T(8,128)(2,1)} %bitcast.41), custom_call_target="tpu_custom_call" | custom-call | tf_op jit(solution)/shard_map/pallas_call | solution.py:96
  77.3 0.0 copy-done.2
  77.3 1.0 copy.16.pairing
  78.4 34.4 %shard_map.84 = (bf16[4,4,224,256]{3,2,1,0:T(8,128)(2,1)}, bf16[4,4,224,256]{3,2,1,0:T(8,128)(2,1)}, f32[768,128]{1,0:T(8,128)}) custom-call(bf16[2,224,256]{2,1,0:T(8,128)(2,1)} %shard_map.83.e, s32[1,1024]{1,0:T(1,128)} %bitcast.43, s32[1024,1]{1,0:T(8,128)} %copy.16.pairing), custom_call_target="tpu_custom_call" | custom-call | tf_op jit(solution)/shard_map/pallas_call | solution.py:266
  112.8 0.0 copy-start.1
  112.8 7.6 %fusion.12.g = bf16[768,512]{1,0:T(8,128)(2,1)} fusion(bf16[3584,256]{1,0:T(8,128)(2,1)} %bitcast.45, bf16[3584,256]{1,0:T(8,128)(2,1)} %bitcast.44, bf16[1,768,3584]{2,1,0:T(8,128)(2,1)} %param.12), kind=kOutput, calls=%fused_computation.9 | convolution fusion | flops 2826305536 | bytes 9961472 | tf_op jit(solution)/shard_map/dot_general | solution.py:469
  120.3 0.0 copy-done.1
  120.3 0.9 copy.18
  121.3 22.9 %shard_map.85.v = bf16[768,512]{1,0:T(8,128)(2,1)} custom-call(bf16[768,512]{1,0:T(8,128)(2,1)} %fusion.12.g, f32[768,128]{1,0:T(8,128)} %bitcast.39, f32[768,128]{1,0:T(8,128)} %get-tuple-element.14.margin_q), custom_call_target="tpu_custom_call" | custom-call | tf_op jit(solution)/shard_map/pallas_call | solution.py:433
  144.2 35.7 %shard_map.86 = f32[2,224,256]{2,1,0:T(8,128)} custom-call(bf16[4,4,224,768]{3,2,1,0:T(8,128)(2,1)} %bitcast.36, bf16[768,512]{1,0:T(8,128)(2,1)} %shard_map.85.v), custom_call_target="tpu_custom_call" | custom-call | tf_op jit(solution)/shard_map/pallas_call | solution.py:185
  179.9 1.0 convert_bitcast_fusion.1
  180.9 0.2 copy.19
  181.2 0.8 reshape.27
Async XLA Ops:
  0.0 37.4 %copy-start = (f32[1,3584]{1,0:T(1,128)S(1)}, f32[1,3584]{1,0:T(1,128)}, u32[]{:S(2)}) copy-start(f32[1,3584]{1,0:T(1,128)} %param.13) | copy-start | bytes 43012
  37.4 40.0 %copy-start.2 = (s32[1024]{0:T(1024)S(1)}, s32[1024]{0:T(1024)}, u32[]{:S(2)}) copy-start(s32[1024]{0:T(1024)} %param.14) | copy-start | bytes 12292
  112.8 7.6 %copy-start.1 = (f32[128,768]{1,0:T(8,128)S(1)}, f32[128,768]{1,0:T(8,128)}, u32[]{:S(2)}) copy-start(f32[128,768]{1,0:T(8,128)} %get-tuple-element.13) | copy-start | bytes 1179652

commit v21 on v20

--- a/solution.py
+++ b/solution.py
@@ -234,17 +234,19 @@
         second.append(c)
     oa[a] = g1a[...]
     f, q = margin.shape
-    n_rows = pairing.shape[0]
+    n_rows = pairing.shape[1]
     lat0 = lax.axis_index("latent") * f
     row0 = lax.axis_index("row") * (LAYERS * q) + lax.axis_index("layer") * q
     lat_ids = lat0 + lax.broadcasted_iota(jnp.int32, (f, n_rows), 0)
     target_hot = (lat_ids == targets[...]).astype(jnp.bfloat16)
-    row_ids = row0 + lax.broadcasted_iota(jnp.int32, (n_rows, q), 1)
-    every_row = lax.broadcasted_iota(jnp.int32, (n_rows, q), 0)
+    row_ids = row0 + lax.broadcasted_iota(jnp.int32, (q, n_rows), 0)
+    every_row = lax.broadcasted_iota(jnp.int32, (q, n_rows), 1)
     pair_table = (
         (every_row == row_ids).astype(jnp.float32) - (pairing[...] == row_ids).astype(jnp.float32)
     ).astype(jnp.bfloat16)
-    margin[...] = jnp.dot(target_hot, pair_table, preferred_element_type=jnp.float32)
+    margin[...] = lax.dot_general(
+        target_hot, pair_table, (((1,), (1,)), ((), ())), preferred_element_type=jnp.float32
+    )
     for j in range(RING):
         ob[j, b] = g1b[j]
     for t in peers_x:
@@ -461,7 +463,7 @@
     clean_t = jnp.swapaxes(clean_part.reshape(2, half, chunk), 1, 2)
     recon_error = latent_reduce(recon_part.astype(jnp.bfloat16), bias_part[:, None], clean_t, 3)
     error_a, error_b, margin_q = latent_gather(
-        recon_error, targets.reshape(1, all_rows), pairing.reshape(all_rows, 1), lat_count, 4
+        recon_error, targets.reshape(1, all_rows), pairing.reshape(1, all_rows), lat_count, 4
     )
     error_all = jnp.concatenate(
         [error_a.reshape(d_model, half), error_b.reshape(d_model, half)], axis=1

time: 182 us -> 181 us (level)
  no operation moved by 1% of the time
where the time goes in v21:
time: 181 us
  Pallas kernels  159 us (88%)
  matrix products  13 us (7%)
  local copies, waits for them, and re-layouts  4.82 us (3%)
  other arithmetic  3.34 us (2%)
    pallas_call x1, Pallas kernels, latent_reduce(): pl.pallas_call(_reduce_kernel, out_shape=jax.ShapeDtypeStruct((2, h, c),...  37.1 us
    pallas_call x1, Pallas kernels, latent_reduce_mm(): pl.pallas_call(_reduce_mm_kernel, out_shape=jax.ShapeDtypeStruct((2, d, h...  35.7 us
    pallas_call x1, Pallas kernels, latent_gather(): pl.pallas_call(_gather_kernel, out_shape=(full, full, jax.ShapeDtypeStruc...  34.2 us
    pallas_call x1, Pallas kernels, layer_pre(): pl.pallas_call(_layer_pre_kernel, out_shape=(jax.ShapeDtypeStruct((rows,...  29.6 us
    pallas_call x1, Pallas kernels, layer_grad(): pl.pallas_call(_layer_grad_kernel, out_shape=jax.ShapeDtypeStruct((cols,...  22.9 us
    dot_general x1, matrix products, local(): jnp.dot(dec_weight[0], error_all, preferred_element_type=jnp.float32)  7.57 us
    unnamed x1, matrix products  5.47 us

profile of v21, /device:TPU:1, one launch (start us, length us, event | category | flops | bytes accessed | tf_op | source)
XLA Modules:
  0.0 180.8 jit_solution(2134312835674285311)
XLA Ops:
  0.0 0.0 copy-start
  0.0 29.6 %shard_map.82 = (bf16[512,768]{1,0:T(8,128)(2,1)}, f32[128,768]{1,0:T(8,128)}) custom-call(bf16[512,3584]{1,0:T(8,128)(2,1)} %bitcast.38, bf16[3584,768]{1,0:T(8,128)(2,1)} %bitcast.35, f32[768]{0:T(1024)} %bias.1), custom_call_target="tpu_custom_call" | custom-call | tf_op jit(solution)/shard_map/pallas_call | solution.py:374
  29.6 5.5 %fusion = f32[512,3584]{0,1:S(1)} fusion(bf16[512,768]{1,0:T(8,128)(2,1)} %get-tuple-element.10, bf16[1,768,3584]{2,1,0:T(8,128)(2,1)} %param.12), kind=kOutput, calls=%fused_computation | convolution fusion | flops 2818572288 | bytes 13631488
  35.1 2.3 %convert_bitcast_fusion.x = bf16[4,4,224,512]{3,2,1,0:T(8,128)(2,1)} fusion(f32[512,4,4,224]{0,3,2,1:T(8,128)S(1)} %bitcast.37), kind=kLoop, calls=%fused_computation.7 | loop fusion | flops 1835008 | bytes 11010048 | tf_op jit(solution)/shard_map/convert_element_type | solution.py:464
  37.4 0.0 copy-done
  37.4 0.1 dynamic-slice_bitcast_fusion
  37.4 0.8 copy.15.bias
  38.2 1.1 constant_dynamic-slice_fusion
  39.4 0.8 copy.14
  40.2 37.1 %shard_map.83.e = bf16[2,224,256]{2,1,0:T(8,128)(2,1)} custom-call(bf16[4,4,224,512]{3,2,1,0:T(8,128)(2,1)} %convert_bitcast_fusion.x, f32[224,1]{1,0:T(8,128)} %copy.15.bias, bf16[2,224,256]{2,1,0:T(8,128)(2,1)} %bitcast.41), custom_call_target="tpu_custom_call" | custom-call | tf_op jit(solution)/shard_map/pallas_call | solution.py:96
  77.3 34.2 %shard_map.84 = (bf16[4,4,224,256]{3,2,1,0:T(8,128)(2,1)}, bf16[4,4,224,256]{3,2,1,0:T(8,128)(2,1)}, f32[768,128]{1,0:T(8,128)}) custom-call(bf16[2,224,256]{2,1,0:T(8,128)(2,1)} %shard_map.83.e, s32[1,1024]{1,0:T(1,128)} %bitcast.42, s32[1,1024]{1,0:T(1,128)} %bitcast.43), custom_call_target="tpu_custom_call" | custom-call | tf_op jit(solution)/shard_map/pallas_call | solution.py:268
  111.5 0.0 copy-start.1
  111.6 7.6 %fusion.12.g = bf16[768,512]{1,0:T(8,128)(2,1)} fusion(bf16[3584,256]{1,0:T(8,128)(2,1)} %bitcast.45, bf16[3584,256]{1,0:T(8,128)(2,1)} %bitcast.44, bf16[1,768,3584]{2,1,0:T(8,128)(2,1)} %param.12), kind=kOutput, calls=%fused_computation.9 | convolution fusion | flops 2826305536 | bytes 9961472 | tf_op jit(solution)/shard_map/dot_general | solution.py:471
  119.1 0.0 copy-done.1
  119.1 0.9 copy.17
  120.0 22.9 %shard_map.85.v = bf16[768,512]{1,0:T(8,128)(2,1)} custom-call(bf16[768,512]{1,0:T(8,128)(2,1)} %fusion.12.g, f32[768,128]{1,0:T(8,128)} %bitcast.39, f32[768,128]{1,0:T(8,128)} %get-tuple-element.14.margin_q), custom_call_target="tpu_custom_call" | custom-call | tf_op jit(solution)/shard_map/pallas_call | solution.py:435
  143.0 35.7 %shard_map.86 = f32[2,224,256]{2,1,0:T(8,128)} custom-call(bf16[4,4,224,768]{3,2,1,0:T(8,128)(2,1)} %bitcast.36, bf16[768,512]{1,0:T(8,128)(2,1)} %shard_map.85.v), custom_call_target="tpu_custom_call" | custom-call | tf_op jit(solution)/shard_map/pallas_call | solution.py:185
  178.6 1.0 convert_bitcast_fusion.1
  179.7 0.2 copy.18
  179.9 0.8 reshape.27
Async XLA Ops:
  0.0 37.4 %copy-start = (f32[1,3584]{1,0:T(1,128)S(1)}, f32[1,3584]{1,0:T(1,128)}, u32[]{:S(2)}) copy-start(f32[1,3584]{1,0:T(1,128)} %param.13) | copy-start | bytes 43012
  111.5 7.6 %copy-start.1 = (f32[128,768]{1,0:T(8,128)S(1)}, f32[128,768]{1,0:T(8,128)}, u32[]{:S(2)}) copy-start(f32[128,768]{1,0:T(8,128)} %get-tuple-element.13) | copy-start | bytes 1179652

commit v22 on v21

--- a/solution.py
+++ b/solution.py
@@ -172,8 +172,8 @@
     for k in range(1, RING):
         own_a = own_a + r2a[(a + k) % RING].astype(jnp.float32)
         own_b = own_b + r2b[(b + k) % RING].astype(jnp.float32)
-    out[0] = own_a
-    out[1] = own_b
+    out[0] = own_a.astype(out.dtype)
+    out[1] = own_b.astype(out.dtype)
     for c in first + second:
         c.wait_send()
 
@@ -184,7 +184,7 @@
     dt = w.dtype
     return pl.pallas_call(
         _reduce_mm_kernel,
-        out_shape=jax.ShapeDtypeStruct((2, d, h), jnp.float32),
+        out_shape=jax.ShapeDtypeStruct((2, d, h), jnp.bfloat16),
         in_specs=[pl.BlockSpec(memory_space=pltpu.VMEM)] * 2,
         out_specs=pl.BlockSpec(memory_space=pltpu.VMEM),
         scratch_shapes=[
@@ -472,7 +472,7 @@
     pre_grad_t = layer_grad(partial_grad_t.astype(jnp.bfloat16), pre_q.T, margin_q)
     enc4 = enc_weight[0].reshape(RING, RING, chunk, lat_count)
     total = latent_reduce_mm(enc4, pre_grad_t, 5)
-    return jnp.swapaxes(total.astype(jnp.bfloat16), 1, 2).reshape(row_count, 1, chunk)
+    return jnp.swapaxes(total, 1, 2).reshape(row_count, 1, chunk)
 
 
 def solution(mesh):

time: 181 us -> 181 us (level)
  no operation moved by 1% of the time
where the time goes in v22:
time: 181 us
  Pallas kernels  159 us (88%)
  matrix products  13 us (7%)
  local copies, waits for them, and re-layouts  5.76 us (3%)
  other arithmetic  2.3 us (1%)
    pallas_call x1, Pallas kernels, latent_reduce(): pl.pallas_call(_reduce_kernel, out_shape=jax.ShapeDtypeStruct((2, h, c),...  37.1 us
    pallas_call x1, Pallas kernels, latent_reduce_mm(): pl.pallas_call(_reduce_mm_kernel, out_shape=jax.ShapeDtypeStruct((2, d, h...  35.6 us
    pallas_call x1, Pallas kernels, latent_gather(): pl.pallas_call(_gather_kernel, out_shape=(full, full, jax.ShapeDtypeStruc...  34.2 us
    pallas_call x1, Pallas kernels, layer_pre(): pl.pallas_call(_layer_pre_kernel, out_shape=(jax.ShapeDtypeStruct((rows,...  29.6 us
    pallas_call x1, Pallas kernels, layer_grad(): pl.pallas_call(_layer_grad_kernel, out_shape=jax.ShapeDtypeStruct((cols,...  22.9 us
    dot_general x1, matrix products, local(): jnp.dot(dec_weight[0], error_all, preferred_element_type=jnp.float32)  7.57 us
    unnamed x1, matrix products  5.47 us

profile of v22, /device:TPU:1, one launch (start us, length us, event | category | flops | bytes accessed | tf_op | source)
XLA Modules:
  0.0 180.6 jit_solution(7253974996573636798)
XLA Ops:
  0.0 0.0 copy-start
  0.0 29.6 %shard_map.82 = (bf16[512,768]{1,0:T(8,128)(2,1)}, f32[128,768]{1,0:T(8,128)}) custom-call(bf16[512,3584]{1,0:T(8,128)(2,1)} %bitcast.37, bf16[3584,768]{1,0:T(8,128)(2,1)} %bitcast.34, f32[768]{0:T(1024)} %bias.1), custom_call_target="tpu_custom_call" | custom-call | tf_op jit(solution)/shard_map/pallas_call | solution.py:374
  29.6 5.5 %fusion = f32[512,3584]{0,1:S(1)} fusion(bf16[512,768]{1,0:T(8,128)(2,1)} %get-tuple-element.10, bf16[1,768,3584]{2,1,0:T(8,128)(2,1)} %param.12), kind=kOutput, calls=%fused_computation | convolution fusion | flops 2818572288 | bytes 13631488
  35.1 2.3 %convert_bitcast_fusion.x = bf16[4,4,224,512]{3,2,1,0:T(8,128)(2,1)} fusion(f32[512,4,4,224]{0,3,2,1:T(8,128)S(1)} %bitcast.36), kind=kLoop, calls=%fused_computation.7 | loop fusion | flops 1835008 | bytes 11010048 | tf_op jit(solution)/shard_map/convert_element_type | solution.py:464
  37.4 0.0 copy-done
  37.4 0.1 dynamic-slice_bitcast_fusion
  37.4 0.8 copy.15.bias
  38.2 1.1 constant_dynamic-slice_fusion
  39.4 0.8 copy.14
  40.2 37.1 %shard_map.83.e = bf16[2,224,256]{2,1,0:T(8,128)(2,1)} custom-call(bf16[4,4,224,512]{3,2,1,0:T(8,128)(2,1)} %convert_bitcast_fusion.x, f32[224,1]{1,0:T(8,128)} %copy.15.bias, bf16[2,224,256]{2,1,0:T(8,128)(2,1)} %bitcast.41), custom_call_target="tpu_custom_call" | custom-call | tf_op jit(solution)/shard_map/pallas_call | solution.py:96
  77.3 34.2 %shard_map.84 = (bf16[4,4,224,256]{3,2,1,0:T(8,128)(2,1)}, bf16[4,4,224,256]{3,2,1,0:T(8,128)(2,1)}, f32[768,128]{1,0:T(8,128)}) custom-call(bf16[2,224,256]{2,1,0:T(8,128)(2,1)} %shard_map.83.e, s32[1,1024]{1,0:T(1,128)} %bitcast.42, s32[1,1024]{1,0:T(1,128)} %bitcast.43), custom_call_target="tpu_custom_call" | custom-call | tf_op jit(solution)/shard_map/pallas_call | solution.py:268
  111.5 0.0 copy-start.1
  111.6 7.6 %fusion.12.g = bf16[768,512]{1,0:T(8,128)(2,1)} fusion(bf16[3584,256]{1,0:T(8,128)(2,1)} %bitcast.45, bf16[3584,256]{1,0:T(8,128)(2,1)} %bitcast.44, bf16[1,768,3584]{2,1,0:T(8,128)(2,1)} %param.12), kind=kOutput, calls=%fused_computation.9 | convolution fusion | flops 2826305536 | bytes 9961472 | tf_op jit(solution)/shard_map/dot_general | solution.py:471
  119.1 0.0 copy-done.1
  119.1 0.9 copy.17
  120.0 22.9 %shard_map.85.v = bf16[768,512]{1,0:T(8,128)(2,1)} custom-call(bf16[768,512]{1,0:T(8,128)(2,1)} %fusion.12.g, f32[768,128]{1,0:T(8,128)} %bitcast.38, f32[768,128]{1,0:T(8,128)} %get-tuple-element.14.margin_q), custom_call_target="tpu_custom_call" | custom-call | tf_op jit(solution)/shard_map/pallas_call | solution.py:435
  143.0 35.6 %shard_map.86 = bf16[2,224,256]{2,1,0:T(8,128)(2,1)} custom-call(bf16[4,4,224,768]{3,2,1,0:T(8,128)(2,1)} %bitcast.35, bf16[768,512]{1,0:T(8,128)(2,1)} %shard_map.85.v), custom_call_target="tpu_custom_call" | custom-call | tf_op jit(solution)/shard_map/pallas_call | solution.py:185
  178.6 1.2 copy.18
  179.7 0.8 reshape.27
Async XLA Ops:
  0.0 37.4 %copy-start = (f32[1,3584]{1,0:T(1,128)S(1)}, f32[1,3584]{1,0:T(1,128)}, u32[]{:S(2)}) copy-start(f32[1,3584]{1,0:T(1,128)} %param.13) | copy-start | bytes 43012
  111.5 7.6 %copy-start.1 = (f32[128,768]{1,0:T(8,128)S(1)}, f32[128,768]{1,0:T(8,128)}, u32[]{:S(2)}) copy-start(f32[128,768]{1,0:T(8,128)} %get-tuple-element.13) | copy-start | bytes 1179652

commit v23 on v21

--- a/solution.py
+++ b/solution.py
@@ -31,7 +31,7 @@
     )
 
 
-def _reduce_kernel(x, bias, clean, out, r1a, r1b, s1a, s1b, r2a, r2b, send_sems, recv_sems):
+def _reduce_kernel(x, clean, out, r1a, r1b, s1a, s1b, r2a, r2b, send_sems, recv_sems):
     h = x.shape[-1] // 2
     xa = x.at[:, :, :, pl.ds(0, h)]
     xb = x.at[:, :, :, pl.ds(h, h)]
@@ -83,20 +83,20 @@
         own_a = own_a + r2a[t].astype(jnp.float32)
     for t in peers_z:
         own_b = own_b + r2b[t].astype(jnp.float32)
-    out[0] = (own_a + bias[...] - clean[0].astype(jnp.float32)).astype(out.dtype)
-    out[1] = (own_b + bias[...] - clean[1].astype(jnp.float32)).astype(out.dtype)
+    out[0] = (own_a - clean[0]).astype(out.dtype)
+    out[1] = (own_b - clean[1]).astype(out.dtype)
     for c in first + second:
         c.wait_send()
 
 
-def latent_reduce(x, bias, clean, collective_id):
+def latent_reduce(x, clean, collective_id):
     n, _, h, c = x.shape
     c = c // 2
     dt = x.dtype
     return pl.pallas_call(
         _reduce_kernel,
         out_shape=jax.ShapeDtypeStruct((2, h, c), jnp.bfloat16),
-        in_specs=[pl.BlockSpec(memory_space=pltpu.VMEM)] * 3,
+        in_specs=[pl.BlockSpec(memory_space=pltpu.VMEM)] * 2,
         out_specs=pl.BlockSpec(memory_space=pltpu.VMEM),
         scratch_shapes=[
             pltpu.VMEM((n, n, h, c), dt),
@@ -109,7 +109,7 @@
             pltpu.SemaphoreType.DMA((4, n)),
         ],
         compiler_params=pltpu.CompilerParams(collective_id=collective_id, has_side_effects=True),
-    )(x, bias, clean)
+    )(x, clean)
 
 
 def _reduce_mm_kernel(w, v, out, xa, xb, r1a, r1b, s1a, s1b, r2a, r2b, send_sems, recv_sems):
@@ -460,8 +460,8 @@
     recon_part = jnp.einsum("rf,fabd->abdr", features, dec4, preferred_element_type=jnp.float32)
     bias_part = lax.dynamic_slice_in_dim(dec_bias[0], me * chunk, chunk)
     clean_part = lax.dynamic_slice_in_dim(clean_acts[:, 0, :], me * chunk, chunk, axis=1)
-    clean_t = jnp.swapaxes(clean_part.reshape(2, half, chunk), 1, 2)
-    recon_error = latent_reduce(recon_part.astype(jnp.bfloat16), bias_part[:, None], clean_t, 3)
+    clean_t = jnp.swapaxes(clean_part.reshape(2, half, chunk), 1, 2).astype(jnp.float32)
+    recon_error = latent_reduce(recon_part.astype(jnp.bfloat16), clean_t - bias_part[:, None], 3)
     error_a, error_b, margin_q = latent_gather(
         recon_error, targets.reshape(1, all_rows), pairing.reshape(1, all_rows), lat_count, 4
     )

time: 181 us -> 181 us (level)
  no operation moved by 1% of the time
where the time goes in v23:
time: 181 us; the launch traced here: 180 us
  Pallas kernels  159 us (88%)
  matrix products  13 us (7%)
  other arithmetic  4.23 us (2%)
  local copies, waits for them, and re-layouts  3.63 us (2%)
    pallas_call x1, Pallas kernels, latent_reduce(): pl.pallas_call(_reduce_kernel, out_shape=jax.ShapeDtypeStruct((2, h, c),...  37.1 us
    pallas_call x1, Pallas kernels, latent_reduce_mm(): pl.pallas_call(_reduce_mm_kernel, out_shape=jax.ShapeDtypeStruct((2, d, h...  35.7 us
    pallas_call x1, Pallas kernels, latent_gather(): pl.pallas_call(_gather_kernel, out_shape=(full, full, jax.ShapeDtypeStruc...  34.2 us
    pallas_call x1, Pallas kernels, layer_pre(): pl.pallas_call(_layer_pre_kernel, out_shape=(jax.ShapeDtypeStruct((rows,...  29.6 us
    pallas_call x1, Pallas kernels, layer_grad(): pl.pallas_call(_layer_grad_kernel, out_shape=jax.ShapeDtypeStruct((cols,...  22.9 us
    dot_general x1, matrix products, local(): jnp.dot(dec_weight[0], error_all, preferred_element_type=jnp.float32)  7.57 us
    unnamed x1, matrix products  5.47 us

profile of v23, /device:TPU:1, one launch (start us, length us, event | category | flops | bytes accessed | tf_op | source)
XLA Modules:
  0.0 180.5 jit_solution(6841268434787278746)
XLA Ops:
  0.0 0.0 copy-start
  0.0 29.6 %shard_map.82 = (bf16[512,768]{1,0:T(8,128)(2,1)}, f32[128,768]{1,0:T(8,128)}) custom-call(bf16[512,3584]{1,0:T(8,128)(2,1)} %bitcast.39, bf16[3584,768]{1,0:T(8,128)(2,1)} %bitcast.36, f32[768]{0:T(1024)} %bias.1), custom_call_target="tpu_custom_call" | custom-call | tf_op jit(solution)/shard_map/pallas_call | solution.py:374
  29.6 5.5 %fusion = f32[512,3584]{0,1:S(1)} fusion(bf16[512,768]{1,0:T(8,128)(2,1)} %get-tuple-element.10, bf16[1,768,3584]{2,1,0:T(8,128)(2,1)} %param.12), kind=kOutput, calls=%fused_computation | convolution fusion | flops 2818572288 | bytes 13631488
  35.1 2.3 %convert_bitcast_fusion.x = bf16[4,4,224,512]{3,2,1,0:T(8,128)(2,1)} fusion(f32[512,4,4,224]{0,3,2,1:T(8,128)S(1)} %bitcast.38), kind=kLoop, calls=%fused_computation.7 | loop fusion | flops 1835008 | bytes 11010048 | tf_op jit(solution)/shard_map/convert_element_type | solution.py:464
  37.4 1.1 constant_dynamic-slice_fusion.1
  38.5 0.1 copy.25
  38.6 0.3 reshape.28
  38.9 0.0 copy-done
  38.9 0.1 constant_dynamic-slice_fusion
  39.0 0.9 fusion.17.clean
  39.9 37.1 %shard_map.83.e = bf16[2,224,256]{2,1,0:T(8,128)(2,1)} custom-call(bf16[4,4,224,512]{3,2,1,0:T(8,128)(2,1)} %convert_bitcast_fusion.x, f32[2,224,256]{2,1,0:T(8,128)} %fusion.17.clean), custom_call_target="tpu_custom_call" | custom-call | tf_op jit(solution)/shard_map/pallas_call | solution.py:96
  77.0 34.2 %shard_map.84 = (bf16[4,4,224,256]{3,2,1,0:T(8,128)(2,1)}, bf16[4,4,224,256]{3,2,1,0:T(8,128)(2,1)}, f32[768,128]{1,0:T(8,128)}) custom-call(bf16[2,224,256]{2,1,0:T(8,128)(2,1)} %shard_map.83.e, s32[1,1024]{1,0:T(1,128)} %bitcast.41, s32[1,1024]{1,0:T(1,128)} %bitcast.42), custom_call_target="tpu_custom_call" | custom-call | tf_op jit(solution)/shard_map/pallas_call | solution.py:268
  111.2 0.0 copy-start.1
  111.2 7.6 %fusion.12.g = bf16[768,512]{1,0:T(8,128)(2,1)} fusion(bf16[3584,256]{1,0:T(8,128)(2,1)} %bitcast.45, bf16[3584,256]{1,0:T(8,128)(2,1)} %bitcast.44, bf16[1,768,3584]{2,1,0:T(8,128)(2,1)} %param.12), kind=kOutput, calls=%fused_computation.9 | convolution fusion | flops 2826305536 | bytes 9961472 | tf_op jit(solution)/shard_map/dot_general | solution.py:471
  118.8 0.0 copy-done.1
  118.8 0.9 copy.22
  119.7 22.9 %shard_map.85.v = bf16[768,512]{1,0:T(8,128)(2,1)} custom-call(bf16[768,512]{1,0:T(8,128)(2,1)} %fusion.12.g, f32[768,128]{1,0:T(8,128)} %bitcast.40, f32[768,128]{1,0:T(8,128)} %get-tuple-element.14.margin_q), custom_call_target="tpu_custom_call" | custom-call | tf_op jit(solution)/shard_map/pallas_call | solution.py:435
  142.7 35.7 %shard_map.86 = f32[2,224,256]{2,1,0:T(8,128)} custom-call(bf16[4,4,224,768]{3,2,1,0:T(8,128)(2,1)} %bitcast.37, bf16[768,512]{1,0:T(8,128)(2,1)} %shard_map.85.v), custom_call_target="tpu_custom_call" | custom-call | tf_op jit(solution)/shard_map/pallas_call | solution.py:185
  178.3 1.0 convert_bitcast_fusion.1
  179.4 0.2 copy.23
  179.6 0.8 reshape.27
Async XLA Ops:
  0.0 38.9 %copy-start = (f32[1,3584]{1,0:T(1,128)S(1)}, f32[1,3584]{1,0:T(1,128)}, u32[]{:S(2)}) copy-start(f32[1,3584]{1,0:T(1,128)} %param.13) | copy-start | bytes 43012
  111.2 7.6 %copy-start.1 = (f32[128,768]{1,0:T(8,128)S(1)}, f32[128,768]{1,0:T(8,128)}, u32[]{:S(2)}) copy-start(f32[128,768]{1,0:T(8,128)} %get-tuple-element.13) | copy-start | bytes 1179652

commit v24 on v23

--- a/solution.py
+++ b/solution.py
@@ -345,7 +345,7 @@
 def _layer_pre_kernel(inp, w, bias, feats, pre_q, x, *scratch):
     def finish(total):
         pre = total + bias[...].reshape(1, -1)
-        pre_q[...] = pre
+        pre_q[...] = pre.T
         return jnp.maximum(pre, 0.0).astype(feats.dtype)
 
     def produce(i):
@@ -374,7 +374,7 @@
     return pl.pallas_call(
         _layer_pre_kernel,
         out_shape=(jax.ShapeDtypeStruct((rows, cols), jnp.bfloat16),
-                   jax.ShapeDtypeStruct((q, cols), jnp.float32)),
+                   jax.ShapeDtypeStruct((cols, q), jnp.float32)),
         in_specs=[pl.BlockSpec(memory_space=pltpu.VMEM)] * 3,
         out_specs=(pl.BlockSpec(memory_space=pltpu.VMEM), pl.BlockSpec(memory_space=pltpu.VMEM)),
         scratch_shapes=[pltpu.VMEM((rows, cols), jnp.float32)]
@@ -469,7 +469,7 @@
         [error_a.reshape(d_model, half), error_b.reshape(d_model, half)], axis=1
     )
     partial_grad_t = jnp.dot(dec_weight[0], error_all, preferred_element_type=jnp.float32)
-    pre_grad_t = layer_grad(partial_grad_t.astype(jnp.bfloat16), pre_q.T, margin_q)
+    pre_grad_t = layer_grad(partial_grad_t.astype(jnp.bfloat16), pre_q, margin_q)
     enc4 = enc_weight[0].reshape(RING, RING, chunk, lat_count)
     total = latent_reduce_mm(enc4, pre_grad_t, 5)
     return jnp.swapaxes(total.astype(jnp.bfloat16), 1, 2).reshape(row_count, 1, chunk)

time: 181 us -> 180 us (level)
  no operation moved by 1% of the time
where the time goes in v24:
time: 180 us
  Pallas kernels  160 us (89%)
  matrix products  13 us (7%)
  other arithmetic  4.24 us (2%)
  local copies, waits for them, and re-layouts  2.71 us (2%)
    pallas_call x1, Pallas kernels, latent_reduce(): pl.pallas_call(_reduce_kernel, out_shape=jax.ShapeDtypeStruct((2, h, c),...  37.1 us
    pallas_call x1, Pallas kernels, latent_reduce_mm(): pl.pallas_call(_reduce_mm_kernel, out_shape=jax.ShapeDtypeStruct((2, d, h...  35.7 us
    pallas_call x1, Pallas kernels, latent_gather(): pl.pallas_call(_gather_kernel, out_shape=(full, full, jax.ShapeDtypeStruc...  34.2 us
    pallas_call x1, Pallas kernels, layer_pre(): pl.pallas_call(_layer_pre_kernel, out_shape=(jax.ShapeDtypeStruct((rows,...  29.7 us
    pallas_call x1, Pallas kernels, layer_grad(): pl.pallas_call(_layer_grad_kernel, out_shape=jax.ShapeDtypeStruct((cols,...  22.9 us
    dot_general x1, matrix products, local(): jnp.dot(dec_weight[0], error_all, preferred_element_type=jnp.float32)  7.54 us
    unnamed x1, matrix products  5.47 us

profile of v24, /device:TPU:1, one launch (start us, length us, event | category | flops | bytes accessed | tf_op | source)
XLA Modules:
  0.0 179.7 jit_solution(7072505703005783574)
XLA Ops:
  0.0 0.0 copy-start
  0.0 29.7 %shard_map.82 = (bf16[512,768]{1,0:T(8,128)(2,1)}, f32[768,128]{1,0:T(8,128)}) custom-call(bf16[512,3584]{1,0:T(8,128)(2,1)} %bitcast.38, bf16[3584,768]{1,0:T(8,128)(2,1)} %bitcast.35, f32[768]{0:T(1024)} %bias.1), custom_call_target="tpu_custom_call" | custom-call | tf_op jit(solution)/shard_map/pallas_call | solution.py:374
  29.7 5.5 %fusion = f32[512,3584]{0,1:S(1)} fusion(bf16[512,768]{1,0:T(8,128)(2,1)} %get-tuple-element.10, bf16[1,768,3584]{2,1,0:T(8,128)(2,1)} %param.12), kind=kOutput, calls=%fused_computation | convolution fusion | flops 2818572288 | bytes 13631488
  35.2 2.3 %convert_bitcast_fusion.x = bf16[4,4,224,512]{3,2,1,0:T(8,128)(2,1)} fusion(f32[512,4,4,224]{0,3,2,1:T(8,128)S(1)} %bitcast.37), kind=kLoop, calls=%fused_computation.7 | loop fusion | flops 1835008 | bytes 11010048 | tf_op jit(solution)/shard_map/convert_element_type | solution.py:464
  37.5 1.1 constant_dynamic-slice_fusion.1
  38.6 0.1 copy.22
  38.8 0.3 reshape.28
  39.1 0.0 copy-done
  39.1 0.1 constant_dynamic-slice_fusion
  39.2 0.9 fusion.17.clean
  40.1 37.1 %shard_map.83.e = bf16[2,224,256]{2,1,0:T(8,128)(2,1)} custom-call(bf16[4,4,224,512]{3,2,1,0:T(8,128)(2,1)} %convert_bitcast_fusion.x, f32[2,224,256]{2,1,0:T(8,128)} %fusion.17.clean), custom_call_target="tpu_custom_call" | custom-call | tf_op jit(solution)/shard_map/pallas_call | solution.py:96
  77.1 34.2 %shard_map.84 = (bf16[4,4,224,256]{3,2,1,0:T(8,128)(2,1)}, bf16[4,4,224,256]{3,2,1,0:T(8,128)(2,1)}, f32[768,128]{1,0:T(8,128)}) custom-call(bf16[2,224,256]{2,1,0:T(8,128)(2,1)} %shard_map.83.e, s32[1,1024]{1,0:T(1,128)} %bitcast.39, s32[1,1024]{1,0:T(1,128)} %bitcast.40), custom_call_target="tpu_custom_call" | custom-call | tf_op jit(solution)/shard_map/pallas_call | solution.py:268
  111.4 7.5 %fusion.12.g = bf16[768,512]{1,0:T(8,128)(2,1)} fusion(bf16[3584,256]{1,0:T(8,128)(2,1)} %bitcast.43, bf16[3584,256]{1,0:T(8,128)(2,1)} %bitcast.42, bf16[1,768,3584]{2,1,0:T(8,128)(2,1)} %param.12), kind=kOutput, calls=%fused_computation.9 | convolution fusion | flops 2826305536 | bytes 9961472 | tf_op jit(solution)/shard_map/dot_general | solution.py:471
  118.9 22.9 %shard_map.85.v = bf16[768,512]{1,0:T(8,128)(2,1)} custom-call(bf16[768,512]{1,0:T(8,128)(2,1)} %fusion.12.g, f32[768,128]{1,0:T(8,128)} %get-tuple-element.13.pre_q, f32[768,128]{1,0:T(8,128)} %get-tuple-element.14.margin_q), custom_call_target="tpu_custom_call" | custom-call | tf_op jit(solution)/shard_map/pallas_call | solution.py:435
  141.8 35.7 %shard_map.86 = f32[2,224,256]{2,1,0:T(8,128)} custom-call(bf16[4,4,224,768]{3,2,1,0:T(8,128)(2,1)} %bitcast.36, bf16[768,512]{1,0:T(8,128)(2,1)} %shard_map.85.v), custom_call_target="tpu_custom_call" | custom-call | tf_op jit(solution)/shard_map/pallas_call | solution.py:185
  177.5 1.0 convert_bitcast_fusion.1
  178.6 0.2 copy.20
  178.8 0.8 reshape.27
Async XLA Ops:
  0.0 39.1 %copy-start = (f32[1,3584]{1,0:T(1,128)S(1)}, f32[1,3584]{1,0:T(1,128)}, u32[]{:S(2)}) copy-start(f32[1,3584]{1,0:T(1,128)} %param.13) | copy-start | bytes 43012
